TPU v7x, 512 devices: a whole 4x8x8 slice. The times are simulated.
512 devices in a mesh: gz: 32 (over y_lo, z), gy: 16 (over y_hi, x, core).
Axes of the slice: x: 4, y: 8 (y_hi: 2, y_lo: 4; y = y_hi * 4 + y_lo), z: 8, core: 2. Of those that a mesh axis runs over, the one named last changes fastest.
Arguments:
- features: bfloat16 [64, 64, 128, 128], P(None, 'gz', 'gy'), may hold values from -6 to 6
- conv_weight: bfloat16 [3, 3, 64, 192], replicated, may hold values from -0.15625 to 0.15625
- down_weight: bfloat16 [2, 2, 128, 128], replicated, may hold values from -0.25 to 0.25
- cotangent: bfloat16 [128, 32, 4096], P(None, 'gz', 'gy'), may hold values from -6 to 6
Outputs:
- section_out: bfloat16 [128, 32, 4096], P(None, 'gz', 'gy')
- grad_field: float32 [64, 64, 128, 128], P(None, 'gz', 'gy')
- grad_conv: float32 [3, 3, 64, 192], replicated
- grad_down: float32 [2, 2, 128, 128], replicated
All inputs are finite; a program needn't handle non-finite values.
Results may differ from a plain program's by a relative error of at most 0.005.
Values may be sent and summed in bfloat16 or wider, within the bound.
A program may use at most 64 MiB of HBM per device.

v0:
```python
import math

import jax
import jax.numpy as jnp
from jax import lax
from jax.sharding import PartitionSpec as P


def extended(cells, sides, width):
    for axis, dim in sides:
        count = lax.axis_size(axis)
        head = lax.slice_in_dim(cells, 0, width, axis=dim)
        tail = lax.slice_in_dim(cells, cells.shape[dim] - width, cells.shape[dim], axis=dim)
        cells = jnp.concatenate(
            [
                lax.ppermute(tail, axis, [(i, (i + 1) % count) for i in range(count)]),
                cells,
                lax.ppermute(head, axis, [((i + 1) % count, i) for i in range(count)]),
            ],
            axis=dim,
        )
    return cells


def widen(framed):
    return jnp.concatenate([jnp.roll(framed, 1 - tap_x, axis=3) for tap_x in range(3)], axis=0)


def fold_along(spread, channels):
    result = jnp.roll(spread[0:channels], -1, axis=3)
    result = result + spread[channels : 2 * channels]
    result = result + jnp.roll(spread[2 * channels : 3 * channels], 1, axis=3)
    return result


def body(features, conv_weight, down_weight, cotangent):
    channels, plane_count, row_count, breadth = features.shape
    out_channels = down_weight.shape[2]
    cell_count = plane_count * row_count * breadth * lax.axis_size("gz") * lax.axis_size("gy")
    grad_scale = 1.0 / math.sqrt(cell_count)
    framed = extended(features, (("gz", 1), ("gy", 2)), 1)
    columns = widen(framed)
    preact = jnp.zeros((channels, plane_count, row_count, breadth), jnp.float32)
    for tap_z in range(3):
        for tap_y in range(3):
            window = columns[:, tap_z : tap_z + plane_count, tap_y : tap_y + row_count]
            preact = preact + jnp.einsum(
                "oj,jzyx->ozyx",
                conv_weight[tap_z, tap_y],
                window,
                preferred_element_type=jnp.float32,
            )
    hidden = jax.nn.silu(preact).astype(jnp.bfloat16)
    blocks = hidden.reshape(channels, plane_count // 2, 2, row_count // 2, 2, breadth // 2, 2)
    down_split = down_weight.reshape(2, 2, out_channels, 2, channels)
    coarse = jnp.einsum(
        "aboei,iZaYbXe->oZYX", down_split, blocks, preferred_element_type=jnp.float32
    )
    section_out = coarse.reshape(out_channels, plane_count // 2, -1).astype(jnp.bfloat16)
    coarse_cot = cotangent.reshape(out_channels, plane_count // 2, row_count // 2, breadth // 2)
    hidden_grad = jnp.einsum(
        "aboei,oZYX->iZaYbXe", down_split, coarse_cot, preferred_element_type=jnp.float32
    )
    hidden_grad = hidden_grad.reshape(channels, plane_count, row_count, breadth)
    local_down = jnp.einsum(
        "oZYX,iZaYbXe->aboei", coarse_cot, blocks, preferred_element_type=jnp.float32
    )
    local_down = local_down.reshape(2, 2, out_channels, 2 * channels)
    gate_sig = jax.nn.sigmoid(preact)
    gate_grad = (hidden_grad * gate_sig * (1.0 + preact * (1.0 - gate_sig))).astype(jnp.bfloat16)
    kernel_rows = []
    for tap_z in range(3):
        row_list = []
        for tap_y in range(3):
            window = columns[:, tap_z : tap_z + plane_count, tap_y : tap_y + row_count]
            row_list.append(
                jnp.einsum("ozyx,jzyx->oj", gate_grad, window, preferred_element_type=jnp.float32)
            )
        kernel_rows.append(jnp.stack(row_list, axis=0))
    local_conv = jnp.stack(kernel_rows, axis=0)
    spread = jnp.zeros((3 * channels, plane_count + 2, row_count + 2, breadth), jnp.float32)
    for tap_z in range(3):
        for tap_y in range(3):
            term = jnp.einsum(
                "oj,ozyx->jzyx",
                conv_weight[tap_z, tap_y],
                gate_grad,
                preferred_element_type=jnp.float32,
            )
            spread = spread.at[:, tap_z : tap_z + plane_count, tap_y : tap_y + row_count].add(term)
    folded = fold_along(spread, channels)
    bordered = extended(folded.astype(jnp.bfloat16), (("gz", 1), ("gy", 2)), 1).astype(folded.dtype)
    plane_fold = bordered[:, 2 : plane_count + 2]
    plane_fold = plane_fold.at[:, 0].add(bordered[:, 0])
    plane_fold = plane_fold.at[:, plane_count - 1].add(bordered[:, plane_count + 3])
    row_fold = plane_fold[:, :, 2 : row_count + 2]
    row_fold = row_fold.at[:, :, 0].add(plane_fold[:, :, 0])
    row_fold = row_fold.at[:, :, row_count - 1].add(plane_fold[:, :, row_count + 3])
    summed_conv, summed_down = lax.psum((local_conv, local_down), ("gz", "gy"))
    grad_conv = summed_conv * grad_scale
    grad_down = summed_down * grad_scale
    return (section_out, row_fold, grad_conv, grad_down)


def solution(mesh):
    return jax.shard_map(
        body,
        mesh=mesh,
        in_specs=(P(None, "gz", "gy", None), P(), P(), P(None, "gz", "gy")),
        out_specs=(P(None, "gz", "gy"), P(None, "gz", "gy", None), P(), P()),
        check_vma=False,
    )
```

profile of v0, /device:TPU:1, one launch (start us, length us, event | category | flops | bytes accessed | tf_op | source)
XLA Modules:
  0.0 376.9 jit_solution(9793615416757885688)
XLA Ops:
  7.2 1.0 fusion.104
  8.2 4.8 %collective-permute-start = (bf16[64,1,8,128]{3,0,2,1:T(8,128)(2,1)S(1)}, bf16[64,1,8,128]{3,0,2,1:T(8,128)(2,1)S(1)}, u32[]{:S(2)}, u32[]{:S(2)}) collective-permute-start(bf16[64,1,8,128]{3,0,2,1:T(8,128)(2,1)S(1)} %copy.161), channel_id=1, source_target_pairs={{0,16},{16,32},{32,48},{48,64},{64,80},{80,96},{96,112},{112,128},... | collective-permute-start | bytes 393224 | tf_op jit(solution)/shard_map/ppermute | solution.py:16
  13.1 11.6 %collective-permute-start.1 = (bf16[64,1,8,128]{3,0,2,1:T(8,128)(2,1)S(1)}, bf16[64,1,8,128]{3,0,2,1:T(8,128)(2,1)S(1)}, u32[]{:S(2)}, u32[]{:S(2)}) collective-permute-start(bf16[64,1,8,128]{3,0,2,1:T(8,128)(2,1)S(1)} %copy.162), channel_id=1, source_target_pairs={{16,0},{32,16},{48,32},{64,48},{80,64},{96,80},{112,96},{128,112},... | collective-permute-start | bytes 393224 | tf_op jit(solution)/shard_map/ppermute | solution.py:18
  24.7 1.0 copy.74
  25.8 1.0 copy.75
  26.7 0.3 convolution_bitcast_fusion.1
  27.1 0.6 fusion.105
  27.7 0.8 copy.76
  28.5 0.3 copy.77
  28.8 0.8 and_reduce_fusion
  29.8 4.0 %collective-permute-start.2 = (bf16[64,4,1,128]{3,0,2,1:T(8,128)(2,1)S(1)}, bf16[64,4,1,128]{3,0,2,1:T(8,128)(2,1)S(1)}, u32[]{:S(2)}, u32[]{:S(2)}) collective-permute-start(bf16[64,4,1,128]{3,0,2,1:T(8,128)(2,1)S(1)} %get-tuple-element.197), channel_id=1, source_target_pairs={{0,1},{1,2},{2,3},{3,4},{4,5},{5,6},{6,7},{7,8},{8,9},{9,10},{10,1... | collective-permute-start | bytes 196616 | tf_op jit(solution)/shard_map/ppermute | solution.py:16
  33.7 1.9 collective-permute-start.3
  35.7 0.6 fusion.106
  36.3 3.4 collective-permute-done.3
  39.7 0.3 fusion.101
  40.0 0.3 fusion.102
  40.3 1.2 maximum_maximum_fusion
  41.5 0.3 fusion.36
  41.8 0.3 fusion.39
  42.0 0.3 fusion.42
  42.3 0.3 fusion.45
  42.6 0.3 fusion.48
  42.8 0.3 fusion.51
  43.6 1.8 fusion.99
  45.4 0.5 multiply_convert_fusion
  45.9 0.4 convolution_bitcast_fusion
  46.3 0.4 scatter-add.44
  46.7 1.8 fusion.7
  48.5 2.4 fusion
  51.0 0.6 fusion.6
  51.6 0.6 fusion.5
  52.2 0.6 fusion.4
  52.8 0.6 fusion.3
  53.4 0.6 fusion.2
  54.0 0.6 fusion.1
  54.6 0.5 fusion.97
  55.1 1.4 copy-done
  56.5 2.0 fusion.98
  58.5 0.4 convolution_bitcast_fusion.10
  58.9 1.0 convolution_bitcast_fusion.11
  59.9 1.0 convolution_bitcast_fusion.6
  60.9 1.0 convolution_bitcast_fusion.7
  61.9 1.0 convolution_bitcast_fusion.8
  62.9 1.0 convolution_bitcast_fusion.9
  63.9 1.0 convolution_bitcast_fusion.3
  64.9 1.0 convolution_bitcast_fusion.4
  65.9 1.0 convolution_bitcast_fusion.5
  66.9 1.0 copy.72
  67.9 2.8 fusion.9
  70.8 2.1 collective-permute-start.4
  72.9 7.5 %collective-permute-start.5 = (bf16[64,1,10,128]{3,0,2,1:T(8,128)(2,1)S(1)}, bf16[64,1,10,128]{3,0,2,1:T(8,128)(2,1)S(1)}, u32[]{:S(2)}, u32[]{:S(2)}) collective-permute-start(bf16[64,1,10,128]{3,0,2,1:T(8,128)(2,1)S(1)} %get-tuple-element.190), channel_id=1, source_target_pairs={{16,0},{32,16},{48,32},{64,48},{80,64},{96,80},{112,96},{128,112},... | collective-permute-start | bytes 491528 | tf_op jit(solution)/shard_map/ppermute | solution.py:18
  80.4 1.6 copy.73
  82.0 0.3 dot_general.118
  82.3 0.3 fusion.29
  82.7 0.3 fusion.19
  83.0 0.8 copy.97
  83.8 0.7 copy.98
  84.7 2.1 collective-permute-start.6
  86.8 6.8 %collective-permute-start.7 = (bf16[64,6,1,128]{3,0,2,1:T(8,128)(2,1)S(1)}, bf16[64,6,1,128]{3,0,2,1:T(8,128)(2,1)S(1)}, u32[]{:S(2)}, u32[]{:S(2)}) collective-permute-start(bf16[64,6,1,128]{3,0,2,1:T(8,128)(2,1)S(1)} %get-tuple-element.188), channel_id=1, source_target_pairs={{1,0},{2,1},{3,2},{4,3},{5,4},{6,5},{7,6},{8,7},{9,8},{10,9},{11,1... | collective-permute-start | bytes 294920 | tf_op jit(solution)/shard_map/ppermute | solution.py:18
  93.7 0.9 pad_maximum_fusion.1
  95.2 1.1 copy.99
  96.3 270.2 %all-reduce.4.cloned.1.call-done = (f32[3,3,64,192]{3,2,1,0:T(8,128)}, f32[2,2,128,128]{3,2,1,0:T(8,128)}) async-done(((f32[3,3,64,192]{3,2,1,0:T(8,128)}, f32[2,2,128,128]{3,2,1,0:T(8,128)}), (f32[3,3,64,192]{3,2,1,0:T(8,128)}, f32[2,2,128,128]{3,2,1,0:T(8,128)})) %all-reduce.4.cloned.1.call-update) | async-done | bytes 704528 | tf_op jit(solution)/shard_map/psum | solution.py:99
  366.4 1.9 broadcast_multiply_fusion
  368.4 1.7 broadcast_multiply_fusion.1
  (56 shorter events, 1.5 us)
Async XLA Ops:
  7.2 359.3 %all-reduce.4.cloned.1.call-start = ((), (), s32[]{:S(2)}) async-start(), calls=%async_computation | async-start | bytes 1703936 | tf_op jit(solution)/shard_map/psum | solution.py:99
  8.2 21.4 %collective-permute-start = (bf16[64,1,8,128]{3,0,2,1:T(8,128)(2,1)S(1)}, bf16[64,1,8,128]{3,0,2,1:T(8,128)(2,1)S(1)}, u32[]{:S(2)}, u32[]{:S(2)}) collective-permute-start(bf16[64,1,8,128]{3,0,2,1:T(8,128)(2,1)S(1)} %copy.161), channel_id=1, source_target_pairs={{0,16},{16,32},{32,48},{48,64},{64,80},{80,96},{96,112},{112,128},... | collective-permute-start | bytes 393224 | tf_op jit(solution)/shard_map/ppermute | solution.py:16
  13.1 16.6 %collective-permute-start.1 = (bf16[64,1,8,128]{3,0,2,1:T(8,128)(2,1)S(1)}, bf16[64,1,8,128]{3,0,2,1:T(8,128)(2,1)S(1)}, u32[]{:S(2)}, u32[]{:S(2)}) collective-permute-start(bf16[64,1,8,128]{3,0,2,1:T(8,128)(2,1)S(1)} %copy.162), channel_id=1, source_target_pairs={{16,0},{32,16},{48,32},{64,48},{80,64},{96,80},{112,96},{128,112},... | collective-permute-start | bytes 393224 | tf_op jit(solution)/shard_map/ppermute | solution.py:18
  27.1 1.7 copy-start.12
  27.6 2.0 copy-start.3
  29.8 6.5 %collective-permute-start.2 = (bf16[64,4,1,128]{3,0,2,1:T(8,128)(2,1)S(1)}, bf16[64,4,1,128]{3,0,2,1:T(8,128)(2,1)S(1)}, u32[]{:S(2)}, u32[]{:S(2)}) collective-permute-start(bf16[64,4,1,128]{3,0,2,1:T(8,128)(2,1)S(1)} %get-tuple-element.197), channel_id=1, source_target_pairs={{0,1},{1,2},{2,3},{3,4},{4,5},{5,6},{6,7},{7,8},{8,9},{9,10},{10,1... | collective-permute-start | bytes 196616 | tf_op jit(solution)/shard_map/ppermute | solution.py:16
  33.7 5.9 %collective-permute-start.3 = (bf16[64,4,1,128]{3,0,2,1:T(8,128)(2,1)S(1)}, bf16[64,4,1,128]{3,0,2,1:T(8,128)(2,1)S(1)}, u32[]{:S(2)}, u32[]{:S(2)}) collective-permute-start(bf16[64,4,1,128]{3,0,2,1:T(8,128)(2,1)S(1)} %get-tuple-element.198), channel_id=1, source_target_pairs={{1,0},{2,1},{3,2},{4,3},{5,4},{6,5},{7,6},{8,7},{9,8},{10,9},{11,1... | collective-permute-start | bytes 196616 | tf_op jit(solution)/shard_map/ppermute | solution.py:18
  40.3 1.2 copy-start.2
  54.6 1.9 copy-start
  70.8 11.6 %copy-start.1 = (bf16[64,2,8,128]{0,3,2,1:T(8,128)(2,1)S(1)}, bf16[64,2,8,128]{0,3,2,1:T(8,128)(2,1)}, u32[]{:S(2)}) copy-start(bf16[64,2,8,128]{0,3,2,1:T(8,128)(2,1)} %copy.72) | copy-start | bytes 786436
  70.8 12.2 %copy-start.9 = (f32[1,64,192]{2,1,0:T(8,128)S(1)}, f32[1,64,192]{2,1,0:T(8,128)}, u32[]{:S(2)}) copy-start(f32[1,64,192]{2,1,0:T(8,128)} %convolution_bitcast_fusion.3) | copy-start | bytes 147460
  70.8 12.2 %copy-start.10 = (f32[1,64,192]{2,1,0:T(8,128)S(1)}, f32[1,64,192]{2,1,0:T(8,128)}, u32[]{:S(2)}) copy-start(f32[1,64,192]{2,1,0:T(8,128)} %convolution_bitcast_fusion.4) | copy-start | bytes 147460
  70.8 12.2 %copy-start.11 = (f32[1,64,192]{2,1,0:T(8,128)S(1)}, f32[1,64,192]{2,1,0:T(8,128)}, u32[]{:S(2)}) copy-start(f32[1,64,192]{2,1,0:T(8,128)} %convolution_bitcast_fusion.5) | copy-start | bytes 147460
  70.8 13.8 %collective-permute-start.4 = (bf16[64,1,10,128]{3,0,2,1:T(8,128)(2,1)S(1)}, bf16[64,1,10,128]{3,0,2,1:T(8,128)(2,1)S(1)}, u32[]{:S(2)}, u32[]{:S(2)}) collective-permute-start(bf16[64,1,10,128]{3,0,2,1:T(8,128)(2,1)S(1)} %get-tuple-element.189), channel_id=1, source_target_pairs={{0,16},{16,32},{32,48},{48,64},{64,80},{80,96},{96,112},{112,128},... | collective-permute-start | bytes 491528 | tf_op jit(solution)/shard_map/ppermute | solution.py:16
  72.9 11.8 %collective-permute-start.5 = (bf16[64,1,10,128]{3,0,2,1:T(8,128)(2,1)S(1)}, bf16[64,1,10,128]{3,0,2,1:T(8,128)(2,1)S(1)}, u32[]{:S(2)}, u32[]{:S(2)}) collective-permute-start(bf16[64,1,10,128]{3,0,2,1:T(8,128)(2,1)S(1)} %get-tuple-element.190), channel_id=1, source_target_pairs={{16,0},{32,16},{48,32},{64,48},{80,64},{96,80},{112,96},{128,112},... | collective-permute-start | bytes 491528 | tf_op jit(solution)/shard_map/ppermute | solution.py:18
  80.4 4.2 %copy-start.4 = (f32[1,64,192]{2,1,0:T(8,128)S(1)}, f32[1,64,192]{2,1,0:T(8,128)}, u32[]{:S(2)}) copy-start(f32[1,64,192]{2,1,0:T(8,128)} %convolution_bitcast_fusion.11) | copy-start | bytes 147460
  80.4 4.2 %copy-start.5 = (f32[1,64,192]{2,1,0:T(8,128)S(1)}, f32[1,64,192]{2,1,0:T(8,128)}, u32[]{:S(2)}) copy-start(f32[1,64,192]{2,1,0:T(8,128)} %convolution_bitcast_fusion.6) | copy-start | bytes 147460
  80.4 4.2 %copy-start.6 = (f32[1,64,192]{2,1,0:T(8,128)S(1)}, f32[1,64,192]{2,1,0:T(8,128)}, u32[]{:S(2)}) copy-start(f32[1,64,192]{2,1,0:T(8,128)} %convolution_bitcast_fusion.7) | copy-start | bytes 147460
  80.4 4.2 %copy-start.7 = (f32[1,64,192]{2,1,0:T(8,128)S(1)}, f32[1,64,192]{2,1,0:T(8,128)}, u32[]{:S(2)}) copy-start(f32[1,64,192]{2,1,0:T(8,128)} %convolution_bitcast_fusion.8) | copy-start | bytes 147460
  80.4 4.2 %copy-start.8 = (f32[1,64,192]{2,1,0:T(8,128)S(1)}, f32[1,64,192]{2,1,0:T(8,128)}, u32[]{:S(2)}) copy-start(f32[1,64,192]{2,1,0:T(8,128)} %convolution_bitcast_fusion.9) | copy-start | bytes 147460
  84.7 9.9 %collective-permute-start.6 = (bf16[64,6,1,128]{3,0,2,1:T(8,128)(2,1)S(1)}, bf16[64,6,1,128]{3,0,2,1:T(8,128)(2,1)S(1)}, u32[]{:S(2)}, u32[]{:S(2)}) collective-permute-start(bf16[64,6,1,128]{3,0,2,1:T(8,128)(2,1)S(1)} %get-tuple-element.187), channel_id=1, source_target_pairs={{0,1},{1,2},{2,3},{3,4},{4,5},{5,6},{6,7},{7,8},{8,9},{9,10},{10,1... | collective-permute-start | bytes 294920 | tf_op jit(solution)/shard_map/ppermute | solution.py:16
  86.8 7.8 %collective-permute-start.7 = (bf16[64,6,1,128]{3,0,2,1:T(8,128)(2,1)S(1)}, bf16[64,6,1,128]{3,0,2,1:T(8,128)(2,1)S(1)}, u32[]{:S(2)}, u32[]{:S(2)}) collective-permute-start(bf16[64,6,1,128]{3,0,2,1:T(8,128)(2,1)S(1)} %get-tuple-element.188), channel_id=1, source_target_pairs={{1,0},{2,1},{3,2},{4,3},{5,4},{6,5},{7,6},{8,7},{9,8},{10,9},{11,1... | collective-permute-start | bytes 294920 | tf_op jit(solution)/shard_map/ppermute | solution.py:18
Sparse Core Ops, SparseCore 0:
  94.7 271.6 all-reduce.3
where the time goes:
time: 377 us
  waiting for transfers between devices  274 us (73%)
  starting transfers between devices  40.8 us (11%)
  matrix products  20.1 us (5%)
  local copies, waits for them, and re-layouts  17.8 us (5%)
  between operations  14.7 us (4%)
  other arithmetic  9.84 us (3%)
    psum x1, waiting for transfers between devices, body(): summed_conv, summed_down = lax.psum((local_conv, local_down), ('gz', 'gy'))  270 us
    ppermute x4, starting transfers between devices, extended(): lax.ppermute(head, axis, [((i + 1) % count, i) for i in range(count)])  27.8 us
    ppermute x4, starting transfers between devices, extended(): lax.ppermute(tail, axis, [(i, (i + 1) % count) for i in range(count)])  13 us
    dot_general x9, matrix products, body(): jnp.einsum('ozyx,jzyx->oj', gate_grad, window, preferred_element_type=jnp...  8.38 us
    dot_general x9, matrix products, body(): jnp.einsum('oj,ozyx->jzyx', conv_weight[tap_z, tap_y], gate_grad, preferr...  8.23 us
  transfers between devices with their start and end apart: 9, of which 2 were waited for; matrix products, arithmetic and copies ran while one was open for 3% of the time, Pallas kernels for 0%

commit v1 on v0

--- a/solution.py
+++ b/solution.py
@@ -1,9 +1,16 @@
+import functools
 import math
 
 import jax
 import jax.numpy as jnp
 from jax import lax
+from jax.experimental import pallas as pl
+from jax.experimental.pallas import tpu as pltpu
 from jax.sharding import PartitionSpec as P
+
+MESH_ID = pl.DeviceIdType.MESH
+BIT_ORDER = (("gy", 0), ("gy", 1), ("gz", 0), ("gz", 3), ("gy", 2), ("gz", 1), ("gz", 4), ("gz", 2), ("gy", 3))
+HALVINGS = 4
 
 
 def extended(cells, sides, width):
@@ -31,6 +38,100 @@
     result = result + spread[channels : 2 * channels]
     result = result + jnp.roll(spread[2 * channels : 3 * channels], 1, axis=3)
     return result
+
+
+def mesh_bits():
+    sizes = {"gz": lax.axis_size("gz"), "gy": lax.axis_size("gy")}
+    return [(axis, b) for axis, b in BIT_ORDER if (1 << b) < sizes[axis]]
+
+
+def allreduce_kernel(bits, halvings, x_ref, o_ref, *scratch):
+    halve_bufs = scratch[:halvings]
+    work, double_buf, send_sems, recv_sems = scratch[halvings:]
+    here = {"gz": lax.axis_index("gz"), "gy": lax.axis_index("gy")}
+
+    def bit_of(axis, b):
+        return (here[axis] // (1 << b)) % 2
+
+    def partner(axis, b):
+        flip = here[axis] + (1 - 2 * bit_of(axis, b)) * (1 << b)
+        return (flip, here["gy"]) if axis == "gz" else (here["gz"], flip)
+
+    barrier = pltpu.get_barrier_semaphore()
+    for axis, b in bits:
+        pl.semaphore_signal(barrier, inc=1, device_id=partner(axis, b), device_id_type=MESH_ID)
+    pl.semaphore_wait(barrier, len(bits))
+
+    def exchange(step, axis, b, src, dst):
+        copy = pltpu.make_async_remote_copy(
+            src_ref=src,
+            dst_ref=dst,
+            send_sem=send_sems.at[step],
+            recv_sem=recv_sems.at[step],
+            device_id=partner(axis, b),
+            device_id_type=MESH_ID,
+        )
+        copy.start()
+        copy.wait()
+
+    lo, length, step = 0, o_ref.shape[0], 0
+    for k in range(halvings):
+        axis, b = bits[k]
+        half = length // 2
+        bit = bit_of(axis, b)
+        keep = pl.multiple_of(lo + bit * half, 8)
+        give = pl.multiple_of(lo + (1 - bit) * half, 8)
+        source = x_ref if k == 0 else work
+        exchange(step, axis, b, source.at[pl.ds(give, half)], halve_bufs[k])
+        work[pl.ds(keep, half)] = source[pl.ds(keep, half)] + halve_bufs[k][...]
+        lo, length, step = keep, half, step + 1
+    for j, (axis, b) in enumerate(bits[halvings:]):
+        exchange(step, axis, b, work.at[pl.ds(lo, length)], double_buf.at[j])
+        work[pl.ds(lo, length)] = work[pl.ds(lo, length)] + double_buf[j]
+        step += 1
+    o_ref[pl.ds(lo, length)] = work[pl.ds(lo, length)]
+    for k in reversed(range(halvings)):
+        axis, b = bits[k]
+        region = o_ref.at[pl.ds(lo, length)]
+        exchange(step, axis, b, region, region)
+        lo = pl.multiple_of(lo - bit_of(axis, b) * length, 8)
+        length, step = length * 2, step + 1
+
+
+def allreduce(flat, halvings=HALVINGS):
+    bits = mesh_bits()
+    halvings = min(halvings, len(bits))
+    rows = flat.shape[0]
+    segment = rows >> halvings
+    steps = len(bits) + halvings
+    scratch = [pltpu.VMEM((rows >> (k + 1), 128), jnp.float32) for k in range(halvings)]
+    scratch += [
+        pltpu.VMEM(flat.shape, jnp.float32),
+        pltpu.VMEM((max(len(bits) - halvings, 1), segment, 128), jnp.float32),
+        pltpu.SemaphoreType.DMA((steps,)),
+        pltpu.SemaphoreType.DMA((steps,)),
+    ]
+    return pl.pallas_call(
+        functools.partial(allreduce_kernel, bits, halvings),
+        out_shape=jax.ShapeDtypeStruct(flat.shape, jnp.float32),
+        in_specs=[pl.BlockSpec(memory_space=pltpu.VMEM)],
+        out_specs=pl.BlockSpec(memory_space=pltpu.VMEM),
+        scratch_shapes=scratch,
+        compiler_params=pltpu.CompilerParams(collective_id=0, has_side_effects=True),
+    )(flat)
+
+
+def summed_gradients(local_conv, local_down):
+    sizes = (local_conv.size, local_down.size)
+    flat = jnp.concatenate([local_conv.reshape(-1), local_down.reshape(-1)])
+    unit = 128 * 8 << HALVINGS
+    padded = -(-flat.size // unit) * unit
+    flat = jnp.pad(flat, (0, padded - flat.size)).reshape(-1, 128)
+    total = allreduce(flat).reshape(-1)
+    return (
+        total[: sizes[0]].reshape(local_conv.shape),
+        total[sizes[0] : sizes[0] + sizes[1]].reshape(local_down.shape),
+    )
 
 
 def body(features, conv_weight, down_weight, cotangent):
@@ -96,7 +197,7 @@
     row_fold = plane_fold[:, :, 2 : row_count + 2]
     row_fold = row_fold.at[:, :, 0].add(plane_fold[:, :, 0])
     row_fold = row_fold.at[:, :, row_count - 1].add(plane_fold[:, :, row_count + 3])
-    summed_conv, summed_down = lax.psum((local_conv, local_down), ("gz", "gy"))
+    summed_conv, summed_down = summed_gradients(local_conv, local_down)
     grad_conv = summed_conv * grad_scale
     grad_down = summed_down * grad_scale
     return (section_out, row_fold, grad_conv, grad_down)

time: 377 us -> 160 us (0.42)
  the two profiles are of different devices: /device:TPU:1 before, /device:TPU:15 now
where the time goes in v1:
time: 160 us; the launch traced here: 159 us
  Pallas kernels  50.8 us (32%)
  starting transfers between devices  39.4 us (25%)
  local copies, waits for them, and re-layouts  21.6 us (14%)
  waiting for transfers between devices  19.6 us (12%)
  matrix products  15.2 us (10%)
  other arithmetic  11 us (7%)
    pallas_call x1, Pallas kernels, allreduce(): pl.pallas_call(functools.partial(allreduce_kernel, bits, halvings), out_s...  50.8 us
    ppermute x4, starting transfers between devices, extended(): lax.ppermute(tail, axis, [(i, (i + 1) % count) for i in range(count)])  23.3 us
    ppermute x4, waiting for transfers between devices, extended(): lax.ppermute(head, axis, [((i + 1) % count, i) for i in range(count)])  19.6 us
    ppermute x4, starting transfers between devices, extended(): lax.ppermute(head, axis, [((i + 1) % count, i) for i in range(count)])  16.1 us
    dot_general x9, matrix products, body(): jnp.einsum('oj,ozyx->jzyx', conv_weight[tap_z, tap_y], gate_grad, preferr...  8.29 us
    unnamed x22, local copies, waits for them, and re-layouts  5.44 us
    dot_general x9, matrix products, body(): jnp.einsum('ozyx,jzyx->oj', gate_grad, window, preferred_element_type=jnp...  3.4 us
  transfers between devices with their start and end apart: 8, of which 2 were waited for; matrix products, arithmetic and copies ran while one was open for 6% of the time, Pallas kernels for 0%

profile of v1, /device:TPU:15, one launch (start us, length us, event | category | flops | bytes accessed | tf_op | source)
XLA Modules:
  0.0 158.9 jit_solution(11457402058172521977)
XLA Ops:
  0.6 1.0 fusion.104
  1.6 4.0 %collective-permute-start = (bf16[64,1,8,128]{3,0,2,1:T(8,128)(2,1)S(1)}, bf16[64,1,8,128]{3,0,2,1:T(8,128)(2,1)S(1)}, u32[]{:S(2)}, u32[]{:S(2)}) collective-permute-start(bf16[64,1,8,128]{3,0,2,1:T(8,128)(2,1)S(1)} %copy.160), channel_id=1, source_target_pairs={{0,16},{16,32},{32,48},{48,64},{64,80},{80,96},{96,112},{112,128},... | collective-permute-start | bytes 393224 | tf_op jit(solution)/shard_map/ppermute | solution.py:23
  5.7 8.5 %collective-permute-start.1 = (bf16[64,1,8,128]{3,0,2,1:T(8,128)(2,1)S(1)}, bf16[64,1,8,128]{3,0,2,1:T(8,128)(2,1)S(1)}, u32[]{:S(2)}, u32[]{:S(2)}) collective-permute-start(bf16[64,1,8,128]{3,0,2,1:T(8,128)(2,1)S(1)} %copy.161), channel_id=1, source_target_pairs={{16,0},{32,16},{48,32},{64,48},{80,64},{96,80},{112,96},{128,112},... | collective-permute-start | bytes 393224 | tf_op jit(solution)/shard_map/ppermute | solution.py:25
  14.2 1.0 copy.73
  15.2 1.0 copy.74
  16.2 0.3 convolution_bitcast_fusion.1
  16.6 0.6 fusion.105
  17.2 0.8 copy.75
  18.0 0.3 copy.76
  18.3 0.8 and_reduce_fusion
  19.3 8.2 %collective-permute-start.2 = (bf16[64,4,1,128]{3,0,2,1:T(8,128)(2,1)S(1)}, bf16[64,4,1,128]{3,0,2,1:T(8,128)(2,1)S(1)}, u32[]{:S(2)}, u32[]{:S(2)}) collective-permute-start(bf16[64,4,1,128]{3,0,2,1:T(8,128)(2,1)S(1)} %get-tuple-element.195), channel_id=1, source_target_pairs={{0,1},{1,2},{2,3},{3,4},{4,5},{5,6},{6,7},{7,8},{8,9},{9,10},{10,1... | collective-permute-start | bytes 196616 | tf_op jit(solution)/shard_map/ppermute | solution.py:23
  27.5 1.9 %collective-permute-start.3 = (bf16[64,4,1,128]{3,0,2,1:T(8,128)(2,1)S(1)}, bf16[64,4,1,128]{3,0,2,1:T(8,128)(2,1)S(1)}, u32[]{:S(2)}, u32[]{:S(2)}) collective-permute-start(bf16[64,4,1,128]{3,0,2,1:T(8,128)(2,1)S(1)} %get-tuple-element.196), channel_id=1, source_target_pairs={{1,0},{2,1},{3,2},{4,3},{5,4},{6,5},{7,6},{8,7},{9,8},{10,9},{11,1... | collective-permute-start | bytes 196616 | tf_op jit(solution)/shard_map/ppermute | solution.py:25
  29.4 0.6 fusion.106
  30.0 9.8 %collective-permute-done.3 = bf16[64,4,1,128]{3,0,2,1:T(8,128)(2,1)S(1)} collective-permute-done((bf16[64,4,1,128]{3,0,2,1:T(8,128)(2,1)S(1)}, bf16[64,4,1,128]{3,0,2,1:T(8,128)(2,1)S(1)}, u32[]{:S(2)}, u32[]{:S(2)}) %collective-permute-start.3) | collective-permute-done | bytes 65568 | tf_op jit(solution)/shard_map/ppermute | solution.py:25
  39.9 0.3 fusion.101
  40.2 0.3 fusion.102
  40.5 1.4 maximum_maximum_fusion
  41.9 0.3 fusion.36
  42.2 0.3 fusion.39
  44.0 1.8 %fusion.99 = (bf16[192,2,8,128]{3,0,2,1:T(8,128)(2,1)S(1)}, bf16[192,2,8,128]{3,0,2,1:T(8,128)(2,1)S(1)}, bf16[192,2,8,128]{3,0,2,1:T(8,128)(2,1)S(1)}, bf16[192...) fusion(bf16[192,4,10,128]{3,0,2,1:T(8,128)(2,1)S(1)} %maximum_m, ...), kind=kLoop, calls=%fused_computation.148 | loop fusion | bytes 14155776 | tf_op jit(solution)/shard_map/slice | solution.py:147
  45.8 0.5 multiply_convert_fusion
  46.3 0.4 convolution_bitcast_fusion
  46.7 0.4 scatter-add.44
  47.1 1.8 %fusion.7 = f32[192,4,10,128]{3,0,2,1:T(8,128)S(1)} fusion(f32[192,4,10,128]{3,0,2,1:T(8,128)S(1)} %scatter-add.44, s32[]{:T(128)} %bitcast.45, s32[]{:T(128)} %bitcast.46, bf16[64,2,8,128]{3,0,2,1:T(8,128)(2,1)S(1)} %get-tuple-element.193, bf16[3,3,64,192]{3,2,1,0:T(8,128)(2,1)S(1)} %copy-done.2), kind=kOutput, calls=%fused_computation.16 | convolution fusion | flops 50724864 | bytes 3440648 | tf_op jit(solution)/shard_map/oj,ozyx->jzyx/dot_general | solution.py:185
  48.9 2.5 %fusion = f32[192,4,10,128]{3,0,2,1:T(8,128)S(1)} fusion(f32[192,4,10,128]{3,0,2,1:T(8,128)S(1)} %fusion.7, s32[]{:T(128)} %bitcast.50, s32[]{:T(128)} %bitcast.51, bf16[64,2,8,128]{3,0,2,1:T(8,128)(2,1)S(1)} %get-tuple-element.193, pred[]{:T(512)} %and_reduce_fusion, bf16[3,3,64,192]{3,2,1,0:T(8,128)(2,1)S(1)} %copy-done.2), kind=kOutput, calls=%fused_computation.2 | convolution fusion | flops 51118080 | bytes 3440649 | tf_op jit(solution)/shard_map/oj,ozyx->jzyx/dot_general | solution.py:185
  51.4 0.6 fusion.6
  52.0 0.6 fusion.5
  52.6 0.6 fusion.4
  53.2 0.6 fusion.3
  53.8 0.6 fusion.2
  54.4 0.6 fusion.1
  55.1 0.5 fusion.97
  55.5 1.4 copy-done
  56.9 2.0 %fusion.98 = (f32[64,4,10,127]{3,0,2,1:T(8,128)}, f32[64,4,10,127]{3,0,2,1:T(8,128)}) fusion(f32[192,4,10,128]{3,0,2,1:T(8,128)S(1)} %fusion.1), kind=kLoop, calls=%fused_computation.147 | loop fusion | bytes 5201920 | tf_op jit(solution)/shard_map/jit(_roll_static)/slice | solution.py:39
  58.9 0.4 convolution_bitcast_fusion.10
  59.3 0.4 convolution_bitcast_fusion.11
  59.7 0.4 convolution_bitcast_fusion.12
  60.1 0.4 convolution_bitcast_fusion.7
  60.4 0.4 convolution_bitcast_fusion.8
  60.8 0.4 convolution_bitcast_fusion.9
  61.2 0.4 convolution_bitcast_fusion.4
  61.6 0.4 convolution_bitcast_fusion.5
  62.0 0.4 convolution_bitcast_fusion.6
  62.4 1.1 reshape.553
  63.5 0.3 copy.71
  63.8 0.3 convolution_bitcast_fusion.2
  64.2 1.0 copy.96
  65.2 1.3 reshape_reshape.3
  66.5 1.9 %fusion.29.x_ref = f32[1408,128]{1,0:T(8,128)} fusion(f32[65536]{0:T(1024)S(1)} %reshape_reshape.3, f32[110592]{0:T(1024)} %reshape.553), kind=kLoop, calls=%fused_computation.55 | loop fusion | flops 720896 | bytes 1425408 | tf_op jit(solution)/shard_map/reshape | solution.py:129
  68.4 50.8 %shard_map.75 = f32[1408,128]{1,0:T(8,128)} custom-call(f32[1408,128]{1,0:T(8,128)} %fusion.29.x_ref), custom_call_target="tpu_custom_call" | custom-call | tf_op jit(solution)/shard_map/pallas_call | solution.py:114
  119.2 1.8 %slice_multiply_fusion = f32[864,128]{1,0:T(8,128)} fusion(f32[1408,128]{1,0:T(8,128)} %shard_map.75), kind=kLoop, calls=%fused_computation.63 | loop fusion | flops 110592 | bytes 884736 | tf_op jit(solution)/shard_map/mul | solution.py:201
  121.0 2.0 %mul.37 = f32[3,3,64,192]{3,2,1,0:T(8,128)} reshape(f32[864,128]{1,0:T(8,128)} %slice_multiply_fusion) | data formatting | bytes 884736 | tf_op jit(solution)/shard_map/mul | solution.py:201
  123.0 2.8 %fusion.9 = bf16[64,4,10,128]{3,0,2,1:T(8,128)(2,1)S(1)} fusion(f32[192,4,10,128]{3,0,2,1:T(8,128)} %copy-done, f32[64,4,10,1]{3,0,2,1:T(8,128)S(1)} %get-tuple-element.173, f32[64,4,10,127]{3,0,2,1:T(8,128)} %get-tuple-element.175, f32[64,4,10,127]{3,0,2,1:T(8,128)} %get-tuple-element.174, f32[64,4,10,1]{3,0,2,1:T(8,128)S(1)} %get-tuple-element.172), kind=kLoop, calls=%fused_computation.21 | loop fusion | flops 1638400 | bytes 4587520 | tf_op jit(solution)/shard_map/convert_element_type | solution.py:193
  125.9 3.7 %collective-permute-start.4 = (bf16[64,1,10,128]{3,0,2,1:T(8,128)(2,1)S(1)}, bf16[64,1,10,128]{3,0,2,1:T(8,128)(2,1)S(1)}, u32[]{:S(2)}, u32[]{:S(2)}) collective-permute-start(bf16[64,1,10,128]{3,0,2,1:T(8,128)(2,1)S(1)} %get-tuple-element.187), channel_id=1, source_target_pairs={{0,16},{16,32},{32,48},{48,64},{64,80},{80,96},{96,112},{112,128},... | collective-permute-start | bytes 491528 | tf_op jit(solution)/shard_map/ppermute | solution.py:23
  129.6 3.8 %collective-permute-start.5 = (bf16[64,1,10,128]{3,0,2,1:T(8,128)(2,1)S(1)}, bf16[64,1,10,128]{3,0,2,1:T(8,128)(2,1)S(1)}, u32[]{:S(2)}, u32[]{:S(2)}) collective-permute-start(bf16[64,1,10,128]{3,0,2,1:T(8,128)(2,1)S(1)} %get-tuple-element.188), channel_id=1, source_target_pairs={{16,0},{32,16},{48,32},{64,48},{80,64},{96,80},{112,96},{128,112},... | collective-permute-start | bytes 491528 | tf_op jit(solution)/shard_map/ppermute | solution.py:25
  133.5 1.5 copy.72
  135.0 0.3 dot_general.118
  135.3 1.7 %slice_multiply_fusion.1 = f32[512,128]{1,0:T(8,128)} fusion(f32[1408,128]{1,0:T(8,128)} %shard_map.75), kind=kLoop, calls=%fused_computation.68 | loop fusion | flops 65536 | bytes 524288 | tf_op jit(solution)/shard_map/mul | solution.py:202
  137.0 7.4 %collective-permute-start.6 = (bf16[64,6,1,128]{3,0,2,1:T(8,128)(2,1)S(1)}, bf16[64,6,1,128]{3,0,2,1:T(8,128)(2,1)S(1)}, u32[]{:S(2)}, u32[]{:S(2)}) collective-permute-start(bf16[64,6,1,128]{3,0,2,1:T(8,128)(2,1)S(1)} %get-tuple-element.185), channel_id=1, source_target_pairs={{0,1},{1,2},{2,3},{3,4},{4,5},{5,6},{6,7},{7,8},{8,9},{9,10},{10,1... | collective-permute-start | bytes 294920 | tf_op jit(solution)/shard_map/ppermute | solution.py:23
  144.4 1.9 %collective-permute-start.7 = (bf16[64,6,1,128]{3,0,2,1:T(8,128)(2,1)S(1)}, bf16[64,6,1,128]{3,0,2,1:T(8,128)(2,1)S(1)}, u32[]{:S(2)}, u32[]{:S(2)}) collective-permute-start(bf16[64,6,1,128]{3,0,2,1:T(8,128)(2,1)S(1)} %get-tuple-element.186), channel_id=1, source_target_pairs={{1,0},{2,1},{3,2},{4,3},{5,4},{6,5},{7,6},{8,7},{9,8},{10,9},{11,1... | collective-permute-start | bytes 294920 | tf_op jit(solution)/shard_map/ppermute | solution.py:25
  146.3 0.3 fusion.19
  146.6 0.7 copy.97
  147.4 9.8 %collective-permute-done.7 = bf16[64,6,1,128]{3,0,2,1:T(8,128)(2,1)S(1)} collective-permute-done((bf16[64,6,1,128]{3,0,2,1:T(8,128)(2,1)S(1)}, bf16[64,6,1,128]{3,0,2,1:T(8,128)(2,1)S(1)}, u32[]{:S(2)}, u32[]{:S(2)}) %collective-permute-start.7) | collective-permute-done | bytes 98336 | tf_op jit(solution)/shard_map/ppermute | solution.py:25
  157.8 1.1 copy.98
  (46 shorter events, 2.5 us)
Async XLA Ops:
  1.6 17.5 %collective-permute-start = (bf16[64,1,8,128]{3,0,2,1:T(8,128)(2,1)S(1)}, bf16[64,1,8,128]{3,0,2,1:T(8,128)(2,1)S(1)}, u32[]{:S(2)}, u32[]{:S(2)}) collective-permute-start(bf16[64,1,8,128]{3,0,2,1:T(8,128)(2,1)S(1)} %copy.160), channel_id=1, source_target_pairs={{0,16},{16,32},{32,48},{48,64},{64,80},{80,96},{96,112},{112,128},... | collective-permute-start | bytes 393224 | tf_op jit(solution)/shard_map/ppermute | solution.py:23
  5.7 13.5 %collective-permute-start.1 = (bf16[64,1,8,128]{3,0,2,1:T(8,128)(2,1)S(1)}, bf16[64,1,8,128]{3,0,2,1:T(8,128)(2,1)S(1)}, u32[]{:S(2)}, u32[]{:S(2)}) collective-permute-start(bf16[64,1,8,128]{3,0,2,1:T(8,128)(2,1)S(1)} %copy.161), channel_id=1, source_target_pairs={{16,0},{32,16},{48,32},{64,48},{80,64},{96,80},{112,96},{128,112},... | collective-permute-start | bytes 393224 | tf_op jit(solution)/shard_map/ppermute | solution.py:25
  15.2 1.3 copy-start.4
  16.6 1.7 %copy-start.6 = (s32[4]{0:T(128)S(1)}, s32[4]{0:T(128)}, u32[]{:S(2)}) copy-start(s32[4]{0:T(128)} %constant.378.clone.1) | copy-start | bytes 52
  17.2 2.0 %copy-start.3 = (bf16[64,2,8,128]{3,2,1,0:T(8,128)(2,1)S(1)}, bf16[64,2,8,128]{3,2,1,0:T(8,128)(2,1)}, u32[]{:S(2)}) copy-start(bf16[64,2,8,128]{3,2,1,0:T(8,128)(2,1)} %param.30) | copy-start | bytes 786436
  19.3 10.7 %collective-permute-start.2 = (bf16[64,4,1,128]{3,0,2,1:T(8,128)(2,1)S(1)}, bf16[64,4,1,128]{3,0,2,1:T(8,128)(2,1)S(1)}, u32[]{:S(2)}, u32[]{:S(2)}) collective-permute-start(bf16[64,4,1,128]{3,0,2,1:T(8,128)(2,1)S(1)} %get-tuple-element.195), channel_id=1, source_target_pairs={{0,1},{1,2},{2,3},{3,4},{4,5},{5,6},{6,7},{7,8},{8,9},{9,10},{10,1... | collective-permute-start | bytes 196616 | tf_op jit(solution)/shard_map/ppermute | solution.py:23
  27.5 12.3 %collective-permute-start.3 = (bf16[64,4,1,128]{3,0,2,1:T(8,128)(2,1)S(1)}, bf16[64,4,1,128]{3,0,2,1:T(8,128)(2,1)S(1)}, u32[]{:S(2)}, u32[]{:S(2)}) collective-permute-start(bf16[64,4,1,128]{3,0,2,1:T(8,128)(2,1)S(1)} %get-tuple-element.196), channel_id=1, source_target_pairs={{1,0},{2,1},{3,2},{4,3},{5,4},{6,5},{7,6},{8,7},{9,8},{10,9},{11,1... | collective-permute-start | bytes 196616 | tf_op jit(solution)/shard_map/ppermute | solution.py:25
  40.5 1.4 copy-start.2
  55.1 1.9 %copy-start = (f32[192,4,10,128]{3,0,2,1:T(8,128)}, f32[192,4,10,128]{3,0,2,1:T(8,128)S(1)}, u32[]{:S(2)}) copy-start(f32[192,4,10,128]{3,0,2,1:T(8,128)S(1)} %fusion.1) | copy-start | bytes 11796484
  63.8 55.4 %copy-start.1 = (bf16[64,2,8,128]{0,3,2,1:T(8,128)(2,1)}, bf16[64,2,8,128]{0,3,2,1:T(8,128)(2,1)S(1)}, u32[]{:S(2)}) copy-start(bf16[64,2,8,128]{0,3,2,1:T(8,128)(2,1)S(1)} %copy.71) | copy-start | bytes 786436
  125.9 20.5 %copy-start.5 = (bf16[2,2,128,128]{2,3,1,0:T(8,128)(2,1)S(1)}, bf16[2,2,128,128]{2,3,1,0:T(8,128)(2,1)}, u32[]{:S(2)}) copy-start(bf16[2,2,128,128]{2,3,1,0:T(8,128)(2,1)} %copy-done.4) | copy-start | bytes 393220
  125.9 11.1 %collective-permute-start.4 = (bf16[64,1,10,128]{3,0,2,1:T(8,128)(2,1)S(1)}, bf16[64,1,10,128]{3,0,2,1:T(8,128)(2,1)S(1)}, u32[]{:S(2)}, u32[]{:S(2)}) collective-permute-start(bf16[64,1,10,128]{3,0,2,1:T(8,128)(2,1)S(1)} %get-tuple-element.187), channel_id=1, source_target_pairs={{0,16},{16,32},{32,48},{48,64},{64,80},{80,96},{96,112},{112,128},... | collective-permute-start | bytes 491528 | tf_op jit(solution)/shard_map/ppermute | solution.py:23
  129.6 7.3 %collective-permute-start.5 = (bf16[64,1,10,128]{3,0,2,1:T(8,128)(2,1)S(1)}, bf16[64,1,10,128]{3,0,2,1:T(8,128)(2,1)S(1)}, u32[]{:S(2)}, u32[]{:S(2)}) collective-permute-start(bf16[64,1,10,128]{3,0,2,1:T(8,128)(2,1)S(1)} %get-tuple-element.188), channel_id=1, source_target_pairs={{16,0},{32,16},{48,32},{64,48},{80,64},{96,80},{112,96},{128,112},... | collective-permute-start | bytes 491528 | tf_op jit(solution)/shard_map/ppermute | solution.py:25
  137.0 10.3 %collective-permute-start.6 = (bf16[64,6,1,128]{3,0,2,1:T(8,128)(2,1)S(1)}, bf16[64,6,1,128]{3,0,2,1:T(8,128)(2,1)S(1)}, u32[]{:S(2)}, u32[]{:S(2)}) collective-permute-start(bf16[64,6,1,128]{3,0,2,1:T(8,128)(2,1)S(1)} %get-tuple-element.185), channel_id=1, source_target_pairs={{0,1},{1,2},{2,3},{3,4},{4,5},{5,6},{6,7},{7,8},{8,9},{9,10},{10,1... | collective-permute-start | bytes 294920 | tf_op jit(solution)/shard_map/ppermute | solution.py:23
  144.4 12.8 %collective-permute-start.7 = (bf16[64,6,1,128]{3,0,2,1:T(8,128)(2,1)S(1)}, bf16[64,6,1,128]{3,0,2,1:T(8,128)(2,1)S(1)}, u32[]{:S(2)}, u32[]{:S(2)}) collective-permute-start(bf16[64,6,1,128]{3,0,2,1:T(8,128)(2,1)S(1)} %get-tuple-element.186), channel_id=1, source_target_pairs={{1,0},{2,1},{3,2},{4,3},{5,4},{6,5},{7,6},{8,7},{9,8},{10,9},{11,1... | collective-permute-start | bytes 294920 | tf_op jit(solution)/shard_map/ppermute | solution.py:25

commit v2 on v1

--- a/solution.py
+++ b/solution.py
@@ -38,6 +38,87 @@
     result = result + spread[channels : 2 * channels]
     result = result + jnp.roll(spread[2 * channels : 3 * channels], 1, axis=3)
     return result
+
+
+NEIGHBOURS = ((1, 0), (-1, 0), (0, 1), (0, -1), (1, 1), (1, -1), (-1, 1), (-1, -1))
+
+
+def halo_kernel(offsets, *refs):
+    count = len(offsets)
+    sources, targets = refs[:count], refs[count : 2 * count]
+    send_sems, recv_sems = refs[2 * count :]
+    sizes = (lax.axis_size("gz"), lax.axis_size("gy"))
+    here = (lax.axis_index("gz"), lax.axis_index("gy"))
+
+    def device(dz, dy):
+        return ((here[0] + dz + sizes[0]) % sizes[0], (here[1] + dy + sizes[1]) % sizes[1])
+
+    barrier = pltpu.get_barrier_semaphore()
+    for dz, dy in offsets:
+        pl.semaphore_signal(barrier, inc=1, device_id=device(dz, dy), device_id_type=MESH_ID)
+    pl.semaphore_wait(barrier, count)
+    copies = []
+    for i, (dz, dy) in enumerate(offsets):
+        copy = pltpu.make_async_remote_copy(
+            src_ref=sources[i],
+            dst_ref=targets[i],
+            send_sem=send_sems.at[i],
+            recv_sem=recv_sems.at[i],
+            device_id=device(dz, dy),
+            device_id_type=MESH_ID,
+        )
+        copy.start()
+        copies.append(copy)
+    for copy in copies:
+        copy.wait()
+
+
+def halo_swap(pieces, collective_id):
+    flat = [p.reshape(-1, 128) for p in pieces]
+    vmem = pl.BlockSpec(memory_space=pltpu.VMEM)
+    got = pl.pallas_call(
+        functools.partial(halo_kernel, NEIGHBOURS),
+        out_shape=[jax.ShapeDtypeStruct(f.shape, f.dtype) for f in flat],
+        in_specs=[vmem] * len(flat),
+        out_specs=[vmem] * len(flat),
+        scratch_shapes=[pltpu.SemaphoreType.DMA((len(flat),)), pltpu.SemaphoreType.DMA((len(flat),))],
+        compiler_params=pltpu.CompilerParams(collective_id=collective_id, has_side_effects=True),
+    )(*flat)
+    return [g.reshape(p.shape) for g, p in zip(got, pieces)]
+
+
+def ranges(shift, count, border):
+    if shift == 1:
+        return slice(border + count - 1, border + count)
+    if shift == -1:
+        return slice(border, border + 1)
+    return slice(border, border + count)
+
+
+def framed_features(features):
+    _, planes, rows, _ = features.shape
+    pieces = [features[:, ranges(dz, planes, 0), ranges(dy, rows, 0)] for dz, dy in NEIGHBOURS]
+    got = dict(zip(NEIGHBOURS, halo_swap(pieces, 1)))
+    lines = []
+    for dz in (1, 0, -1):
+        middle = features if dz == 0 else got[(dz, 0)]
+        lines.append(jnp.concatenate([got[(dz, 1)], middle, got[(dz, -1)]], axis=2))
+    return jnp.concatenate(lines, axis=1)
+
+
+def folded_grad(spread):
+    _, planes, rows, _ = spread.shape
+    planes, rows = planes - 2, rows - 2
+    own = spread[:, 1 : planes + 1, 1 : rows + 1]
+    pieces = []
+    for dz, dy in NEIGHBOURS:
+        zs = slice(planes + 1, planes + 2) if dz == 1 else slice(0, 1) if dz == -1 else slice(1, planes + 1)
+        ys = slice(rows + 1, rows + 2) if dy == 1 else slice(0, 1) if dy == -1 else slice(1, rows + 1)
+        pieces.append(spread[:, zs, ys].astype(jnp.bfloat16))
+    got = halo_swap(pieces, 2)
+    for (dz, dy), piece in zip(NEIGHBOURS, got):
+        own = own.at[:, ranges(-dz, planes, 0), ranges(-dy, rows, 0)].add(piece.astype(own.dtype))
+    return own
 
 
 def mesh_bits():
@@ -139,7 +220,7 @@
     out_channels = down_weight.shape[2]
     cell_count = plane_count * row_count * breadth * lax.axis_size("gz") * lax.axis_size("gy")
     grad_scale = 1.0 / math.sqrt(cell_count)
-    framed = extended(features, (("gz", 1), ("gy", 2)), 1)
+    framed = framed_features(features)
     columns = widen(framed)
     preact = jnp.zeros((channels, plane_count, row_count, breadth), jnp.float32)
     for tap_z in range(3):
@@ -189,14 +270,7 @@
                 preferred_element_type=jnp.float32,
             )
             spread = spread.at[:, tap_z : tap_z + plane_count, tap_y : tap_y + row_count].add(term)
-    folded = fold_along(spread, channels)
-    bordered = extended(folded.astype(jnp.bfloat16), (("gz", 1), ("gy", 2)), 1).astype(folded.dtype)
-    plane_fold = bordered[:, 2 : plane_count + 2]
-    plane_fold = plane_fold.at[:, 0].add(bordered[:, 0])
-    plane_fold = plane_fold.at[:, plane_count - 1].add(bordered[:, plane_count + 3])
-    row_fold = plane_fold[:, :, 2 : row_count + 2]
-    row_fold = row_fold.at[:, :, 0].add(plane_fold[:, :, 0])
-    row_fold = row_fold.at[:, :, row_count - 1].add(plane_fold[:, :, row_count + 3])
+    row_fold = folded_grad(fold_along(spread, channels))
     summed_conv, summed_down = summed_gradients(local_conv, local_down)
     grad_conv = summed_conv * grad_scale
     grad_down = summed_down * grad_scale

time: 160 us -> 152 us (0.950)
  the two profiles are of different devices: /device:TPU:15 before, /device:TPU:1 now
where the time goes in v2:
time: 152 us; the launch traced here: 151 us
  Pallas kernels  92.1 us (61%)
  local copies, waits for them, and re-layouts  28 us (18%)
  matrix products  17.7 us (12%)
  other arithmetic  11.4 us (8%)
    pallas_call x1, Pallas kernels, allreduce(): pl.pallas_call(functools.partial(allreduce_kernel, bits, halvings), out_s...  52.4 us
    pallas_call x2, Pallas kernels, halo_swap(): pl.pallas_call(functools.partial(halo_kernel, NEIGHBOURS), out_shape=[jax...  39.7 us
    dot_general x9, matrix products, body(): jnp.einsum('oj,ozyx->jzyx', conv_weight[tap_z, tap_y], gate_grad, preferr...  8.19 us
    unnamed x59, local copies, waits for them, and re-layouts  5.83 us
    dot_general x9, matrix products, body(): jnp.einsum('oj,jzyx->ozyx', conv_weight[tap_z, tap_y], window, preferred_...  5.3 us
    reshape x4, local copies, waits for them, and re-layouts, halo_swap(): return [g.reshape(p.shape) for g, p in zip(got, pieces)]  3.38 us
    dot_general x9, matrix products, body(): jnp.einsum('ozyx,jzyx->oj', gate_grad, window, preferred_element_type=jnp...  3.34 us
    slice x1, local copies, waits for them, and re-layouts, body(): window = columns[:, tap_z:tap_z + plane_count, tap_y:tap_y + row_count]  3.04 us

profile of v2, /device:TPU:1, one launch (start us, length us, event | category | flops | bytes accessed | tf_op | source)
XLA Modules:
  0.0 150.6 jit_solution(16338200243883511782)
XLA Ops:
  0.6 1.0 copy.88
  1.7 0.6 slice_bitcast_fusion.6
  2.3 1.7 %slice_bitcast_fusion = (bf16[512,128]{1,0:T(8,128)(2,1)}, bf16[512,128]{1,0:T(8,128)(2,1)}) fusion(bf16[64,2,8,128]{3,2,1,0:T(8,128)(2,1)} %param.38), kind=kLoop, calls=%fused_computation.74 | loop fusion | bytes 524288 | tf_op jit(solution)/shard_map/reshape | solution.py:77
  4.0 1.1 fusion.95
  5.1 0.6 copy.155
  5.8 0.6 copy.156
  6.4 24.7 %shard_map.75 = (bf16[512,128]{1,0:T(8,128)(2,1)}, bf16[512,128]{1,0:T(8,128)(2,1)}, bf16[128,128]{1,0:T(8,128)(2,1)}, bf16[128,128]{1,0:T(8,128)(2,1)}, bf16[64...) custom-call(bf16[512,128]{1,0:T(8,128)(2,1)} %get-tuple-element.288.refs_0_, ...), custom_call_target="tpu_custom_call" | custom-call | tf_op jit(solution)/shard_map/pallas_call | solution.py:79
  31.1 0.9 copy.92
  32.1 0.9 copy.96
  33.0 0.8 copy.93
  33.8 0.8 copy.95
  34.5 0.9 maximum_maximum_fusion.1
  36.1 0.4 copy-done.13
  36.5 2.0 %maximum_maximum_fusion = bf16[192,4,10,128]{3,0,2,1:T(8,128)(2,1)S(1)} fusion(bf16[64,4,10,1]{3,0,2,1:T(8,128)(2,1)S(1)} %get-tuple-element.276, bf16[64,4,10,127]{3,0,2,1:T(8,128)(2,1)S(1)} %get-tuple-element.278, bf16[64,1,1,128]{3,0,2,1:T(8,128)(2,1)S(1)} %bitcast.314, bf16[64,1,8,128]{3,0,2,1:T(8,128)(2,1)S(1)} %copy.96, ...), kind=kLoop, calls=%fused_computation.1 | loop fusion | flops 25559040 | bytes 3932160 | tf_op jit(solution)/shard_map/concatenate | solution.py:33
  38.5 3.0 %fusion.90 = (bf16[192,2,8,128]{3,0,2,1:T(8,128)(2,1)}, bf16[192,2,8,128]{3,0,2,1:T(8,128)(2,1)}, bf16[192,2,8,128]{3,0,2,1:T(8,128)(2,1)}, bf16[192,2,8,128]{3,...) fusion(bf16[192,4,10,128]{3,0,2,1:T(8,128)(2,1)S(1)} %maximum_m, ...), kind=kLoop, calls=%fused_computation.162 | loop fusion | bytes 14155776 | tf_op jit(solution)/shard_map/slice | solution.py:228
  43.4 1.1 convolution_add_fusion.1
  45.1 0.8 copy.101
  45.9 1.1 copy.102
  47.0 2.4 %multiply_convert_fusion = (bf16[64,2,8,128]{3,0,2,1:T(8,128)(2,1)S(1)}, bf16[64,2,8,128]{3,0,2,1:T(8,128)(2,1)}) fusion(f32[64,2,8,128]{3,0,2,1:T(8,128)} %copy.102, f32[2,8,128,64]{2,3,1,0:T(8,128)} %convolution_add_fusion.1, bf16[192,4,10,128]{3,0,2,1:T(8,128)(2,1)S(1)} %maximum_maximum_fusion, bf16[3,3,64,192]{3,2,1,0:T(8,128)(2,1)S(1)} %copy-done), kind=kOutput, calls=%fused_computation.58 | convolution fusion | flops 51904512 | bytes 2392064 | tf_op jit(solution)/shard_map/oj,jzyx->ozyx/dot_general | solution.py:229
  49.5 0.4 convolution_bitcast_fusion.10
  49.8 0.4 convolution_bitcast_fusion.11
  50.2 0.4 copy-done.7
  50.6 0.4 convolution_bitcast_fusion.12
  51.0 0.4 convolution_bitcast_fusion.7
  51.4 0.4 convolution_bitcast_fusion.8
  51.8 0.4 convolution_bitcast_fusion.9
  52.2 0.4 copy-done.3
  52.5 0.4 convolution_bitcast_fusion.4
  52.9 0.4 convolution_bitcast_fusion.5
  53.4 0.4 convolution_bitcast_fusion.6
  55.5 0.9 fusion.21.x_ref
  56.4 52.4 %shard_map.77 = f32[1408,128]{1,0:T(8,128)} custom-call(f32[1408,128]{1,0:T(8,128)} %fusion.21.x_ref), custom_call_target="tpu_custom_call" | custom-call | tf_op jit(solution)/shard_map/pallas_call | solution.py:195
  108.8 1.0 slice_multiply_fusion
  109.8 1.0 mul.37
  110.8 1.7 %slice_multiply_fusion.1 = f32[512,128]{1,0:T(8,128)} fusion(f32[1408,128]{1,0:T(8,128)} %shard_map.77), kind=kLoop, calls=%fused_computation.66 | loop fusion | flops 65536 | bytes 524288 | tf_op jit(solution)/shard_map/mul | solution.py:276
  112.4 0.4 convolution_bitcast_fusion
  112.8 0.4 scatter-add.56
  113.3 0.6 fusion.98
  113.9 1.8 %fusion.7 = f32[192,4,10,128]{3,0,2,1:T(8,128)S(1)} fusion(f32[192,4,10,128]{3,0,2,1:T(8,128)S(1)} %scatter-add.56, s32[]{:T(128)} %bitcast.59, s32[]{:T(128)} %bitcast.60, bf16[64,2,8,128]{3,0,2,1:T(8,128)(2,1)S(1)} %get-tuple-element.279, bf16[3,3,64,192]{3,2,1,0:T(8,128)(2,1)S(1)} %copy-done), kind=kOutput, calls=%fused_computation.16 | convolution fusion | flops 50724864 | bytes 3440648 | tf_op jit(solution)/shard_map/oj,ozyx->jzyx/dot_general | solution.py:266
  115.7 0.8 and_reduce_fusion
  116.5 0.6 fusion.97
  117.1 2.4 %fusion = f32[192,4,10,128]{3,0,2,1:T(8,128)S(1)} fusion(f32[192,4,10,128]{3,0,2,1:T(8,128)S(1)} %fusion.7, s32[]{:T(128)} %bitcast.64, s32[]{:T(128)} %bitcast.65, bf16[64,2,8,128]{3,0,2,1:T(8,128)(2,1)S(1)} %get-tuple-element.279, pred[]{:T(512)} %get-tuple-element.296, bf16[3,3,64,192]{3,2,1,0:T(8,128)(2,1)S(1)} %copy-done), kind=kOutput, calls=%fused_computation.2 | convolution fusion | flops 51118080 | bytes 3440649 | tf_op jit(solution)/shard_map/oj,ozyx->jzyx/dot_general | solution.py:266
  119.5 0.6 fusion.6
  120.1 0.6 fusion.5
  120.7 0.6 fusion.4
  121.3 0.6 fusion.3
  121.9 0.6 fusion.2
  122.5 0.6 fusion.1
  123.2 0.7 fusion.88
  123.8 0.5 fusion.89
  124.3 0.8 fusion.86
  125.1 0.7 copy.201
  125.9 0.7 copy.202
  126.6 0.6 copy.105
  127.3 0.6 copy.106
  127.9 0.6 slice_bitcast_fusion.2
  128.5 14.9 %shard_map.76 = (bf16[512,128]{1,0:T(8,128)(2,1)}, bf16[512,128]{1,0:T(8,128)(2,1)}, bf16[128,128]{1,0:T(8,128)(2,1)}, bf16[128,128]{1,0:T(8,128)(2,1)}, bf16[64...) custom-call(bf16[512,128]{1,0:T(8,128)(2,1)} %bitcast.299, ...), custom_call_target="tpu_custom_call" | custom-call | tf_op jit(solution)/shard_map/pallas_call | solution.py:79
  143.5 1.0 bitcast_convert_fusion.1
  145.0 0.6 fusion.96
  145.6 2.0 %fusion.27 = f32[64,2,8,128]{3,0,2,1:T(8,128)S(1)} fusion(f32[64,2,8,128]{3,0,2,1:T(8,128)S(1)} %fusion.30, s32[]{:T(128)} %bitcast.100, s32[]{:T(128)} %bitcast.101, bf16[64,128]{1,0:T(8,128)(2,1)S(1)} %copy-done.23, pred[]{:T(512)} %get-tuple-element.295), kind=kLoop, calls=%fused_computation.81 | loop fusion | flops 24576 | bytes 81929 | tf_op jit(solution)/shard_map/scatter-add | solution.py:120
  147.6 1.1 copy.132
  148.7 0.5 copy.98
  149.2 0.3 dot_general.118
  149.8 0.7 copy.131
  (86 shorter events, 5.5 us)
Async XLA Ops:
  35.7 0.7 copy-start.13
  35.7 0.7 copy-start.14
  35.7 0.7 copy-start.15
  35.7 0.7 copy-start.16
  38.5 3.1 %copy-start = (bf16[3,3,64,192]{3,2,1,0:T(8,128)(2,1)S(1)}, bf16[3,3,64,192]{3,2,1,0:T(8,128)(2,1)}, u32[]{:S(2)}) copy-start(bf16[3,3,64,192]{3,2,1,0:T(8,128)(2,1)} %param.39) | copy-start | bytes 663556
  43.1 1.3 copy-start.12
  43.1 1.5 copy-start.17
  47.0 2.4 %copy-start.9 = (bf16[192,2,8,128]{3,0,2,1:T(8,128)(2,1)S(1)}, bf16[192,2,8,128]{3,0,2,1:T(8,128)(2,1)}, u32[]{:S(2)}) copy-start(bf16[192,2,8,128]{3,0,2,1:T(8,128)(2,1)} %get-tuple-element.265) | copy-start | bytes 2359300
  47.0 2.8 %copy-start.8 = (bf16[192,2,8,128]{3,0,2,1:T(8,128)(2,1)S(1)}, bf16[192,2,8,128]{3,0,2,1:T(8,128)(2,1)}, u32[]{:S(2)}) copy-start(bf16[192,2,8,128]{3,0,2,1:T(8,128)(2,1)} %get-tuple-element.266) | copy-start | bytes 2359300
  49.4 1.1 copy-start.7
  49.5 1.5 copy-start.6
  49.8 1.5 %copy-start.5 = (bf16[192,2,8,128]{3,0,2,1:T(8,128)(2,1)S(1)}, bf16[192,2,8,128]{3,0,2,1:T(8,128)(2,1)}, u32[]{:S(2)}) copy-start(bf16[192,2,8,128]{3,0,2,1:T(8,128)(2,1)} %get-tuple-element.263) | copy-start | bytes 2359300
  50.2 1.5 %copy-start.4 = (bf16[192,2,8,128]{3,0,2,1:T(8,128)(2,1)S(1)}, bf16[192,2,8,128]{3,0,2,1:T(8,128)(2,1)}, u32[]{:S(2)}) copy-start(bf16[192,2,8,128]{3,0,2,1:T(8,128)(2,1)} %get-tuple-element.264) | copy-start | bytes 2359300
  51.3 1.2 copy-start.3
  51.7 1.2 copy-start.2
  52.1 1.3 copy-start.1
  53.3 1.0 copy-start.10
  113.3 2.4 %copy-start.24 = (s32[4]{0:T(128)S(1)}, s32[4]{0:T(128)}, u32[]{:S(2)}) copy-start(s32[4]{0:T(128)} %constant.480.clone.1) | copy-start | bytes 52
  113.3 2.4 %copy-start.25 = (s32[4]{0:T(128)S(1)}, s32[4]{0:T(128)}, u32[]{:S(2)}) copy-start(s32[4]{0:T(128)} %constant.484.clone.1) | copy-start | bytes 52
  143.5 1.2 copy-start.11
  143.5 1.3 copy-start.19
  143.5 1.4 copy-start.18
  143.5 1.4 copy-start.22
  143.5 2.0 %copy-start.23 = (bf16[64,128]{1,0:T(8,128)(2,1)S(1)}, bf16[64,128]{1,0:T(8,128)(2,1)}, u32[]{:S(2)}) copy-start(bf16[64,128]{1,0:T(8,128)(2,1)} %get-tuple-element.237) | copy-start | bytes 49156
  144.5 3.0 %copy-start.21 = (bf16[64,128]{1,0:T(8,128)(2,1)S(1)}, bf16[64,128]{1,0:T(8,128)(2,1)}, u32[]{:S(2)}) copy-start(bf16[64,128]{1,0:T(8,128)(2,1)} %get-tuple-element.238) | copy-start | bytes 49156
  144.6 3.0 %copy-start.20 = (bf16[64,128]{1,0:T(8,128)(2,1)S(1)}, bf16[64,128]{1,0:T(8,128)(2,1)}, u32[]{:S(2)}) copy-start(bf16[64,128]{1,0:T(8,128)(2,1)} %get-tuple-element.239) | copy-start | bytes 49156

commit v3 on v2

--- a/solution.py
+++ b/solution.py
@@ -106,16 +106,21 @@
     return jnp.concatenate(lines, axis=1)
 
 
-def folded_grad(spread):
+def border_pieces(spread):
     _, planes, rows, _ = spread.shape
     planes, rows = planes - 2, rows - 2
-    own = spread[:, 1 : planes + 1, 1 : rows + 1]
     pieces = []
     for dz, dy in NEIGHBOURS:
         zs = slice(planes + 1, planes + 2) if dz == 1 else slice(0, 1) if dz == -1 else slice(1, planes + 1)
         ys = slice(rows + 1, rows + 2) if dy == 1 else slice(0, 1) if dy == -1 else slice(1, rows + 1)
         pieces.append(spread[:, zs, ys].astype(jnp.bfloat16))
-    got = halo_swap(pieces, 2)
+    return pieces
+
+
+def folded_grad(spread, got):
+    _, planes, rows, _ = spread.shape
+    planes, rows = planes - 2, rows - 2
+    own = spread[:, 1 : planes + 1, 1 : rows + 1]
     for (dz, dy), piece in zip(NEIGHBOURS, got):
         own = own.at[:, ranges(-dz, planes, 0), ranges(-dy, rows, 0)].add(piece.astype(own.dtype))
     return own
@@ -126,10 +131,18 @@
     return [(axis, b) for axis, b in BIT_ORDER if (1 << b) < sizes[axis]]
 
 
-def allreduce_kernel(bits, halvings, x_ref, o_ref, *scratch):
+def allreduce_kernel(bits, halvings, offsets, x_ref, *refs):
+    count = len(offsets)
+    pieces, o_ref = refs[:count], refs[count]
+    landed = refs[count + 1 : 2 * count + 1]
+    scratch = refs[2 * count + 1 :]
     halve_bufs = scratch[:halvings]
-    work, double_buf, send_sems, recv_sems = scratch[halvings:]
+    work, double_buf, send_sems, recv_sems, halo_send, halo_recv = scratch[halvings:]
     here = {"gz": lax.axis_index("gz"), "gy": lax.axis_index("gy")}
+    sizes = {"gz": lax.axis_size("gz"), "gy": lax.axis_size("gy")}
+
+    def neighbour(dz, dy):
+        return ((here["gz"] + dz + sizes["gz"]) % sizes["gz"], (here["gy"] + dy + sizes["gy"]) % sizes["gy"])
 
     def bit_of(axis, b):
         return (here[axis] // (1 << b)) % 2
@@ -141,7 +154,21 @@
     barrier = pltpu.get_barrier_semaphore()
     for axis, b in bits:
         pl.semaphore_signal(barrier, inc=1, device_id=partner(axis, b), device_id_type=MESH_ID)
-    pl.semaphore_wait(barrier, len(bits))
+    for dz, dy in offsets:
+        pl.semaphore_signal(barrier, inc=1, device_id=neighbour(dz, dy), device_id_type=MESH_ID)
+    pl.semaphore_wait(barrier, len(bits) + count)
+    halo = []
+    for i, (dz, dy) in enumerate(offsets):
+        copy = pltpu.make_async_remote_copy(
+            src_ref=pieces[i],
+            dst_ref=landed[i],
+            send_sem=halo_send.at[i],
+            recv_sem=halo_recv.at[i],
+            device_id=neighbour(dz, dy),
+            device_id_type=MESH_ID,
+        )
+        copy.start()
+        halo.append(copy)
 
     def exchange(step, axis, b, src, dst):
         copy = pltpu.make_async_remote_copy(
@@ -177,9 +204,13 @@
         exchange(step, axis, b, region, region)
         lo = pl.multiple_of(lo - bit_of(axis, b) * length, 8)
         length, step = length * 2, step + 1
-
-
-def allreduce(flat, halvings=HALVINGS):
+    for copy in halo:
+        copy.wait()
+
+
+def allreduce(flat, pieces=(), halvings=HALVINGS):
+    offsets = NEIGHBOURS[: len(pieces)]
+    pieces = [p.reshape(-1, 128) for p in pieces]
     bits = mesh_bits()
     halvings = min(halvings, len(bits))
     rows = flat.shape[0]
@@ -191,27 +222,34 @@
         pltpu.VMEM((max(len(bits) - halvings, 1), segment, 128), jnp.float32),
         pltpu.SemaphoreType.DMA((steps,)),
         pltpu.SemaphoreType.DMA((steps,)),
+        pltpu.SemaphoreType.DMA((max(len(pieces), 1),)),
+        pltpu.SemaphoreType.DMA((max(len(pieces), 1),)),
     ]
-    return pl.pallas_call(
-        functools.partial(allreduce_kernel, bits, halvings),
-        out_shape=jax.ShapeDtypeStruct(flat.shape, jnp.float32),
-        in_specs=[pl.BlockSpec(memory_space=pltpu.VMEM)],
-        out_specs=pl.BlockSpec(memory_space=pltpu.VMEM),
+    vmem = pl.BlockSpec(memory_space=pltpu.VMEM)
+    outs = pl.pallas_call(
+        functools.partial(allreduce_kernel, bits, halvings, offsets),
+        out_shape=[jax.ShapeDtypeStruct(flat.shape, jnp.float32)]
+        + [jax.ShapeDtypeStruct(p.shape, p.dtype) for p in pieces],
+        in_specs=[vmem] * (1 + len(pieces)),
+        out_specs=[vmem] * (1 + len(pieces)),
         scratch_shapes=scratch,
         compiler_params=pltpu.CompilerParams(collective_id=0, has_side_effects=True),
-    )(flat)
-
-
-def summed_gradients(local_conv, local_down):
+    )(flat, *pieces)
+    return outs[0], outs[1:]
+
+
+def summed_gradients(local_conv, local_down, pieces):
     sizes = (local_conv.size, local_down.size)
     flat = jnp.concatenate([local_conv.reshape(-1), local_down.reshape(-1)])
     unit = 128 * 8 << HALVINGS
     padded = -(-flat.size // unit) * unit
     flat = jnp.pad(flat, (0, padded - flat.size)).reshape(-1, 128)
-    total = allreduce(flat).reshape(-1)
+    total, got = allreduce(flat, [p.reshape(-1, 128) for p in pieces])
+    total = total.reshape(-1)
     return (
         total[: sizes[0]].reshape(local_conv.shape),
         total[sizes[0] : sizes[0] + sizes[1]].reshape(local_down.shape),
+        [g.reshape(p.shape) for g, p in zip(got, pieces)],
     )
 
 
@@ -270,8 +308,9 @@
                 preferred_element_type=jnp.float32,
             )
             spread = spread.at[:, tap_z : tap_z + plane_count, tap_y : tap_y + row_count].add(term)
-    row_fold = folded_grad(fold_along(spread, channels))
-    summed_conv, summed_down = summed_gradients(local_conv, local_down)
+    folded = fold_along(spread, channels)
+    summed_conv, summed_down, got = summed_gradients(local_conv, local_down, border_pieces(folded))
+    row_fold = folded_grad(folded, got)
     grad_conv = summed_conv * grad_scale
     grad_down = summed_down * grad_scale
     return (section_out, row_fold, grad_conv, grad_down)

time: 152 us -> 137 us (0.901)
  Pallas kernels: 92.1 us -> 79.8 us
  other arithmetic: 11.4 us -> 9.45 us
    pallas_call x2 -> x1, Pallas kernels: 39.7 us -> 24.7 us  [halo_swap(): pl.pallas_call(functools.partial(halo_kernel, NEIGHBOURS), out_shape=[jax...]
    pallas_call x1, Pallas kernels: 52.4 us -> 55.1 us  [allreduce(): pl.pallas_call(functools.partial(allreduce_kernel, bits, halvings, offset...]
    unnamed x59 -> x61, local copies, waits for them, and re-layouts: 5.83 us -> 5.83 us
where the time goes in v3:
time: 137 us; the launch traced here: 136 us
  Pallas kernels  79.8 us (58%)
  local copies, waits for them, and re-layouts  27.8 us (20%)
  matrix products  17.8 us (13%)
  other arithmetic  9.45 us (7%)
  between operations  1.37 us (1%)
    pallas_call x1, Pallas kernels, allreduce(): pl.pallas_call(functools.partial(allreduce_kernel, bits, halvings, offset...  55.1 us
    pallas_call x1, Pallas kernels, halo_swap(): pl.pallas_call(functools.partial(halo_kernel, NEIGHBOURS), out_shape=[jax...  24.7 us
    dot_general x9, matrix products, body(): jnp.einsum('oj,ozyx->jzyx', conv_weight[tap_z, tap_y], gate_grad, preferr...  8.22 us
    unnamed x61, local copies, waits for them, and re-layouts  5.83 us
    dot_general x9, matrix products, body(): jnp.einsum('oj,jzyx->ozyx', conv_weight[tap_z, tap_y], window, preferred_...  5.3 us
    reshape x4, local copies, waits for them, and re-layouts, halo_swap(): return [g.reshape(p.shape) for g, p in zip(got, pieces)]  3.38 us
    dot_general x9, matrix products, body(): jnp.einsum('ozyx,jzyx->oj', gate_grad, window, preferred_element_type=jnp...  3.34 us
    slice x1, local copies, waits for them, and re-layouts, body(): window = columns[:, tap_z:tap_z + plane_count, tap_y:tap_y + row_count]  3.06 us

profile of v3, /device:TPU:1, one launch (start us, length us, event | category | flops | bytes accessed | tf_op | source)
XLA Modules:
  0.0 136.1 jit_solution(14357503616126733339)
XLA Ops:
  0.6 1.0 copy.88
  1.7 0.6 slice_bitcast_fusion.6
  2.3 1.7 %slice_bitcast_fusion = (bf16[512,128]{1,0:T(8,128)(2,1)}, bf16[512,128]{1,0:T(8,128)(2,1)}) fusion(bf16[64,2,8,128]{3,2,1,0:T(8,128)(2,1)} %param.38), kind=kLoop, calls=%fused_computation.74 | loop fusion | bytes 524288 | tf_op jit(solution)/shard_map/reshape | solution.py:77
  4.0 1.1 fusion.95
  5.1 0.6 copy.155
  5.7 0.6 copy.156
  6.4 24.7 %shard_map.75 = (bf16[512,128]{1,0:T(8,128)(2,1)}, bf16[512,128]{1,0:T(8,128)(2,1)}, bf16[128,128]{1,0:T(8,128)(2,1)}, bf16[128,128]{1,0:T(8,128)(2,1)}, bf16[64...) custom-call(bf16[512,128]{1,0:T(8,128)(2,1)} %get-tuple-element.290.refs_0_, ...), custom_call_target="tpu_custom_call" | custom-call | tf_op jit(solution)/shard_map/pallas_call | solution.py:79
  31.1 0.9 copy.92
  32.0 0.9 copy.96
  33.0 0.8 copy.93
  33.7 0.8 copy.95
  34.5 0.9 maximum_maximum_fusion.1
  36.0 0.4 copy-done.14
  36.4 2.0 %maximum_maximum_fusion = bf16[192,4,10,128]{3,0,2,1:T(8,128)(2,1)S(1)} fusion(bf16[64,4,10,1]{3,0,2,1:T(8,128)(2,1)S(1)} %get-tuple-element.278, bf16[64,4,10,127]{3,0,2,1:T(8,128)(2,1)S(1)} %get-tuple-element.280, bf16[64,1,1,128]{3,0,2,1:T(8,128)(2,1)S(1)} %bitcast.314, bf16[64,1,8,128]{3,0,2,1:T(8,128)(2,1)S(1)} %copy.96, ...), kind=kLoop, calls=%fused_computation.1 | loop fusion | flops 25559040 | bytes 3932160 | tf_op jit(solution)/shard_map/concatenate | solution.py:33
  38.4 3.1 %fusion.90 = (bf16[192,2,8,128]{3,0,2,1:T(8,128)(2,1)}, bf16[192,2,8,128]{3,0,2,1:T(8,128)(2,1)}, bf16[192,2,8,128]{3,0,2,1:T(8,128)(2,1)}, bf16[192,2,8,128]{3,...) fusion(bf16[192,4,10,128]{3,0,2,1:T(8,128)(2,1)S(1)} %maximum_m, ...), kind=kLoop, calls=%fused_computation.162 | loop fusion | bytes 14155776 | tf_op jit(solution)/shard_map/slice | solution.py:266
  43.4 1.1 convolution_add_fusion.1
  44.7 0.3 convolution_bitcast_fusion.1
  45.0 0.8 copy.101
  45.9 1.1 copy.102
  47.0 2.4 %multiply_convert_fusion = (bf16[64,2,8,128]{3,0,2,1:T(8,128)(2,1)S(1)}, bf16[64,2,8,128]{3,0,2,1:T(8,128)(2,1)}) fusion(f32[64,2,8,128]{3,0,2,1:T(8,128)} %copy.102, f32[2,8,128,64]{2,3,1,0:T(8,128)} %convolution_add_fusion.1, bf16[192,4,10,128]{3,0,2,1:T(8,128)(2,1)S(1)} %maximum_maximum_fusion, bf16[3,3,64,192]{3,2,1,0:T(8,128)(2,1)S(1)} %copy-done), kind=kOutput, calls=%fused_computation.58 | convolution fusion | flops 51904512 | bytes 2392064 | tf_op jit(solution)/shard_map/oj,jzyx->ozyx/dot_general | solution.py:267
  49.4 0.4 convolution_bitcast_fusion.10
  49.8 0.4 convolution_bitcast_fusion.11
  50.2 0.4 copy-done.7
  50.5 0.4 convolution_bitcast_fusion.12
  50.9 0.4 convolution_bitcast_fusion.7
  51.3 0.4 convolution_bitcast_fusion.8
  51.7 0.4 convolution_bitcast_fusion.9
  52.1 0.4 copy-done.3
  52.5 0.4 convolution_bitcast_fusion.4
  52.9 0.4 convolution_bitcast_fusion.5
  53.3 0.4 convolution_bitcast_fusion.6
  54.5 0.3 convolution_bitcast_fusion.2
  55.4 0.9 fusion.21.x_ref
  56.3 0.4 convolution_bitcast_fusion
  56.7 0.4 scatter-add.56
  57.2 0.6 fusion.98
  57.8 1.8 %fusion.7 = f32[192,4,10,128]{3,0,2,1:T(8,128)S(1)} fusion(f32[192,4,10,128]{3,0,2,1:T(8,128)S(1)} %scatter-add.56, s32[]{:T(128)} %bitcast.59, s32[]{:T(128)} %bitcast.60, bf16[64,2,8,128]{3,0,2,1:T(8,128)(2,1)S(1)} %get-tuple-element.281, bf16[3,3,64,192]{3,2,1,0:T(8,128)(2,1)S(1)} %copy-done), kind=kOutput, calls=%fused_computation.16 | convolution fusion | flops 50724864 | bytes 3440648 | tf_op jit(solution)/shard_map/oj,ozyx->jzyx/dot_general | solution.py:304
  59.6 0.7 and_reduce_fusion
  60.3 0.6 fusion.97
  60.9 2.4 %fusion = f32[192,4,10,128]{3,0,2,1:T(8,128)S(1)} fusion(f32[192,4,10,128]{3,0,2,1:T(8,128)S(1)} %fusion.7, s32[]{:T(128)} %bitcast.64, s32[]{:T(128)} %bitcast.65, bf16[64,2,8,128]{3,0,2,1:T(8,128)(2,1)S(1)} %get-tuple-element.281, pred[]{:T(512)} %get-tuple-element.298, bf16[3,3,64,192]{3,2,1,0:T(8,128)(2,1)S(1)} %copy-done), kind=kOutput, calls=%fused_computation.2 | convolution fusion | flops 51118080 | bytes 3440649 | tf_op jit(solution)/shard_map/oj,ozyx->jzyx/dot_general | solution.py:304
  63.3 0.6 fusion.6
  63.9 0.6 fusion.5
  64.5 0.6 fusion.4
  65.2 0.6 fusion.3
  65.8 0.6 fusion.2
  66.4 0.6 fusion.1
  67.0 0.5 fusion.88
  67.5 0.5 fusion.89
  67.9 1.0 fusion.86
  69.0 0.7 copy.201
  69.7 0.7 copy.202
  70.5 0.6 copy.125
  71.1 0.6 copy.126
  71.8 0.6 slice_bitcast_fusion.2
  72.4 55.1 %shard_map.76 = (f32[1408,128]{1,0:T(8,128)}, bf16[512,128]{1,0:T(8,128)(2,1)}, bf16[512,128]{1,0:T(8,128)(2,1)}, bf16[128,128]{1,0:T(8,128)(2,1)}, bf16[128,128...) custom-call(f32[1408,128]{1,0:T(8,128)} %fusion.21.x_ref, ...), custom_call_target="tpu_custom_call" | custom-call | tf_op jit(solution)/shard_map/pallas_call | solution.py:229
  127.5 1.0 bitcast_convert_fusion.1
  128.9 0.6 fusion.96
  129.5 1.9 %fusion.27 = f32[64,2,8,128]{3,0,2,1:T(8,128)S(1)} fusion(f32[64,2,8,128]{3,0,2,1:T(8,128)S(1)} %fusion.30, s32[]{:T(128)} %bitcast.136, s32[]{:T(128)} %bitcast.137, bf16[64,128]{1,0:T(8,128)(2,1)S(1)} %copy-done.24, pred[]{:T(512)} %get-tuple-element.297), kind=kLoop, calls=%fused_computation.81 | loop fusion | flops 24576 | bytes 81929 | tf_op jit(solution)/shard_map/scatter-add | solution.py:125
  131.4 1.1 copy.132
  132.6 1.0 mul.37
  133.6 0.7 slice_multiply_fusion.1
  134.3 0.5 copy.98
  134.8 0.3 dot_general.118
  135.4 0.7 copy.131
  (87 shorter events, 4.9 us)
Async XLA Ops:
  35.7 0.7 copy-start.14
  35.7 0.7 copy-start.15
  35.7 0.7 copy-start.16
  35.7 0.7 copy-start.17
  38.4 3.1 %copy-start = (bf16[3,3,64,192]{3,2,1,0:T(8,128)(2,1)S(1)}, bf16[3,3,64,192]{3,2,1,0:T(8,128)(2,1)}, u32[]{:S(2)}) copy-start(bf16[3,3,64,192]{3,2,1,0:T(8,128)(2,1)} %param.39) | copy-start | bytes 663556
  43.1 1.3 copy-start.13
  43.1 1.5 %copy-start.18 = (bf16[128,1,256]{2,0,1:T(8,128)(2,1)S(1)}, bf16[128,1,256]{2,0,1:T(8,128)(2,1)}, u32[]{:S(2)}) copy-start(bf16[128,1,256]{2,0,1:T(8,128)(2,1)} %param.41) | copy-start | bytes 196612
  47.0 2.4 %copy-start.9 = (bf16[192,2,8,128]{3,0,2,1:T(8,128)(2,1)S(1)}, bf16[192,2,8,128]{3,0,2,1:T(8,128)(2,1)}, u32[]{:S(2)}) copy-start(bf16[192,2,8,128]{3,0,2,1:T(8,128)(2,1)} %get-tuple-element.267) | copy-start | bytes 2359300
  47.0 2.8 %copy-start.8 = (bf16[192,2,8,128]{3,0,2,1:T(8,128)(2,1)S(1)}, bf16[192,2,8,128]{3,0,2,1:T(8,128)(2,1)}, u32[]{:S(2)}) copy-start(bf16[192,2,8,128]{3,0,2,1:T(8,128)(2,1)} %get-tuple-element.268) | copy-start | bytes 2359300
  49.4 1.1 copy-start.7
  49.4 1.5 %copy-start.6 = (bf16[192,2,8,128]{3,0,2,1:T(8,128)(2,1)S(1)}, bf16[192,2,8,128]{3,0,2,1:T(8,128)(2,1)}, u32[]{:S(2)}) copy-start(bf16[192,2,8,128]{3,0,2,1:T(8,128)(2,1)} %get-tuple-element.264) | copy-start | bytes 2359300
  49.8 1.5 %copy-start.5 = (bf16[192,2,8,128]{3,0,2,1:T(8,128)(2,1)S(1)}, bf16[192,2,8,128]{3,0,2,1:T(8,128)(2,1)}, u32[]{:S(2)}) copy-start(bf16[192,2,8,128]{3,0,2,1:T(8,128)(2,1)} %get-tuple-element.265) | copy-start | bytes 2359300
  50.2 1.5 %copy-start.4 = (bf16[192,2,8,128]{3,0,2,1:T(8,128)(2,1)S(1)}, bf16[192,2,8,128]{3,0,2,1:T(8,128)(2,1)}, u32[]{:S(2)}) copy-start(bf16[192,2,8,128]{3,0,2,1:T(8,128)(2,1)} %get-tuple-element.266) | copy-start | bytes 2359300
  51.3 1.2 copy-start.3
  51.7 1.2 copy-start.2
  52.1 1.3 copy-start.1
  53.3 1.0 copy-start.11
  57.1 2.4 %copy-start.25 = (s32[4]{0:T(128)S(1)}, s32[4]{0:T(128)}, u32[]{:S(2)}) copy-start(s32[4]{0:T(128)} %constant.480.clone.1) | copy-start | bytes 52
  57.2 2.4 %copy-start.26 = (s32[4]{0:T(128)S(1)}, s32[4]{0:T(128)}, u32[]{:S(2)}) copy-start(s32[4]{0:T(128)} %constant.484.clone.1) | copy-start | bytes 52
  127.4 1.2 copy-start.12
  127.5 1.3 copy-start.20
  127.5 1.4 %copy-start.19 = (bf16[128,128]{1,0:T(8,128)(2,1)S(1)}, bf16[128,128]{1,0:T(8,128)(2,1)}, u32[]{:S(2)}) copy-start(bf16[128,128]{1,0:T(8,128)(2,1)} %get-tuple-element.236) | copy-start | bytes 98308
  127.5 1.4 %copy-start.23 = (bf16[64,128]{1,0:T(8,128)(2,1)S(1)}, bf16[64,128]{1,0:T(8,128)(2,1)}, u32[]{:S(2)}) copy-start(bf16[64,128]{1,0:T(8,128)(2,1)} %get-tuple-element.237) | copy-start | bytes 49156
  127.5 2.0 %copy-start.24 = (bf16[64,128]{1,0:T(8,128)(2,1)S(1)}, bf16[64,128]{1,0:T(8,128)(2,1)}, u32[]{:S(2)}) copy-start(bf16[64,128]{1,0:T(8,128)(2,1)} %get-tuple-element.238) | copy-start | bytes 49156
  128.5 2.9 %copy-start.22 = (bf16[64,128]{1,0:T(8,128)(2,1)S(1)}, bf16[64,128]{1,0:T(8,128)(2,1)}, u32[]{:S(2)}) copy-start(bf16[64,128]{1,0:T(8,128)(2,1)} %get-tuple-element.239) | copy-start | bytes 49156
  128.5 2.9 %copy-start.21 = (bf16[64,128]{1,0:T(8,128)(2,1)S(1)}, bf16[64,128]{1,0:T(8,128)(2,1)}, u32[]{:S(2)}) copy-start(bf16[64,128]{1,0:T(8,128)(2,1)} %get-tuple-element.240) | copy-start | bytes 49156
  128.6 4.0 %copy-start.10 = (f32[1408,128]{1,0:T(8,128)S(1)}, f32[1408,128]{1,0:T(8,128)}, u32[]{:S(2)}) copy-start(f32[1408,128]{1,0:T(8,128)} %get-tuple-element.241) | copy-start | bytes 2162692

commit v4 on v3

--- a/solution.py
+++ b/solution.py
@@ -9,7 +9,17 @@
 from jax.sharding import PartitionSpec as P
 
 MESH_ID = pl.DeviceIdType.MESH
-BIT_ORDER = (("gy", 0), ("gy", 1), ("gz", 0), ("gz", 3), ("gy", 2), ("gz", 1), ("gz", 4), ("gz", 2), ("gy", 3))
+BIT_ORDER = (
+    (("gy", 0), ("gy", 0)),
+    (("gy", 1), ("gz", 0)),
+    (("gz", 0), ("gz", 3)),
+    (("gz", 3), ("gy", 1)),
+    (("gy", 2), ("gz", 1)),
+    (("gz", 1), ("gy", 2)),
+    (("gz", 4), ("gz", 2)),
+    (("gz", 2), ("gz", 4)),
+    (("gy", 3), ("gy", 3)),
+)
 HALVINGS = 4
 
 
@@ -128,7 +138,8 @@
 
 def mesh_bits():
     sizes = {"gz": lax.axis_size("gz"), "gy": lax.axis_size("gy")}
-    return [(axis, b) for axis, b in BIT_ORDER if (1 << b) < sizes[axis]]
+    orders = [[pair[c] for pair in BIT_ORDER if (1 << pair[c][1]) < sizes[pair[c][0]]] for c in (0, 1)]
+    return list(zip(*orders))
 
 
 def allreduce_kernel(bits, halvings, offsets, x_ref, *refs):
@@ -144,16 +155,26 @@
     def neighbour(dz, dy):
         return ((here["gz"] + dz + sizes["gz"]) % sizes["gz"], (here["gy"] + dy + sizes["gy"]) % sizes["gy"])
 
-    def bit_of(axis, b):
-        return (here[axis] // (1 << b)) % 2
-
-    def partner(axis, b):
-        flip = here[axis] + (1 - 2 * bit_of(axis, b)) * (1 << b)
-        return (flip, here["gy"]) if axis == "gz" else (here["gz"], flip)
+    core = here["gy"] % 2
+
+    def pick(pair):
+        (axis0, b0), (axis1, b1) = pair
+        a0, a1 = int(axis0 == "gy"), int(axis1 == "gy")
+        return a0 + (a1 - a0) * core, (1 << b0) + ((1 << b1) - (1 << b0)) * core
+
+    def bit_of(pair):
+        which, weight = pick(pair)
+        value = here["gz"] + (here["gy"] - here["gz"]) * which
+        return (value // weight) % 2
+
+    def partner(pair):
+        which, weight = pick(pair)
+        step = (1 - 2 * bit_of(pair)) * weight
+        return (here["gz"] + step * (1 - which), here["gy"] + step * which)
 
     barrier = pltpu.get_barrier_semaphore()
-    for axis, b in bits:
-        pl.semaphore_signal(barrier, inc=1, device_id=partner(axis, b), device_id_type=MESH_ID)
+    for pair in bits:
+        pl.semaphore_signal(barrier, inc=1, device_id=partner(pair), device_id_type=MESH_ID)
     for dz, dy in offsets:
         pl.semaphore_signal(barrier, inc=1, device_id=neighbour(dz, dy), device_id_type=MESH_ID)
     pl.semaphore_wait(barrier, len(bits) + count)
@@ -170,13 +191,13 @@
         copy.start()
         halo.append(copy)
 
-    def exchange(step, axis, b, src, dst):
+    def exchange(step, pair, src, dst):
         copy = pltpu.make_async_remote_copy(
             src_ref=src,
             dst_ref=dst,
             send_sem=send_sems.at[step],
             recv_sem=recv_sems.at[step],
-            device_id=partner(axis, b),
+            device_id=partner(pair),
             device_id_type=MESH_ID,
         )
         copy.start()
@@ -184,25 +205,25 @@
 
     lo, length, step = 0, o_ref.shape[0], 0
     for k in range(halvings):
-        axis, b = bits[k]
+        pair = bits[k]
         half = length // 2
-        bit = bit_of(axis, b)
+        bit = bit_of(pair)
         keep = pl.multiple_of(lo + bit * half, 8)
         give = pl.multiple_of(lo + (1 - bit) * half, 8)
         source = x_ref if k == 0 else work
-        exchange(step, axis, b, source.at[pl.ds(give, half)], halve_bufs[k])
+        exchange(step, pair, source.at[pl.ds(give, half)], halve_bufs[k])
         work[pl.ds(keep, half)] = source[pl.ds(keep, half)] + halve_bufs[k][...]
         lo, length, step = keep, half, step + 1
-    for j, (axis, b) in enumerate(bits[halvings:]):
-        exchange(step, axis, b, work.at[pl.ds(lo, length)], double_buf.at[j])
+    for j, pair in enumerate(bits[halvings:]):
+        exchange(step, pair, work.at[pl.ds(lo, length)], double_buf.at[j])
         work[pl.ds(lo, length)] = work[pl.ds(lo, length)] + double_buf[j]
         step += 1
     o_ref[pl.ds(lo, length)] = work[pl.ds(lo, length)]
     for k in reversed(range(halvings)):
-        axis, b = bits[k]
+        pair = bits[k]
         region = o_ref.at[pl.ds(lo, length)]
-        exchange(step, axis, b, region, region)
-        lo = pl.multiple_of(lo - bit_of(axis, b) * length, 8)
+        exchange(step, pair, region, region)
+        lo = pl.multiple_of(lo - bit_of(pair) * length, 8)
         length, step = length * 2, step + 1
     for copy in halo:
         copy.wait()

time: 137 us -> 136 us (level)
  Pallas kernels: 79.8 us -> 78.4 us
    pallas_call x1, Pallas kernels: 55.1 us -> 53.6 us  [allreduce(): pl.pallas_call(functools.partial(allreduce_kernel, bits, halvings, offset...]
where the time goes in v4:
time: 136 us; the launch traced here: 135 us
  Pallas kernels  78.4 us (58%)
  local copies, waits for them, and re-layouts  27.8 us (20%)
  matrix products  17.8 us (13%)
  other arithmetic  9.45 us (7%)
  between operations  1.37 us (1%)
    pallas_call x1, Pallas kernels, allreduce(): pl.pallas_call(functools.partial(allreduce_kernel, bits, halvings, offset...  53.6 us
    pallas_call x1, Pallas kernels, halo_swap(): pl.pallas_call(functools.partial(halo_kernel, NEIGHBOURS), out_shape=[jax...  24.7 us
    dot_general x9, matrix products, body(): jnp.einsum('oj,ozyx->jzyx', conv_weight[tap_z, tap_y], gate_grad, preferr...  8.22 us
    unnamed x61, local copies, waits for them, and re-layouts  5.83 us
    dot_general x9, matrix products, body(): jnp.einsum('oj,jzyx->ozyx', conv_weight[tap_z, tap_y], window, preferred_...  5.3 us
    reshape x4, local copies, waits for them, and re-layouts, halo_swap(): return [g.reshape(p.shape) for g, p in zip(got, pieces)]  3.38 us
    dot_general x9, matrix products, body(): jnp.einsum('ozyx,jzyx->oj', gate_grad, window, preferred_element_type=jnp...  3.34 us
    slice x1, local copies, waits for them, and re-layouts, body(): window = columns[:, tap_z:tap_z + plane_count, tap_y:tap_y + row_count]  3.06 us

profile of v4, /device:TPU:1, one launch (start us, length us, event | category | flops | bytes accessed | tf_op | source)
XLA Modules:
  0.0 134.7 jit_solution(10984764231189419925)
XLA Ops:
  0.6 1.0 copy.88
  1.7 0.6 slice_bitcast_fusion.6
  2.3 1.7 %slice_bitcast_fusion = (bf16[512,128]{1,0:T(8,128)(2,1)}, bf16[512,128]{1,0:T(8,128)(2,1)}) fusion(bf16[64,2,8,128]{3,2,1,0:T(8,128)(2,1)} %param.38), kind=kLoop, calls=%fused_computation.74 | loop fusion | bytes 524288 | tf_op jit(solution)/shard_map/reshape | solution.py:87
  4.0 1.1 fusion.95
  5.1 0.6 copy.155
  5.7 0.6 copy.156
  6.4 24.7 %shard_map.75 = (bf16[512,128]{1,0:T(8,128)(2,1)}, bf16[512,128]{1,0:T(8,128)(2,1)}, bf16[128,128]{1,0:T(8,128)(2,1)}, bf16[128,128]{1,0:T(8,128)(2,1)}, bf16[64...) custom-call(bf16[512,128]{1,0:T(8,128)(2,1)} %get-tuple-element.290.refs_0_, ...), custom_call_target="tpu_custom_call" | custom-call | tf_op jit(solution)/shard_map/pallas_call | solution.py:89
  31.1 0.9 copy.92
  32.0 0.9 copy.96
  33.0 0.8 copy.93
  33.7 0.8 copy.95
  34.5 0.9 maximum_maximum_fusion.1
  36.0 0.4 copy-done.14
  36.4 2.0 %maximum_maximum_fusion = bf16[192,4,10,128]{3,0,2,1:T(8,128)(2,1)S(1)} fusion(bf16[64,4,10,1]{3,0,2,1:T(8,128)(2,1)S(1)} %get-tuple-element.278, bf16[64,4,10,127]{3,0,2,1:T(8,128)(2,1)S(1)} %get-tuple-element.280, bf16[64,1,1,128]{3,0,2,1:T(8,128)(2,1)S(1)} %bitcast.314, bf16[64,1,8,128]{3,0,2,1:T(8,128)(2,1)S(1)} %copy.96, ...), kind=kLoop, calls=%fused_computation.1 | loop fusion | flops 25559040 | bytes 3932160 | tf_op jit(solution)/shard_map/concatenate | solution.py:43
  38.4 3.1 %fusion.90 = (bf16[192,2,8,128]{3,0,2,1:T(8,128)(2,1)}, bf16[192,2,8,128]{3,0,2,1:T(8,128)(2,1)}, bf16[192,2,8,128]{3,0,2,1:T(8,128)(2,1)}, bf16[192,2,8,128]{3,...) fusion(bf16[192,4,10,128]{3,0,2,1:T(8,128)(2,1)S(1)} %maximum_m, ...), kind=kLoop, calls=%fused_computation.162 | loop fusion | bytes 14155776 | tf_op jit(solution)/shard_map/slice | solution.py:287
  43.4 1.1 convolution_add_fusion.1
  44.7 0.3 convolution_bitcast_fusion.1
  45.0 0.8 copy.101
  45.9 1.1 copy.102
  47.0 2.4 %multiply_convert_fusion = (bf16[64,2,8,128]{3,0,2,1:T(8,128)(2,1)S(1)}, bf16[64,2,8,128]{3,0,2,1:T(8,128)(2,1)}) fusion(f32[64,2,8,128]{3,0,2,1:T(8,128)} %copy.102, f32[2,8,128,64]{2,3,1,0:T(8,128)} %convolution_add_fusion.1, bf16[192,4,10,128]{3,0,2,1:T(8,128)(2,1)S(1)} %maximum_maximum_fusion, bf16[3,3,64,192]{3,2,1,0:T(8,128)(2,1)S(1)} %copy-done), kind=kOutput, calls=%fused_computation.58 | convolution fusion | flops 51904512 | bytes 2392064 | tf_op jit(solution)/shard_map/oj,jzyx->ozyx/dot_general | solution.py:288
  49.4 0.4 convolution_bitcast_fusion.10
  49.8 0.4 convolution_bitcast_fusion.11
  50.2 0.4 copy-done.7
  50.5 0.4 convolution_bitcast_fusion.12
  50.9 0.4 convolution_bitcast_fusion.7
  51.3 0.4 convolution_bitcast_fusion.8
  51.7 0.4 convolution_bitcast_fusion.9
  52.1 0.4 copy-done.3
  52.5 0.4 convolution_bitcast_fusion.4
  52.9 0.4 convolution_bitcast_fusion.5
  53.3 0.4 convolution_bitcast_fusion.6
  54.5 0.3 convolution_bitcast_fusion.2
  55.4 0.9 fusion.21.x_ref
  56.3 0.4 convolution_bitcast_fusion
  56.7 0.4 scatter-add.56
  57.2 0.6 fusion.98
  57.8 1.8 %fusion.7 = f32[192,4,10,128]{3,0,2,1:T(8,128)S(1)} fusion(f32[192,4,10,128]{3,0,2,1:T(8,128)S(1)} %scatter-add.56, s32[]{:T(128)} %bitcast.59, s32[]{:T(128)} %bitcast.60, bf16[64,2,8,128]{3,0,2,1:T(8,128)(2,1)S(1)} %get-tuple-element.281, bf16[3,3,64,192]{3,2,1,0:T(8,128)(2,1)S(1)} %copy-done), kind=kOutput, calls=%fused_computation.16 | convolution fusion | flops 50724864 | bytes 3440648 | tf_op jit(solution)/shard_map/oj,ozyx->jzyx/dot_general | solution.py:325
  59.6 0.7 and_reduce_fusion
  60.3 0.6 fusion.97
  60.9 2.4 %fusion = f32[192,4,10,128]{3,0,2,1:T(8,128)S(1)} fusion(f32[192,4,10,128]{3,0,2,1:T(8,128)S(1)} %fusion.7, s32[]{:T(128)} %bitcast.64, s32[]{:T(128)} %bitcast.65, bf16[64,2,8,128]{3,0,2,1:T(8,128)(2,1)S(1)} %get-tuple-element.281, pred[]{:T(512)} %get-tuple-element.298, bf16[3,3,64,192]{3,2,1,0:T(8,128)(2,1)S(1)} %copy-done), kind=kOutput, calls=%fused_computation.2 | convolution fusion | flops 51118080 | bytes 3440649 | tf_op jit(solution)/shard_map/oj,ozyx->jzyx/dot_general | solution.py:325
  63.3 0.6 fusion.6
  63.9 0.6 fusion.5
  64.5 0.6 fusion.4
  65.2 0.6 fusion.3
  65.8 0.6 fusion.2
  66.4 0.6 fusion.1
  67.0 0.5 fusion.88
  67.5 0.5 fusion.89
  67.9 1.0 fusion.86
  69.0 0.7 copy.201
  69.7 0.7 copy.202
  70.5 0.6 copy.125
  71.1 0.6 copy.126
  71.8 0.6 slice_bitcast_fusion.2
  72.4 53.6 %shard_map.76 = (f32[1408,128]{1,0:T(8,128)}, bf16[512,128]{1,0:T(8,128)(2,1)}, bf16[512,128]{1,0:T(8,128)(2,1)}, bf16[128,128]{1,0:T(8,128)(2,1)}, bf16[128,128...) custom-call(f32[1408,128]{1,0:T(8,128)} %fusion.21.x_ref, ...), custom_call_target="tpu_custom_call" | custom-call | tf_op jit(solution)/shard_map/pallas_call | solution.py:250
  126.1 1.0 bitcast_convert_fusion.1
  127.5 0.6 fusion.96
  128.1 1.9 %fusion.27 = f32[64,2,8,128]{3,0,2,1:T(8,128)S(1)} fusion(f32[64,2,8,128]{3,0,2,1:T(8,128)S(1)} %fusion.30, s32[]{:T(128)} %bitcast.136, s32[]{:T(128)} %bitcast.137, bf16[64,128]{1,0:T(8,128)(2,1)S(1)} %copy-done.24, pred[]{:T(512)} %get-tuple-element.297), kind=kLoop, calls=%fused_computation.81 | loop fusion | flops 24576 | bytes 81929 | tf_op jit(solution)/shard_map/scatter-add | solution.py:135
  130.0 1.1 copy.132
  131.2 1.0 mul.37
  132.1 0.7 slice_multiply_fusion.1
  132.9 0.5 copy.98
  133.4 0.3 dot_general.118
  134.0 0.7 copy.131
  (87 shorter events, 4.9 us)
Async XLA Ops:
  35.7 0.7 copy-start.14
  35.7 0.7 copy-start.15
  35.7 0.7 copy-start.16
  35.7 0.7 copy-start.17
  38.4 3.1 %copy-start = (bf16[3,3,64,192]{3,2,1,0:T(8,128)(2,1)S(1)}, bf16[3,3,64,192]{3,2,1,0:T(8,128)(2,1)}, u32[]{:S(2)}) copy-start(bf16[3,3,64,192]{3,2,1,0:T(8,128)(2,1)} %param.39) | copy-start | bytes 663556
  43.1 1.3 %copy-start.13 = (bf16[2,2,128,128]{3,2,1,0:T(8,128)(2,1)S(1)}, bf16[2,2,128,128]{3,2,1,0:T(8,128)(2,1)}, u32[]{:S(2)}) copy-start(bf16[2,2,128,128]{3,2,1,0:T(8,128)(2,1)} %param.40) | copy-start | bytes 393220
  43.1 1.5 %copy-start.18 = (bf16[128,1,256]{2,0,1:T(8,128)(2,1)S(1)}, bf16[128,1,256]{2,0,1:T(8,128)(2,1)}, u32[]{:S(2)}) copy-start(bf16[128,1,256]{2,0,1:T(8,128)(2,1)} %param.41) | copy-start | bytes 196612
  47.0 2.4 %copy-start.9 = (bf16[192,2,8,128]{3,0,2,1:T(8,128)(2,1)S(1)}, bf16[192,2,8,128]{3,0,2,1:T(8,128)(2,1)}, u32[]{:S(2)}) copy-start(bf16[192,2,8,128]{3,0,2,1:T(8,128)(2,1)} %get-tuple-element.267) | copy-start | bytes 2359300
  47.0 2.8 %copy-start.8 = (bf16[192,2,8,128]{3,0,2,1:T(8,128)(2,1)S(1)}, bf16[192,2,8,128]{3,0,2,1:T(8,128)(2,1)}, u32[]{:S(2)}) copy-start(bf16[192,2,8,128]{3,0,2,1:T(8,128)(2,1)} %get-tuple-element.268) | copy-start | bytes 2359300
  49.4 1.1 copy-start.7
  49.4 1.5 %copy-start.6 = (bf16[192,2,8,128]{3,0,2,1:T(8,128)(2,1)S(1)}, bf16[192,2,8,128]{3,0,2,1:T(8,128)(2,1)}, u32[]{:S(2)}) copy-start(bf16[192,2,8,128]{3,0,2,1:T(8,128)(2,1)} %get-tuple-element.264) | copy-start | bytes 2359300
  49.8 1.5 %copy-start.5 = (bf16[192,2,8,128]{3,0,2,1:T(8,128)(2,1)S(1)}, bf16[192,2,8,128]{3,0,2,1:T(8,128)(2,1)}, u32[]{:S(2)}) copy-start(bf16[192,2,8,128]{3,0,2,1:T(8,128)(2,1)} %get-tuple-element.265) | copy-start | bytes 2359300
  50.2 1.5 %copy-start.4 = (bf16[192,2,8,128]{3,0,2,1:T(8,128)(2,1)S(1)}, bf16[192,2,8,128]{3,0,2,1:T(8,128)(2,1)}, u32[]{:S(2)}) copy-start(bf16[192,2,8,128]{3,0,2,1:T(8,128)(2,1)} %get-tuple-element.266) | copy-start | bytes 2359300
  51.3 1.2 copy-start.3
  51.7 1.2 copy-start.2
  52.1 1.3 copy-start.1
  53.3 1.0 copy-start.11
  57.1 2.4 %copy-start.25 = (s32[4]{0:T(128)S(1)}, s32[4]{0:T(128)}, u32[]{:S(2)}) copy-start(s32[4]{0:T(128)} %constant.480.clone.1) | copy-start | bytes 52
  57.2 2.4 %copy-start.26 = (s32[4]{0:T(128)S(1)}, s32[4]{0:T(128)}, u32[]{:S(2)}) copy-start(s32[4]{0:T(128)} %constant.484.clone.1) | copy-start | bytes 52
  126.0 1.2 copy-start.12
  126.0 1.3 copy-start.20
  126.1 1.4 %copy-start.19 = (bf16[128,128]{1,0:T(8,128)(2,1)S(1)}, bf16[128,128]{1,0:T(8,128)(2,1)}, u32[]{:S(2)}) copy-start(bf16[128,128]{1,0:T(8,128)(2,1)} %get-tuple-element.236) | copy-start | bytes 98308
  126.1 1.4 %copy-start.23 = (bf16[64,128]{1,0:T(8,128)(2,1)S(1)}, bf16[64,128]{1,0:T(8,128)(2,1)}, u32[]{:S(2)}) copy-start(bf16[64,128]{1,0:T(8,128)(2,1)} %get-tuple-element.237) | copy-start | bytes 49156
  126.1 2.0 %copy-start.24 = (bf16[64,128]{1,0:T(8,128)(2,1)S(1)}, bf16[64,128]{1,0:T(8,128)(2,1)}, u32[]{:S(2)}) copy-start(bf16[64,128]{1,0:T(8,128)(2,1)} %get-tuple-element.238) | copy-start | bytes 49156
  127.1 2.9 %copy-start.22 = (bf16[64,128]{1,0:T(8,128)(2,1)S(1)}, bf16[64,128]{1,0:T(8,128)(2,1)}, u32[]{:S(2)}) copy-start(bf16[64,128]{1,0:T(8,128)(2,1)} %get-tuple-element.239) | copy-start | bytes 49156
  127.1 2.9 %copy-start.21 = (bf16[64,128]{1,0:T(8,128)(2,1)S(1)}, bf16[64,128]{1,0:T(8,128)(2,1)}, u32[]{:S(2)}) copy-start(bf16[64,128]{1,0:T(8,128)(2,1)} %get-tuple-element.240) | copy-start | bytes 49156
  127.2 4.0 %copy-start.10 = (f32[1408,128]{1,0:T(8,128)S(1)}, f32[1408,128]{1,0:T(8,128)}, u32[]{:S(2)}) copy-start(f32[1408,128]{1,0:T(8,128)} %get-tuple-element.241) | copy-start | bytes 2162692

commit v5 on v4

--- a/solution.py
+++ b/solution.py
@@ -167,17 +167,23 @@
         value = here["gz"] + (here["gy"] - here["gz"]) * which
         return (value // weight) % 2
 
-    def partner(pair):
-        which, weight = pick(pair)
-        step = (1 - 2 * bit_of(pair)) * weight
-        return (here["gz"] + step * (1 - which), here["gy"] + step * which)
+    def partner(*pairs):
+        device = [here["gz"], here["gy"]]
+        for pair in pairs:
+            which, weight = pick(pair)
+            step = (1 - 2 * bit_of(pair)) * weight
+            device = [device[0] + step * (1 - which), device[1] + step * which]
+        return tuple(device)
+
+    groups = [bits[i : i + 2] for i in range(halvings, len(bits), 2)]
+    reach = [(pair,) for pair in bits] + [tuple(g) for g in groups if len(g) == 2]
 
     barrier = pltpu.get_barrier_semaphore()
-    for pair in bits:
-        pl.semaphore_signal(barrier, inc=1, device_id=partner(pair), device_id_type=MESH_ID)
+    for pairs in reach:
+        pl.semaphore_signal(barrier, inc=1, device_id=partner(*pairs), device_id_type=MESH_ID)
     for dz, dy in offsets:
         pl.semaphore_signal(barrier, inc=1, device_id=neighbour(dz, dy), device_id_type=MESH_ID)
-    pl.semaphore_wait(barrier, len(bits) + count)
+    pl.semaphore_wait(barrier, len(reach) + count)
     halo = []
     for i, (dz, dy) in enumerate(offsets):
         copy = pltpu.make_async_remote_copy(
@@ -192,16 +198,19 @@
         halo.append(copy)
 
     def exchange(step, pair, src, dst):
+        start_copy(step, (pair,), src, dst).wait()
+
+    def start_copy(step, pairs, src, dst):
         copy = pltpu.make_async_remote_copy(
             src_ref=src,
             dst_ref=dst,
             send_sem=send_sems.at[step],
             recv_sem=recv_sems.at[step],
-            device_id=partner(pair),
+            device_id=partner(*pairs),
             device_id_type=MESH_ID,
         )
         copy.start()
-        copy.wait()
+        return copy
 
     lo, length, step = 0, o_ref.shape[0], 0
     for k in range(halvings):
@@ -214,10 +223,21 @@
         exchange(step, pair, source.at[pl.ds(give, half)], halve_bufs[k])
         work[pl.ds(keep, half)] = source[pl.ds(keep, half)] + halve_bufs[k][...]
         lo, length, step = keep, half, step + 1
-    for j, pair in enumerate(bits[halvings:]):
-        exchange(step, pair, work.at[pl.ds(lo, length)], double_buf.at[j])
-        work[pl.ds(lo, length)] = work[pl.ds(lo, length)] + double_buf[j]
-        step += 1
+    slot = 0
+    for group in groups:
+        own = work.at[pl.ds(lo, length)]
+        if len(group) == 1:
+            exchange(step, group[0], own, double_buf.at[slot])
+            work[pl.ds(lo, length)] = own[...] + double_buf[slot]
+            slot, step = slot + 1, step + 1
+            continue
+        flips = [(group[0],), (group[1],), (group[0], group[1])]
+        copies = [start_copy(step + m, f, own, double_buf.at[slot + m]) for m, f in enumerate(flips)]
+        for copy in copies:
+            copy.wait()
+        near, far = double_buf[slot] + own[...], double_buf[slot + 1] + double_buf[slot + 2]
+        work[pl.ds(lo, length)] = near + far
+        slot, step = slot + 3, step + 3
     o_ref[pl.ds(lo, length)] = work[pl.ds(lo, length)]
     for k in reversed(range(halvings)):
         pair = bits[k]
@@ -236,11 +256,13 @@
     halvings = min(halvings, len(bits))
     rows = flat.shape[0]
     segment = rows >> halvings
-    steps = len(bits) + halvings
+    far = len(bits) - halvings
+    slots = 3 * (far // 2) + far % 2
+    steps = 2 * halvings + slots
     scratch = [pltpu.VMEM((rows >> (k + 1), 128), jnp.float32) for k in range(halvings)]
     scratch += [
         pltpu.VMEM(flat.shape, jnp.float32),
-        pltpu.VMEM((max(len(bits) - halvings, 1), segment, 128), jnp.float32),
+        pltpu.VMEM((max(slots, 1), segment, 128), jnp.float32),
         pltpu.SemaphoreType.DMA((steps,)),
         pltpu.SemaphoreType.DMA((steps,)),
         pltpu.SemaphoreType.DMA((max(len(pieces), 1),)),

time: 136 us -> 133 us (0.978)
  Pallas kernels: 78.4 us -> 74.9 us
    pallas_call x1, Pallas kernels: 53.6 us -> 50.2 us  [allreduce(): pl.pallas_call(functools.partial(allreduce_kernel, bits, halvings, offset...]
where the time goes in v5:
time: 133 us; the launch traced here: 131 us
  Pallas kernels  74.9 us (56%)
  local copies, waits for them, and re-layouts  27.8 us (21%)
  matrix products  17.8 us (13%)
  other arithmetic  9.45 us (7%)
  between operations  1.37 us (1%)
    pallas_call x1, Pallas kernels, allreduce(): pl.pallas_call(functools.partial(allreduce_kernel, bits, halvings, offset...  50.2 us
    pallas_call x1, Pallas kernels, halo_swap(): pl.pallas_call(functools.partial(halo_kernel, NEIGHBOURS), out_shape=[jax...  24.7 us
    dot_general x9, matrix products, body(): jnp.einsum('oj,ozyx->jzyx', conv_weight[tap_z, tap_y], gate_grad, preferr...  8.22 us
    unnamed x61, local copies, waits for them, and re-layouts  5.83 us
    dot_general x9, matrix products, body(): jnp.einsum('oj,jzyx->ozyx', conv_weight[tap_z, tap_y], window, preferred_...  5.3 us
    reshape x4, local copies, waits for them, and re-layouts, halo_swap(): return [g.reshape(p.shape) for g, p in zip(got, pieces)]  3.38 us
    dot_general x9, matrix products, body(): jnp.einsum('ozyx,jzyx->oj', gate_grad, window, preferred_element_type=jnp...  3.34 us
    slice x1, local copies, waits for them, and re-layouts, body(): window = columns[:, tap_z:tap_z + plane_count, tap_y:tap_y + row_count]  3.06 us

profile of v5, /device:TPU:1, one launch (start us, length us, event | category | flops | bytes accessed | tf_op | source)
XLA Modules:
  0.0 131.3 jit_solution(13904005878573272927)
XLA Ops:
  0.6 1.0 copy.88
  1.7 0.6 slice_bitcast_fusion.6
  2.3 1.7 %slice_bitcast_fusion = (bf16[512,128]{1,0:T(8,128)(2,1)}, bf16[512,128]{1,0:T(8,128)(2,1)}) fusion(bf16[64,2,8,128]{3,2,1,0:T(8,128)(2,1)} %param.38), kind=kLoop, calls=%fused_computation.74 | loop fusion | bytes 524288 | tf_op jit(solution)/shard_map/reshape | solution.py:87
  4.0 1.1 fusion.95
  5.1 0.6 copy.155
  5.7 0.6 copy.156
  6.4 24.7 %shard_map.75 = (bf16[512,128]{1,0:T(8,128)(2,1)}, bf16[512,128]{1,0:T(8,128)(2,1)}, bf16[128,128]{1,0:T(8,128)(2,1)}, bf16[128,128]{1,0:T(8,128)(2,1)}, bf16[64...) custom-call(bf16[512,128]{1,0:T(8,128)(2,1)} %get-tuple-element.290.refs_0_, ...), custom_call_target="tpu_custom_call" | custom-call | tf_op jit(solution)/shard_map/pallas_call | solution.py:89
  31.1 0.9 copy.92
  32.0 0.9 copy.96
  33.0 0.8 copy.93
  33.7 0.8 copy.95
  34.5 0.9 maximum_maximum_fusion.1
  36.0 0.4 copy-done.14
  36.4 2.0 %maximum_maximum_fusion = bf16[192,4,10,128]{3,0,2,1:T(8,128)(2,1)S(1)} fusion(bf16[64,4,10,1]{3,0,2,1:T(8,128)(2,1)S(1)} %get-tuple-element.278, bf16[64,4,10,127]{3,0,2,1:T(8,128)(2,1)S(1)} %get-tuple-element.280, bf16[64,1,1,128]{3,0,2,1:T(8,128)(2,1)S(1)} %bitcast.314, bf16[64,1,8,128]{3,0,2,1:T(8,128)(2,1)S(1)} %copy.96, ...), kind=kLoop, calls=%fused_computation.1 | loop fusion | flops 25559040 | bytes 3932160 | tf_op jit(solution)/shard_map/concatenate | solution.py:43
  38.4 3.1 %fusion.90 = (bf16[192,2,8,128]{3,0,2,1:T(8,128)(2,1)}, bf16[192,2,8,128]{3,0,2,1:T(8,128)(2,1)}, bf16[192,2,8,128]{3,0,2,1:T(8,128)(2,1)}, bf16[192,2,8,128]{3,...) fusion(bf16[192,4,10,128]{3,0,2,1:T(8,128)(2,1)S(1)} %maximum_m, ...), kind=kLoop, calls=%fused_computation.162 | loop fusion | bytes 14155776 | tf_op jit(solution)/shard_map/slice | solution.py:309
  43.4 1.1 convolution_add_fusion.1
  44.7 0.3 convolution_bitcast_fusion.1
  45.0 0.8 copy.101
  45.9 1.1 copy.102
  47.0 2.4 %multiply_convert_fusion = (bf16[64,2,8,128]{3,0,2,1:T(8,128)(2,1)S(1)}, bf16[64,2,8,128]{3,0,2,1:T(8,128)(2,1)}) fusion(f32[64,2,8,128]{3,0,2,1:T(8,128)} %copy.102, f32[2,8,128,64]{2,3,1,0:T(8,128)} %convolution_add_fusion.1, bf16[192,4,10,128]{3,0,2,1:T(8,128)(2,1)S(1)} %maximum_maximum_fusion, bf16[3,3,64,192]{3,2,1,0:T(8,128)(2,1)S(1)} %copy-done), kind=kOutput, calls=%fused_computation.58 | convolution fusion | flops 51904512 | bytes 2392064 | tf_op jit(solution)/shard_map/oj,jzyx->ozyx/dot_general | solution.py:310
  49.4 0.4 convolution_bitcast_fusion.10
  49.8 0.4 convolution_bitcast_fusion.11
  50.2 0.4 copy-done.7
  50.5 0.4 convolution_bitcast_fusion.12
  50.9 0.4 convolution_bitcast_fusion.7
  51.3 0.4 convolution_bitcast_fusion.8
  51.7 0.4 convolution_bitcast_fusion.9
  52.1 0.4 copy-done.3
  52.5 0.4 convolution_bitcast_fusion.4
  52.9 0.4 convolution_bitcast_fusion.5
  53.3 0.4 convolution_bitcast_fusion.6
  54.5 0.3 convolution_bitcast_fusion.2
  55.4 0.9 fusion.21.x_ref
  56.3 0.4 convolution_bitcast_fusion
  56.7 0.4 scatter-add.56
  57.2 0.6 fusion.98
  57.8 1.8 %fusion.7 = f32[192,4,10,128]{3,0,2,1:T(8,128)S(1)} fusion(f32[192,4,10,128]{3,0,2,1:T(8,128)S(1)} %scatter-add.56, s32[]{:T(128)} %bitcast.59, s32[]{:T(128)} %bitcast.60, bf16[64,2,8,128]{3,0,2,1:T(8,128)(2,1)S(1)} %get-tuple-element.281, bf16[3,3,64,192]{3,2,1,0:T(8,128)(2,1)S(1)} %copy-done), kind=kOutput, calls=%fused_computation.16 | convolution fusion | flops 50724864 | bytes 3440648 | tf_op jit(solution)/shard_map/oj,ozyx->jzyx/dot_general | solution.py:347
  59.6 0.7 and_reduce_fusion
  60.3 0.6 fusion.97
  60.9 2.4 %fusion = f32[192,4,10,128]{3,0,2,1:T(8,128)S(1)} fusion(f32[192,4,10,128]{3,0,2,1:T(8,128)S(1)} %fusion.7, s32[]{:T(128)} %bitcast.64, s32[]{:T(128)} %bitcast.65, bf16[64,2,8,128]{3,0,2,1:T(8,128)(2,1)S(1)} %get-tuple-element.281, pred[]{:T(512)} %get-tuple-element.298, bf16[3,3,64,192]{3,2,1,0:T(8,128)(2,1)S(1)} %copy-done), kind=kOutput, calls=%fused_computation.2 | convolution fusion | flops 51118080 | bytes 3440649 | tf_op jit(solution)/shard_map/oj,ozyx->jzyx/dot_general | solution.py:347
  63.3 0.6 fusion.6
  63.9 0.6 fusion.5
  64.5 0.6 fusion.4
  65.2 0.6 fusion.3
  65.8 0.6 fusion.2
  66.4 0.6 fusion.1
  67.0 0.5 fusion.88
  67.5 0.5 fusion.89
  67.9 1.0 fusion.86
  69.0 0.7 copy.201
  69.7 0.7 copy.202
  70.5 0.6 copy.125
  71.1 0.6 copy.126
  71.8 0.6 slice_bitcast_fusion.2
  72.4 50.2 %shard_map.76 = (f32[1408,128]{1,0:T(8,128)}, bf16[512,128]{1,0:T(8,128)(2,1)}, bf16[512,128]{1,0:T(8,128)(2,1)}, bf16[128,128]{1,0:T(8,128)(2,1)}, bf16[128,128...) custom-call(f32[1408,128]{1,0:T(8,128)} %fusion.21.x_ref, ...), custom_call_target="tpu_custom_call" | custom-call | tf_op jit(solution)/shard_map/pallas_call | solution.py:272
  122.7 1.0 bitcast_convert_fusion.1
  124.1 0.6 fusion.96
  124.7 1.9 %fusion.27 = f32[64,2,8,128]{3,0,2,1:T(8,128)S(1)} fusion(f32[64,2,8,128]{3,0,2,1:T(8,128)S(1)} %fusion.30, s32[]{:T(128)} %bitcast.136, s32[]{:T(128)} %bitcast.137, bf16[64,128]{1,0:T(8,128)(2,1)S(1)} %copy-done.24, pred[]{:T(512)} %get-tuple-element.297), kind=kLoop, calls=%fused_computation.81 | loop fusion | flops 24576 | bytes 81929 | tf_op jit(solution)/shard_map/scatter-add | solution.py:135
  126.6 1.1 copy.132
  127.7 1.0 mul.37
  128.7 0.7 slice_multiply_fusion.1
  129.4 0.5 copy.98
  129.9 0.3 dot_general.118
  130.6 0.7 copy.131
  (87 shorter events, 4.9 us)
Async XLA Ops:
  35.7 0.7 copy-start.14
  35.7 0.7 copy-start.15
  35.7 0.7 copy-start.16
  35.7 0.7 copy-start.17
  38.4 3.1 %copy-start = (bf16[3,3,64,192]{3,2,1,0:T(8,128)(2,1)S(1)}, bf16[3,3,64,192]{3,2,1,0:T(8,128)(2,1)}, u32[]{:S(2)}) copy-start(bf16[3,3,64,192]{3,2,1,0:T(8,128)(2,1)} %param.39) | copy-start | bytes 663556
  43.1 1.3 %copy-start.13 = (bf16[2,2,128,128]{3,2,1,0:T(8,128)(2,1)S(1)}, bf16[2,2,128,128]{3,2,1,0:T(8,128)(2,1)}, u32[]{:S(2)}) copy-start(bf16[2,2,128,128]{3,2,1,0:T(8,128)(2,1)} %param.40) | copy-start | bytes 393220
  43.1 1.5 %copy-start.18 = (bf16[128,1,256]{2,0,1:T(8,128)(2,1)S(1)}, bf16[128,1,256]{2,0,1:T(8,128)(2,1)}, u32[]{:S(2)}) copy-start(bf16[128,1,256]{2,0,1:T(8,128)(2,1)} %param.41) | copy-start | bytes 196612
  47.0 2.4 %copy-start.9 = (bf16[192,2,8,128]{3,0,2,1:T(8,128)(2,1)S(1)}, bf16[192,2,8,128]{3,0,2,1:T(8,128)(2,1)}, u32[]{:S(2)}) copy-start(bf16[192,2,8,128]{3,0,2,1:T(8,128)(2,1)} %get-tuple-element.267) | copy-start | bytes 2359300
  47.0 2.8 %copy-start.8 = (bf16[192,2,8,128]{3,0,2,1:T(8,128)(2,1)S(1)}, bf16[192,2,8,128]{3,0,2,1:T(8,128)(2,1)}, u32[]{:S(2)}) copy-start(bf16[192,2,8,128]{3,0,2,1:T(8,128)(2,1)} %get-tuple-element.268) | copy-start | bytes 2359300
  49.4 1.1 copy-start.7
  49.4 1.5 %copy-start.6 = (bf16[192,2,8,128]{3,0,2,1:T(8,128)(2,1)S(1)}, bf16[192,2,8,128]{3,0,2,1:T(8,128)(2,1)}, u32[]{:S(2)}) copy-start(bf16[192,2,8,128]{3,0,2,1:T(8,128)(2,1)} %get-tuple-element.264) | copy-start | bytes 2359300
  49.8 1.5 %copy-start.5 = (bf16[192,2,8,128]{3,0,2,1:T(8,128)(2,1)S(1)}, bf16[192,2,8,128]{3,0,2,1:T(8,128)(2,1)}, u32[]{:S(2)}) copy-start(bf16[192,2,8,128]{3,0,2,1:T(8,128)(2,1)} %get-tuple-element.265) | copy-start | bytes 2359300
  50.2 1.5 %copy-start.4 = (bf16[192,2,8,128]{3,0,2,1:T(8,128)(2,1)S(1)}, bf16[192,2,8,128]{3,0,2,1:T(8,128)(2,1)}, u32[]{:S(2)}) copy-start(bf16[192,2,8,128]{3,0,2,1:T(8,128)(2,1)} %get-tuple-element.266) | copy-start | bytes 2359300
  51.3 1.2 copy-start.3
  51.7 1.2 copy-start.2
  52.1 1.3 copy-start.1
  53.3 1.0 copy-start.11
  57.1 2.4 %copy-start.25 = (s32[4]{0:T(128)S(1)}, s32[4]{0:T(128)}, u32[]{:S(2)}) copy-start(s32[4]{0:T(128)} %constant.480.clone.1) | copy-start | bytes 52
  57.2 2.4 %copy-start.26 = (s32[4]{0:T(128)S(1)}, s32[4]{0:T(128)}, u32[]{:S(2)}) copy-start(s32[4]{0:T(128)} %constant.484.clone.1) | copy-start | bytes 52
  122.6 1.2 copy-start.12
  122.6 1.3 %copy-start.20 = (bf16[128,128]{1,0:T(8,128)(2,1)S(1)}, bf16[128,128]{1,0:T(8,128)(2,1)}, u32[]{:S(2)}) copy-start(bf16[128,128]{1,0:T(8,128)(2,1)} %get-tuple-element.235) | copy-start | bytes 98308
  122.6 1.4 %copy-start.19 = (bf16[128,128]{1,0:T(8,128)(2,1)S(1)}, bf16[128,128]{1,0:T(8,128)(2,1)}, u32[]{:S(2)}) copy-start(bf16[128,128]{1,0:T(8,128)(2,1)} %get-tuple-element.236) | copy-start | bytes 98308
  122.6 1.4 %copy-start.23 = (bf16[64,128]{1,0:T(8,128)(2,1)S(1)}, bf16[64,128]{1,0:T(8,128)(2,1)}, u32[]{:S(2)}) copy-start(bf16[64,128]{1,0:T(8,128)(2,1)} %get-tuple-element.237) | copy-start | bytes 49156
  122.6 2.0 %copy-start.24 = (bf16[64,128]{1,0:T(8,128)(2,1)S(1)}, bf16[64,128]{1,0:T(8,128)(2,1)}, u32[]{:S(2)}) copy-start(bf16[64,128]{1,0:T(8,128)(2,1)} %get-tuple-element.238) | copy-start | bytes 49156
  123.7 2.9 %copy-start.22 = (bf16[64,128]{1,0:T(8,128)(2,1)S(1)}, bf16[64,128]{1,0:T(8,128)(2,1)}, u32[]{:S(2)}) copy-start(bf16[64,128]{1,0:T(8,128)(2,1)} %get-tuple-element.239) | copy-start | bytes 49156
  123.7 2.9 %copy-start.21 = (bf16[64,128]{1,0:T(8,128)(2,1)S(1)}, bf16[64,128]{1,0:T(8,128)(2,1)}, u32[]{:S(2)}) copy-start(bf16[64,128]{1,0:T(8,128)(2,1)} %get-tuple-element.240) | copy-start | bytes 49156
  123.7 4.0 %copy-start.10 = (f32[1408,128]{1,0:T(8,128)S(1)}, f32[1408,128]{1,0:T(8,128)}, u32[]{:S(2)}) copy-start(f32[1408,128]{1,0:T(8,128)} %get-tuple-element.241) | copy-start | bytes 2162692

commit v6 on v5

--- a/solution.py
+++ b/solution.py
@@ -84,7 +84,7 @@
 
 
 def halo_swap(pieces, collective_id):
-    flat = [p.reshape(-1, 128) for p in pieces]
+    flat = [as_rows(p) for p in pieces]
     vmem = pl.BlockSpec(memory_space=pltpu.VMEM)
     got = pl.pallas_call(
         functools.partial(halo_kernel, NEIGHBOURS),
@@ -94,7 +94,16 @@
         scratch_shapes=[pltpu.SemaphoreType.DMA((len(flat),)), pltpu.SemaphoreType.DMA((len(flat),))],
         compiler_params=pltpu.CompilerParams(collective_id=collective_id, has_side_effects=True),
     )(*flat)
-    return [g.reshape(p.shape) for g, p in zip(got, pieces)]
+    return [from_rows(g, p.shape) for g, p in zip(got, pieces)]
+
+
+def as_rows(piece):
+    return jnp.transpose(piece, (1, 2, 0, 3)).reshape(-1, piece.shape[3])
+
+
+def from_rows(rows, shape):
+    channels, planes, lines, breadth = shape
+    return jnp.transpose(rows.reshape(planes, lines, channels, breadth), (2, 0, 1, 3))
 
 
 def ranges(shift, count, border):
@@ -287,12 +296,12 @@
     unit = 128 * 8 << HALVINGS
     padded = -(-flat.size // unit) * unit
     flat = jnp.pad(flat, (0, padded - flat.size)).reshape(-1, 128)
-    total, got = allreduce(flat, [p.reshape(-1, 128) for p in pieces])
+    total, got = allreduce(flat, [as_rows(p) for p in pieces])
     total = total.reshape(-1)
     return (
         total[: sizes[0]].reshape(local_conv.shape),
         total[sizes[0] : sizes[0] + sizes[1]].reshape(local_down.shape),
-        [g.reshape(p.shape) for g, p in zip(got, pieces)],
+        [from_rows(g, p.shape) for g, p in zip(got, pieces)],
     )
 
 

time: 133 us -> 130 us (0.977)
  local copies, waits for them, and re-layouts: 27.8 us -> 23.8 us
    reshape x7 -> x0, local copies, waits for them, and re-layouts: 6.31 us -> none  [the longest x4 3.38 us: halo_swap(): return [g.reshape(p.shape) for g, p in zip(got, pieces)]]
    transpose x0 -> x6, local copies, waits for them, and re-layouts: none -> 4.72 us  [as_rows(): return jnp.transpose(piece, (1, 2, 0, 3)).reshape(-1, piece.shape[3])]
    scatter-add x8, other arithmetic: 2.08 us -> 3.96 us  [folded_grad(): own.at[:, ranges(-dz, planes, 0), ranges(-dy, rows, 0)]]
    slice x6 -> x2, local copies, waits for them, and re-layouts: 2.81 us -> 1.35 us  [border_pieces(): pieces.append(spread[:, zs, ys].astype(jnp.bfloat16))]
    another operation x4 -> x6, local copies, waits for them, and re-layouts: 1.75 us -> 3.03 us
    unnamed x61 -> x65, local copies, waits for them, and re-layouts: 5.83 us -> 4.74 us
where the time goes in v6:
time: 130 us; the launch traced here: 128 us
  Pallas kernels  74.9 us (58%)
  local copies, waits for them, and re-layouts  23.8 us (18%)
  matrix products  17.8 us (14%)
  other arithmetic  10.4 us (8%)
  between operations  1.36 us (1%)
    pallas_call x1, Pallas kernels, allreduce(): pl.pallas_call(functools.partial(allreduce_kernel, bits, halvings, offset...  50.2 us
    pallas_call x1, Pallas kernels, halo_swap(): pl.pallas_call(functools.partial(halo_kernel, NEIGHBOURS), out_shape=[jax...  24.7 us
    dot_general x9, matrix products, body(): jnp.einsum('oj,ozyx->jzyx', conv_weight[tap_z, tap_y], gate_grad, preferr...  8.22 us
    dot_general x9, matrix products, body(): jnp.einsum('oj,jzyx->ozyx', conv_weight[tap_z, tap_y], window, preferred_...  5.3 us
    unnamed x65, local copies, waits for them, and re-layouts  4.74 us
    transpose x6, local copies, waits for them, and re-layouts, as_rows(): return jnp.transpose(piece, (1, 2, 0, 3)).reshape(-1, piece.shape[3])  4.72 us
    scatter-add x8, other arithmetic, folded_grad(): own.at[:, ranges(-dz, planes, 0), ranges(-dy, rows, 0)]  3.96 us
    dot_general x9, matrix products, body(): jnp.einsum('ozyx,jzyx->oj', gate_grad, window, preferred_element_type=jnp...  3.34 us

profile of v6, /device:TPU:1, one launch (start us, length us, event | category | flops | bytes accessed | tf_op | source)
XLA Modules:
  0.0 128.3 jit_solution(13700628674339045029)
XLA Ops:
  0.6 1.0 copy.88
  1.7 0.6 slice_bitcast_fusion.8
  2.3 1.0 slice_bitcast_fusion
  3.3 0.7 copy.84
  4.0 0.7 copy.85
  4.6 1.1 slice_bitcast_fusion.2
  5.8 0.6 copy.86
  6.4 0.6 copy.87
  7.0 24.7 %shard_map.75 = (bf16[512,128]{1,0:T(8,128)(2,1)}, bf16[512,128]{1,0:T(8,128)(2,1)}, bf16[128,128]{1,0:T(8,128)(2,1)}, bf16[128,128]{1,0:T(8,128)(2,1)}, bf16[64...) custom-call(bf16[512,128]{1,0:T(8,128)(2,1)} %bitcast.334, ...), custom_call_target="tpu_custom_call" | custom-call | tf_op jit(solution)/shard_map/pallas_call | solution.py:89
  31.7 1.1 maximum_maximum_fusion.1
  32.9 0.3 fusion.93
  33.3 0.3 fusion.94
  33.6 0.5 copy-done.11
  34.2 1.9 %maximum_maximum_fusion = bf16[192,4,10,128]{3,0,2,1:T(8,128)(2,1)S(1)} fusion(bf16[64,4,10,1]{3,0,2,1:T(8,128)(2,1)S(1)} %get-tuple-element.278, bf16[64,4,10,127]{3,0,2,1:T(8,128)(2,1)S(1)} %get-tuple-element.280, bf16[64,1,1,128]{3,0,2,1:T(8,128)(2,1)S(1)} %bitcast.356, bf16[64,1,8,128]{3,0,2,1:T(8,128)(2,1)S(1)} %bitcast.331, ...), kind=kLoop, calls=%fused_computation.1 | loop fusion | flops 25559040 | bytes 3932160 | tf_op jit(solution)/shard_map/concatenate | solution.py:43
  36.1 3.1 %fusion.90 = (bf16[192,2,8,128]{3,0,2,1:T(8,128)(2,1)}, bf16[192,2,8,128]{3,0,2,1:T(8,128)(2,1)}, bf16[192,2,8,128]{3,0,2,1:T(8,128)(2,1)}, bf16[192,2,8,128]{3,...) fusion(bf16[192,4,10,128]{3,0,2,1:T(8,128)(2,1)S(1)} %maximum_m, ...), kind=kLoop, calls=%fused_computation.164 | loop fusion | bytes 14155776 | tf_op jit(solution)/shard_map/slice | solution.py:318
  41.1 1.1 convolution_add_fusion.1
  42.4 0.3 convolution_bitcast_fusion.1
  42.7 0.8 copy.99
  43.5 1.1 copy.100
  44.6 2.4 %multiply_convert_fusion = (bf16[64,2,8,128]{3,0,2,1:T(8,128)(2,1)S(1)}, bf16[64,2,8,128]{3,0,2,1:T(8,128)(2,1)}) fusion(f32[64,2,8,128]{3,0,2,1:T(8,128)} %copy.100, f32[2,8,128,64]{2,3,1,0:T(8,128)} %convolution_add_fusion.1, bf16[192,4,10,128]{3,0,2,1:T(8,128)(2,1)S(1)} %maximum_maximum_fusion, bf16[3,3,64,192]{3,2,1,0:T(8,128)(2,1)S(1)} %copy-done), kind=kOutput, calls=%fused_computation.58 | convolution fusion | flops 51904512 | bytes 2392064 | tf_op jit(solution)/shard_map/oj,jzyx->ozyx/dot_general | solution.py:319
  47.1 0.4 convolution_bitcast_fusion.10
  47.5 0.4 convolution_bitcast_fusion.11
  47.9 0.4 copy-done.7
  48.2 0.4 convolution_bitcast_fusion.12
  48.6 0.4 convolution_bitcast_fusion.7
  49.0 0.4 convolution_bitcast_fusion.8
  49.4 0.4 convolution_bitcast_fusion.9
  49.8 0.4 copy-done.3
  50.1 0.4 convolution_bitcast_fusion.4
  50.6 0.4 convolution_bitcast_fusion.5
  51.0 0.4 convolution_bitcast_fusion.6
  51.4 0.3 reshape.776
  52.2 0.3 convolution_bitcast_fusion.2
  53.1 0.9 fusion.21.x_ref
  54.0 0.4 convolution_bitcast_fusion
  54.4 0.4 scatter-add.56
  54.9 0.6 fusion.97
  55.4 1.8 %fusion.7 = f32[192,4,10,128]{3,0,2,1:T(8,128)S(1)} fusion(f32[192,4,10,128]{3,0,2,1:T(8,128)S(1)} %scatter-add.56, s32[]{:T(128)} %bitcast.71, s32[]{:T(128)} %bitcast.72, bf16[64,2,8,128]{3,0,2,1:T(8,128)(2,1)S(1)} %get-tuple-element.281, bf16[3,3,64,192]{3,2,1,0:T(8,128)(2,1)S(1)} %copy-done), kind=kOutput, calls=%fused_computation.16 | convolution fusion | flops 50724864 | bytes 3440648 | tf_op jit(solution)/shard_map/oj,ozyx->jzyx/dot_general | solution.py:356
  57.3 0.8 and_reduce_fusion
  58.0 0.6 fusion.96
  58.6 2.4 %fusion = f32[192,4,10,128]{3,0,2,1:T(8,128)S(1)} fusion(f32[192,4,10,128]{3,0,2,1:T(8,128)S(1)} %fusion.7, s32[]{:T(128)} %bitcast.76, s32[]{:T(128)} %bitcast.77, bf16[64,2,8,128]{3,0,2,1:T(8,128)(2,1)S(1)} %get-tuple-element.281, pred[]{:T(512)} %get-tuple-element.298, bf16[3,3,64,192]{3,2,1,0:T(8,128)(2,1)S(1)} %copy-done), kind=kOutput, calls=%fused_computation.2 | convolution fusion | flops 51118080 | bytes 3440649 | tf_op jit(solution)/shard_map/oj,ozyx->jzyx/dot_general | solution.py:356
  61.1 0.6 fusion.6
  61.7 0.6 fusion.5
  62.3 0.6 fusion.4
  62.9 0.6 fusion.3
  63.5 0.6 fusion.2
  64.1 0.6 fusion.1
  64.7 0.5 fusion.88
  65.2 0.5 fusion.89
  65.7 0.9 fusion.86
  66.6 0.7 fusion.92
  67.3 0.6 fusion.91
  68.0 0.6 slice_bitcast_fusion.4
  68.6 50.2 %shard_map.76 = (f32[1408,128]{1,0:T(8,128)}, bf16[512,128]{1,0:T(8,128)(2,1)}, bf16[512,128]{1,0:T(8,128)(2,1)}, bf16[128,128]{1,0:T(8,128)(2,1)}, bf16[128,128...) custom-call(f32[1408,128]{1,0:T(8,128)} %fusion.21.x_ref, ...), custom_call_target="tpu_custom_call" | custom-call | tf_op jit(solution)/shard_map/pallas_call | solution.py:281
  119.0 1.0 fusion.24
  120.0 1.0 fusion.23
  121.0 0.6 fusion.95
  121.6 1.9 %fusion.27 = f32[64,2,8,128]{3,0,2,1:T(8,128)S(1)} fusion(f32[64,2,8,128]{3,0,2,1:T(8,128)S(1)} %fusion.30, s32[]{:T(128)} %bitcast.156, s32[]{:T(128)} %bitcast.157, bf16[64,128]{1,0:T(8,128)(2,1)S(1)} %copy-done.27, pred[]{:T(512)} %get-tuple-element.297), kind=kLoop, calls=%fused_computation.83 | loop fusion | flops 24576 | bytes 81929 | tf_op jit(solution)/shard_map/scatter-add | solution.py:144
  123.6 1.1 copy.122
  124.7 1.0 mul.37
  125.7 0.7 slice_multiply_fusion.1
  126.4 0.5 copy.96
  126.9 0.3 dot_general.118
  127.5 0.7 copy.121
  (83 shorter events, 3.8 us)
Async XLA Ops:
  33.2 0.9 copy-start.11
  33.2 1.0 copy-start.12
  33.2 1.0 copy-start.14
  33.2 0.9 copy-start.15
  33.2 0.9 copy-start.17
  33.3 0.9 copy-start.18
  33.3 0.9 copy-start.19
  33.3 0.9 copy-start.20
  36.1 3.1 %copy-start = (bf16[3,3,64,192]{3,2,1,0:T(8,128)(2,1)S(1)}, bf16[3,3,64,192]{3,2,1,0:T(8,128)(2,1)}, u32[]{:S(2)}) copy-start(bf16[3,3,64,192]{3,2,1,0:T(8,128)(2,1)} %param.39) | copy-start | bytes 663556
  40.8 1.3 %copy-start.16 = (bf16[2,2,128,128]{3,2,1,0:T(8,128)(2,1)S(1)}, bf16[2,2,128,128]{3,2,1,0:T(8,128)(2,1)}, u32[]{:S(2)}) copy-start(bf16[2,2,128,128]{3,2,1,0:T(8,128)(2,1)} %param.40) | copy-start | bytes 393220
  40.8 1.5 %copy-start.21 = (bf16[128,1,256]{2,0,1:T(8,128)(2,1)S(1)}, bf16[128,1,256]{2,0,1:T(8,128)(2,1)}, u32[]{:S(2)}) copy-start(bf16[128,1,256]{2,0,1:T(8,128)(2,1)} %param.41) | copy-start | bytes 196612
  44.6 2.4 %copy-start.9 = (bf16[192,2,8,128]{3,0,2,1:T(8,128)(2,1)S(1)}, bf16[192,2,8,128]{3,0,2,1:T(8,128)(2,1)}, u32[]{:S(2)}) copy-start(bf16[192,2,8,128]{3,0,2,1:T(8,128)(2,1)} %get-tuple-element.267) | copy-start | bytes 2359300
  44.6 2.8 %copy-start.8 = (bf16[192,2,8,128]{3,0,2,1:T(8,128)(2,1)S(1)}, bf16[192,2,8,128]{3,0,2,1:T(8,128)(2,1)}, u32[]{:S(2)}) copy-start(bf16[192,2,8,128]{3,0,2,1:T(8,128)(2,1)} %get-tuple-element.268) | copy-start | bytes 2359300
  47.1 1.1 copy-start.7
  47.1 1.5 %copy-start.6 = (bf16[192,2,8,128]{3,0,2,1:T(8,128)(2,1)S(1)}, bf16[192,2,8,128]{3,0,2,1:T(8,128)(2,1)}, u32[]{:S(2)}) copy-start(bf16[192,2,8,128]{3,0,2,1:T(8,128)(2,1)} %get-tuple-element.264) | copy-start | bytes 2359300
  47.5 1.5 %copy-start.5 = (bf16[192,2,8,128]{3,0,2,1:T(8,128)(2,1)S(1)}, bf16[192,2,8,128]{3,0,2,1:T(8,128)(2,1)}, u32[]{:S(2)}) copy-start(bf16[192,2,8,128]{3,0,2,1:T(8,128)(2,1)} %get-tuple-element.265) | copy-start | bytes 2359300
  47.8 1.5 %copy-start.4 = (bf16[192,2,8,128]{3,0,2,1:T(8,128)(2,1)S(1)}, bf16[192,2,8,128]{3,0,2,1:T(8,128)(2,1)}, u32[]{:S(2)}) copy-start(bf16[192,2,8,128]{3,0,2,1:T(8,128)(2,1)} %get-tuple-element.266) | copy-start | bytes 2359300
  49.0 1.2 copy-start.3
  49.4 1.2 copy-start.2
  49.7 1.3 copy-start.1
  50.9 1.0 copy-start.13
  54.8 2.4 %copy-start.28 = (s32[4]{0:T(128)S(1)}, s32[4]{0:T(128)}, u32[]{:S(2)}) copy-start(s32[4]{0:T(128)} %constant.480.clone.1) | copy-start | bytes 52
  54.8 2.4 %copy-start.29 = (s32[4]{0:T(128)S(1)}, s32[4]{0:T(128)}, u32[]{:S(2)}) copy-start(s32[4]{0:T(128)} %constant.484.clone.1) | copy-start | bytes 52
  118.8 2.1 %copy-start.23 = (bf16[128,128]{1,0:T(8,128)(2,1)S(1)}, bf16[128,128]{1,0:T(8,128)(2,1)}, u32[]{:S(2)}) copy-start(bf16[128,128]{1,0:T(8,128)(2,1)} %get-tuple-element.235) | copy-start | bytes 98308
  118.8 2.1 %copy-start.22 = (bf16[128,128]{1,0:T(8,128)(2,1)S(1)}, bf16[128,128]{1,0:T(8,128)(2,1)}, u32[]{:S(2)}) copy-start(bf16[128,128]{1,0:T(8,128)(2,1)} %get-tuple-element.236) | copy-start | bytes 98308
  118.9 2.1 %copy-start.26 = (bf16[64,128]{1,0:T(8,128)(2,1)S(1)}, bf16[64,128]{1,0:T(8,128)(2,1)}, u32[]{:S(2)}) copy-start(bf16[64,128]{1,0:T(8,128)(2,1)} %get-tuple-element.237) | copy-start | bytes 49156
  118.9 2.7 %copy-start.27 = (bf16[64,128]{1,0:T(8,128)(2,1)S(1)}, bf16[64,128]{1,0:T(8,128)(2,1)}, u32[]{:S(2)}) copy-start(bf16[64,128]{1,0:T(8,128)(2,1)} %get-tuple-element.238) | copy-start | bytes 49156
  118.9 4.7 %copy-start.25 = (bf16[64,128]{1,0:T(8,128)(2,1)S(1)}, bf16[64,128]{1,0:T(8,128)(2,1)}, u32[]{:S(2)}) copy-start(bf16[64,128]{1,0:T(8,128)(2,1)} %get-tuple-element.239) | copy-start | bytes 49156
  118.9 4.7 %copy-start.24 = (bf16[64,128]{1,0:T(8,128)(2,1)S(1)}, bf16[64,128]{1,0:T(8,128)(2,1)}, u32[]{:S(2)}) copy-start(bf16[64,128]{1,0:T(8,128)(2,1)} %get-tuple-element.240) | copy-start | bytes 49156
  118.9 5.8 %copy-start.10 = (f32[1408,128]{1,0:T(8,128)S(1)}, f32[1408,128]{1,0:T(8,128)}, u32[]{:S(2)}) copy-start(f32[1408,128]{1,0:T(8,128)} %get-tuple-element.241) | copy-start | bytes 2162692

commit v7 on v6

--- a/solution.py
+++ b/solution.py
@@ -290,9 +290,9 @@
     return outs[0], outs[1:]
 
 
-def summed_gradients(local_conv, local_down, pieces):
+def summed_gradients(local_conv, local_down, pieces, scale):
     sizes = (local_conv.size, local_down.size)
-    flat = jnp.concatenate([local_conv.reshape(-1), local_down.reshape(-1)])
+    flat = jnp.concatenate([local_conv.reshape(-1), local_down.reshape(-1)]) * scale
     unit = 128 * 8 << HALVINGS
     padded = -(-flat.size // unit) * unit
     flat = jnp.pad(flat, (0, padded - flat.size)).reshape(-1, 128)
@@ -361,11 +361,9 @@
             )
             spread = spread.at[:, tap_z : tap_z + plane_count, tap_y : tap_y + row_count].add(term)
     folded = fold_along(spread, channels)
-    summed_conv, summed_down, got = summed_gradients(local_conv, local_down, border_pieces(folded))
+    summed_conv, summed_down, got = summed_gradients(local_conv, local_down, border_pieces(folded), grad_scale)
     row_fold = folded_grad(folded, got)
-    grad_conv = summed_conv * grad_scale
-    grad_down = summed_down * grad_scale
-    return (section_out, row_fold, grad_conv, grad_down)
+    return (section_out, row_fold, summed_conv, summed_down)
 
 
 def solution(mesh):

time: 130 us -> 130 us (level)
  local copies, waits for them, and re-layouts: 23.8 us -> 25.4 us
  other arithmetic: 10.4 us -> 8.83 us
    reshape x1 -> x3, local copies, waits for them, and re-layouts: 0.31 us -> 2.19 us  [the longest x1 0.97 us: summed_gradients(): total[:sizes[0]].reshape(local_conv.shape)]
where the time goes in v7:
time: 130 us; the launch traced here: 128 us
  Pallas kernels  74.9 us (58%)
  local copies, waits for them, and re-layouts  25.4 us (20%)
  matrix products  17.8 us (14%)
  other arithmetic  8.83 us (7%)
  between operations  1.37 us (1%)
    pallas_call x1, Pallas kernels, allreduce(): pl.pallas_call(functools.partial(allreduce_kernel, bits, halvings, offset...  50.2 us
    pallas_call x1, Pallas kernels, halo_swap(): pl.pallas_call(functools.partial(halo_kernel, NEIGHBOURS), out_shape=[jax...  24.7 us
    dot_general x9, matrix products, body(): jnp.einsum('oj,ozyx->jzyx', conv_weight[tap_z, tap_y], gate_grad, preferr...  8.22 us
    dot_general x9, matrix products, body(): jnp.einsum('oj,jzyx->ozyx', conv_weight[tap_z, tap_y], window, preferred_...  5.3 us
    unnamed x65, local copies, waits for them, and re-layouts  4.74 us
    transpose x6, local copies, waits for them, and re-layouts, as_rows(): return jnp.transpose(piece, (1, 2, 0, 3)).reshape(-1, piece.shape[3])  4.72 us
    scatter-add x8, other arithmetic, folded_grad(): own.at[:, ranges(-dz, planes, 0), ranges(-dy, rows, 0)]  3.96 us
    dot_general x9, matrix products, body(): jnp.einsum('ozyx,jzyx->oj', gate_grad, window, preferred_element_type=jnp...  3.34 us

profile of v7, /device:TPU:1, one launch (start us, length us, event | category | flops | bytes accessed | tf_op | source)
XLA Modules:
  0.0 128.3 jit_solution(13855713871093225936)
XLA Ops:
  0.6 1.0 copy.88
  1.7 0.6 slice_bitcast_fusion.8
  2.3 1.0 slice_bitcast_fusion
  3.3 0.7 copy.84
  4.0 0.7 copy.85
  4.6 1.1 slice_bitcast_fusion.2
  5.8 0.6 copy.86
  6.4 0.6 copy.87
  7.0 24.7 %shard_map.75 = (bf16[512,128]{1,0:T(8,128)(2,1)}, bf16[512,128]{1,0:T(8,128)(2,1)}, bf16[128,128]{1,0:T(8,128)(2,1)}, bf16[128,128]{1,0:T(8,128)(2,1)}, bf16[64...) custom-call(bf16[512,128]{1,0:T(8,128)(2,1)} %bitcast.334, ...), custom_call_target="tpu_custom_call" | custom-call | tf_op jit(solution)/shard_map/pallas_call | solution.py:89
  31.7 1.1 maximum_maximum_fusion.1
  32.9 0.3 fusion.92
  33.3 0.3 fusion.93
  33.6 0.5 copy-done.11
  34.2 1.9 %maximum_maximum_fusion = bf16[192,4,10,128]{3,0,2,1:T(8,128)(2,1)S(1)} fusion(bf16[64,4,10,1]{3,0,2,1:T(8,128)(2,1)S(1)} %get-tuple-element.278, bf16[64,4,10,127]{3,0,2,1:T(8,128)(2,1)S(1)} %get-tuple-element.280, bf16[64,1,1,128]{3,0,2,1:T(8,128)(2,1)S(1)} %bitcast.356, bf16[64,1,8,128]{3,0,2,1:T(8,128)(2,1)S(1)} %bitcast.331, ...), kind=kLoop, calls=%fused_computation.1 | loop fusion | flops 25559040 | bytes 3932160 | tf_op jit(solution)/shard_map/concatenate | solution.py:43
  36.1 3.1 %fusion.89 = (bf16[192,2,8,128]{3,0,2,1:T(8,128)(2,1)}, bf16[192,2,8,128]{3,0,2,1:T(8,128)(2,1)}, bf16[192,2,8,128]{3,0,2,1:T(8,128)(2,1)}, bf16[192,2,8,128]{3,...) fusion(bf16[192,4,10,128]{3,0,2,1:T(8,128)(2,1)S(1)} %maximum_m, ...), kind=kLoop, calls=%fused_computation.161 | loop fusion | bytes 14155776 | tf_op jit(solution)/shard_map/slice | solution.py:318
  41.1 1.1 convolution_add_fusion.1
  42.4 0.3 convolution_bitcast_fusion.1
  42.7 0.8 copy.99
  43.5 1.1 copy.100
  44.6 2.4 %multiply_convert_fusion = (bf16[64,2,8,128]{3,0,2,1:T(8,128)(2,1)S(1)}, bf16[64,2,8,128]{3,0,2,1:T(8,128)(2,1)}) fusion(f32[64,2,8,128]{3,0,2,1:T(8,128)} %copy.100, f32[2,8,128,64]{2,3,1,0:T(8,128)} %convolution_add_fusion.1, bf16[192,4,10,128]{3,0,2,1:T(8,128)(2,1)S(1)} %maximum_maximum_fusion, bf16[3,3,64,192]{3,2,1,0:T(8,128)(2,1)S(1)} %copy-done), kind=kOutput, calls=%fused_computation.57 | convolution fusion | flops 51904512 | bytes 2392064 | tf_op jit(solution)/shard_map/oj,jzyx->ozyx/dot_general | solution.py:319
  47.1 0.4 convolution_bitcast_fusion.10
  47.5 0.4 convolution_bitcast_fusion.11
  47.9 0.4 copy-done.7
  48.2 0.4 convolution_bitcast_fusion.12
  48.6 0.4 convolution_bitcast_fusion.7
  49.0 0.4 convolution_bitcast_fusion.8
  49.4 0.4 convolution_bitcast_fusion.9
  49.8 0.4 copy-done.3
  50.1 0.4 convolution_bitcast_fusion.4
  50.6 0.4 convolution_bitcast_fusion.5
  51.0 0.4 convolution_bitcast_fusion.6
  51.4 0.3 reshape.776
  52.2 0.3 convolution_bitcast_fusion.2
  53.1 0.9 pad_bitcast_fusion.x_ref
  54.0 0.4 convolution_bitcast_fusion
  54.5 0.4 scatter-add.56
  54.9 0.6 fusion.96
  55.5 1.8 %fusion.7 = f32[192,4,10,128]{3,0,2,1:T(8,128)S(1)} fusion(f32[192,4,10,128]{3,0,2,1:T(8,128)S(1)} %scatter-add.56, s32[]{:T(128)} %bitcast.71, s32[]{:T(128)} %bitcast.72, bf16[64,2,8,128]{3,0,2,1:T(8,128)(2,1)S(1)} %get-tuple-element.281, bf16[3,3,64,192]{3,2,1,0:T(8,128)(2,1)S(1)} %copy-done), kind=kOutput, calls=%fused_computation.16 | convolution fusion | flops 50724864 | bytes 3440648 | tf_op jit(solution)/shard_map/oj,ozyx->jzyx/dot_general | solution.py:356
  57.3 0.8 and_reduce_fusion
  58.1 0.6 fusion.95
  58.7 2.4 %fusion = f32[192,4,10,128]{3,0,2,1:T(8,128)S(1)} fusion(f32[192,4,10,128]{3,0,2,1:T(8,128)S(1)} %fusion.7, s32[]{:T(128)} %bitcast.76, s32[]{:T(128)} %bitcast.77, bf16[64,2,8,128]{3,0,2,1:T(8,128)(2,1)S(1)} %get-tuple-element.281, pred[]{:T(512)} %get-tuple-element.298, bf16[3,3,64,192]{3,2,1,0:T(8,128)(2,1)S(1)} %copy-done), kind=kOutput, calls=%fused_computation.2 | convolution fusion | flops 51118080 | bytes 3440649 | tf_op jit(solution)/shard_map/oj,ozyx->jzyx/dot_general | solution.py:356
  61.1 0.6 fusion.6
  61.7 0.6 fusion.5
  62.3 0.6 fusion.4
  62.9 0.6 fusion.3
  63.6 0.6 fusion.2
  64.2 0.6 fusion.1
  64.8 0.5 fusion.87
  65.3 0.5 fusion.88
  65.7 0.9 fusion.85
  66.7 0.7 fusion.91
  67.4 0.6 fusion.90
  68.0 0.6 slice_bitcast_fusion.4
  68.7 50.2 %shard_map.76 = (f32[1408,128]{1,0:T(8,128)}, bf16[512,128]{1,0:T(8,128)(2,1)}, bf16[512,128]{1,0:T(8,128)(2,1)}, bf16[128,128]{1,0:T(8,128)(2,1)}, bf16[128,128...) custom-call(f32[1408,128]{1,0:T(8,128)} %pad_bitcast_fusion.x_ref, ...), custom_call_target="tpu_custom_call" | custom-call | tf_op jit(solution)/shard_map/pallas_call | solution.py:281
  119.0 1.0 fusion.23
  120.0 1.0 fusion.22
  121.1 0.6 fusion.94
  121.7 1.9 %fusion.26 = f32[64,2,8,128]{3,0,2,1:T(8,128)S(1)} fusion(f32[64,2,8,128]{3,0,2,1:T(8,128)S(1)} %fusion.29, s32[]{:T(128)} %bitcast.156, s32[]{:T(128)} %bitcast.157, bf16[64,128]{1,0:T(8,128)(2,1)S(1)} %copy-done.27, pred[]{:T(512)} %get-tuple-element.297), kind=kLoop, calls=%fused_computation.80 | loop fusion | flops 24576 | bytes 81929 | tf_op jit(solution)/shard_map/scatter-add | solution.py:144
  123.6 1.1 copy.122
  124.8 1.0 reshape.784
  125.8 0.7 slice.807
  126.5 0.5 copy.96
  127.0 0.3 dot_general.118
  127.6 0.7 copy.121
  (84 shorter events, 3.8 us)
Async XLA Ops:
  33.2 0.9 copy-start.11
  33.2 1.0 copy-start.12
  33.2 1.0 copy-start.14
  33.2 0.9 copy-start.15
  33.2 0.9 copy-start.17
  33.3 0.9 copy-start.18
  33.3 0.9 copy-start.19
  33.3 0.9 copy-start.20
  36.1 3.1 %copy-start = (bf16[3,3,64,192]{3,2,1,0:T(8,128)(2,1)S(1)}, bf16[3,3,64,192]{3,2,1,0:T(8,128)(2,1)}, u32[]{:S(2)}) copy-start(bf16[3,3,64,192]{3,2,1,0:T(8,128)(2,1)} %param.39) | copy-start | bytes 663556
  40.8 1.3 %copy-start.16 = (bf16[2,2,128,128]{3,2,1,0:T(8,128)(2,1)S(1)}, bf16[2,2,128,128]{3,2,1,0:T(8,128)(2,1)}, u32[]{:S(2)}) copy-start(bf16[2,2,128,128]{3,2,1,0:T(8,128)(2,1)} %param.40) | copy-start | bytes 393220
  40.8 1.5 %copy-start.21 = (bf16[128,1,256]{2,0,1:T(8,128)(2,1)S(1)}, bf16[128,1,256]{2,0,1:T(8,128)(2,1)}, u32[]{:S(2)}) copy-start(bf16[128,1,256]{2,0,1:T(8,128)(2,1)} %param.41) | copy-start | bytes 196612
  44.6 2.4 %copy-start.9 = (bf16[192,2,8,128]{3,0,2,1:T(8,128)(2,1)S(1)}, bf16[192,2,8,128]{3,0,2,1:T(8,128)(2,1)}, u32[]{:S(2)}) copy-start(bf16[192,2,8,128]{3,0,2,1:T(8,128)(2,1)} %get-tuple-element.267) | copy-start | bytes 2359300
  44.6 2.8 %copy-start.8 = (bf16[192,2,8,128]{3,0,2,1:T(8,128)(2,1)S(1)}, bf16[192,2,8,128]{3,0,2,1:T(8,128)(2,1)}, u32[]{:S(2)}) copy-start(bf16[192,2,8,128]{3,0,2,1:T(8,128)(2,1)} %get-tuple-element.268) | copy-start | bytes 2359300
  47.1 1.1 copy-start.7
  47.1 1.5 %copy-start.6 = (bf16[192,2,8,128]{3,0,2,1:T(8,128)(2,1)S(1)}, bf16[192,2,8,128]{3,0,2,1:T(8,128)(2,1)}, u32[]{:S(2)}) copy-start(bf16[192,2,8,128]{3,0,2,1:T(8,128)(2,1)} %get-tuple-element.264) | copy-start | bytes 2359300
  47.5 1.5 %copy-start.5 = (bf16[192,2,8,128]{3,0,2,1:T(8,128)(2,1)S(1)}, bf16[192,2,8,128]{3,0,2,1:T(8,128)(2,1)}, u32[]{:S(2)}) copy-start(bf16[192,2,8,128]{3,0,2,1:T(8,128)(2,1)} %get-tuple-element.265) | copy-start | bytes 2359300
  47.8 1.5 %copy-start.4 = (bf16[192,2,8,128]{3,0,2,1:T(8,128)(2,1)S(1)}, bf16[192,2,8,128]{3,0,2,1:T(8,128)(2,1)}, u32[]{:S(2)}) copy-start(bf16[192,2,8,128]{3,0,2,1:T(8,128)(2,1)} %get-tuple-element.266) | copy-start | bytes 2359300
  49.0 1.2 copy-start.3
  49.4 1.2 copy-start.2
  49.7 1.3 copy-start.1
  50.9 1.0 copy-start.13
  54.9 2.4 %copy-start.28 = (s32[4]{0:T(128)S(1)}, s32[4]{0:T(128)}, u32[]{:S(2)}) copy-start(s32[4]{0:T(128)} %constant.479.clone.1) | copy-start | bytes 52
  54.9 2.4 %copy-start.29 = (s32[4]{0:T(128)S(1)}, s32[4]{0:T(128)}, u32[]{:S(2)}) copy-start(s32[4]{0:T(128)} %constant.484.clone.1) | copy-start | bytes 52
  118.9 2.1 %copy-start.23 = (bf16[128,128]{1,0:T(8,128)(2,1)S(1)}, bf16[128,128]{1,0:T(8,128)(2,1)}, u32[]{:S(2)}) copy-start(bf16[128,128]{1,0:T(8,128)(2,1)} %get-tuple-element.235) | copy-start | bytes 98308
  118.9 2.1 %copy-start.22 = (bf16[128,128]{1,0:T(8,128)(2,1)S(1)}, bf16[128,128]{1,0:T(8,128)(2,1)}, u32[]{:S(2)}) copy-start(bf16[128,128]{1,0:T(8,128)(2,1)} %get-tuple-element.236) | copy-start | bytes 98308
  118.9 2.1 %copy-start.26 = (bf16[64,128]{1,0:T(8,128)(2,1)S(1)}, bf16[64,128]{1,0:T(8,128)(2,1)}, u32[]{:S(2)}) copy-start(bf16[64,128]{1,0:T(8,128)(2,1)} %get-tuple-element.237) | copy-start | bytes 49156
  118.9 2.7 %copy-start.27 = (bf16[64,128]{1,0:T(8,128)(2,1)S(1)}, bf16[64,128]{1,0:T(8,128)(2,1)}, u32[]{:S(2)}) copy-start(bf16[64,128]{1,0:T(8,128)(2,1)} %get-tuple-element.238) | copy-start | bytes 49156
  118.9 4.7 %copy-start.25 = (bf16[64,128]{1,0:T(8,128)(2,1)S(1)}, bf16[64,128]{1,0:T(8,128)(2,1)}, u32[]{:S(2)}) copy-start(bf16[64,128]{1,0:T(8,128)(2,1)} %get-tuple-element.239) | copy-start | bytes 49156
  118.9 4.7 %copy-start.24 = (bf16[64,128]{1,0:T(8,128)(2,1)S(1)}, bf16[64,128]{1,0:T(8,128)(2,1)}, u32[]{:S(2)}) copy-start(bf16[64,128]{1,0:T(8,128)(2,1)} %get-tuple-element.240) | copy-start | bytes 49156
  118.9 5.8 %copy-start.10 = (f32[1408,128]{1,0:T(8,128)S(1)}, f32[1408,128]{1,0:T(8,128)}, u32[]{:S(2)}) copy-start(f32[1408,128]{1,0:T(8,128)} %get-tuple-element.241) | copy-start | bytes 2162692

commit v8 on v7

--- a/solution.py
+++ b/solution.py
@@ -114,15 +114,37 @@
     return slice(border, border + count)
 
 
-def framed_features(features):
-    _, planes, rows, _ = features.shape
-    pieces = [features[:, ranges(dz, planes, 0), ranges(dy, rows, 0)] for dz, dy in NEIGHBOURS]
-    got = dict(zip(NEIGHBOURS, halo_swap(pieces, 1)))
+def halo_pieces(cells):
+    _, planes, rows, _ = cells.shape
+    return [cells[:, ranges(dz, planes, 0), ranges(dy, rows, 0)] for dz, dy in NEIGHBOURS]
+
+
+def framed(cells, received):
+    got = dict(zip(NEIGHBOURS, received))
     lines = []
     for dz in (1, 0, -1):
-        middle = features if dz == 0 else got[(dz, 0)]
+        middle = cells if dz == 0 else got[(dz, 0)]
         lines.append(jnp.concatenate([got[(dz, 1)], middle, got[(dz, -1)]], axis=2))
     return jnp.concatenate(lines, axis=1)
+
+
+def conv_taps(columns, weight, shape):
+    _, planes, rows, _ = shape
+    total = jnp.zeros(shape, jnp.float32)
+    for tap_z in range(3):
+        for tap_y in range(3):
+            window = columns[:, tap_z : tap_z + planes, tap_y : tap_y + rows]
+            total = total + jnp.einsum(
+                "oj,jzyx->ozyx", weight[tap_z, tap_y], window, preferred_element_type=jnp.float32
+            )
+    return total
+
+
+def transposed_weight(conv_weight):
+    taps_z, taps_y, channels, width = conv_weight.shape
+    split = conv_weight.reshape(taps_z, taps_y, channels, width // channels, channels)
+    split = split[::-1, ::-1, :, ::-1, :]
+    return jnp.transpose(split, (0, 1, 4, 3, 2)).reshape(taps_z, taps_y, channels, width)
 
 
 def border_pieces(spread):
@@ -310,18 +332,8 @@
     out_channels = down_weight.shape[2]
     cell_count = plane_count * row_count * breadth * lax.axis_size("gz") * lax.axis_size("gy")
     grad_scale = 1.0 / math.sqrt(cell_count)
-    framed = framed_features(features)
-    columns = widen(framed)
-    preact = jnp.zeros((channels, plane_count, row_count, breadth), jnp.float32)
-    for tap_z in range(3):
-        for tap_y in range(3):
-            window = columns[:, tap_z : tap_z + plane_count, tap_y : tap_y + row_count]
-            preact = preact + jnp.einsum(
-                "oj,jzyx->ozyx",
-                conv_weight[tap_z, tap_y],
-                window,
-                preferred_element_type=jnp.float32,
-            )
+    columns = widen(framed(features, halo_swap(halo_pieces(features), 1)))
+    preact = conv_taps(columns, conv_weight, features.shape)
     hidden = jax.nn.silu(preact).astype(jnp.bfloat16)
     blocks = hidden.reshape(channels, plane_count // 2, 2, row_count // 2, 2, breadth // 2, 2)
     down_split = down_weight.reshape(2, 2, out_channels, 2, channels)
@@ -350,20 +362,10 @@
             )
         kernel_rows.append(jnp.stack(row_list, axis=0))
     local_conv = jnp.stack(kernel_rows, axis=0)
-    spread = jnp.zeros((3 * channels, plane_count + 2, row_count + 2, breadth), jnp.float32)
-    for tap_z in range(3):
-        for tap_y in range(3):
-            term = jnp.einsum(
-                "oj,ozyx->jzyx",
-                conv_weight[tap_z, tap_y],
-                gate_grad,
-                preferred_element_type=jnp.float32,
-            )
-            spread = spread.at[:, tap_z : tap_z + plane_count, tap_y : tap_y + row_count].add(term)
-    folded = fold_along(spread, channels)
-    summed_conv, summed_down, got = summed_gradients(local_conv, local_down, border_pieces(folded), grad_scale)
-    row_fold = folded_grad(folded, got)
-    return (section_out, row_fold, summed_conv, summed_down)
+    summed_conv, summed_down, got = summed_gradients(local_conv, local_down, halo_pieces(gate_grad), grad_scale)
+    gate_columns = widen(framed(gate_grad, got))
+    grad_field = conv_taps(gate_columns, transposed_weight(conv_weight), features.shape)
+    return (section_out, grad_field, summed_conv, summed_down)
 
 
 def solution(mesh):

time: 130 us -> 117 us (0.900)
  matrix products: 17.8 us -> 11 us
  local copies, waits for them, and re-layouts: 25.4 us -> 22.3 us
  other arithmetic: 8.83 us -> 6.32 us
    dot_general x18, matrix products: 13.5 us -> 5.79 us  [conv_taps(): jnp.einsum('oj,jzyx->ozyx', weight[tap_z, tap_y], window, preferred_eleme...]
    scatter-add x8 -> x0, other arithmetic: 3.96 us -> none  [folded_grad(): own.at[:, ranges(-dz, planes, 0), ranges(-dy, rows, 0)]]
    slice x6 -> x3, local copies, waits for them, and re-layouts: 5.41 us -> 3.1 us  [the longest x1 1.76 us: conv_taps(): window = columns[:, tap_z:tap_z + planes, tap_y:tap_y + rows]]
    concatenate x1 -> x2, other arithmetic: 1.86 us -> 3.89 us  [widen(): jnp.concatenate([jnp.roll(framed, 1 - tap_x, axis=3) for tap_x in range(3...]
    transpose x6, local copies, waits for them, and re-layouts: 4.72 us -> 2.7 us  [as_rows(): return jnp.transpose(piece, (1, 2, 0, 3)).reshape(-1, piece.shape[3])]
    another operation x4 -> x0, local copies, waits for them, and re-layouts: 1.75 us -> none
    another operation x4 -> x0, other arithmetic: 1.73 us -> none
    unnamed x65 -> x46, local copies, waits for them, and re-layouts: 4.74 us -> 5.39 us
where the time goes in v8:
time: 117 us; the launch traced here: 116 us
  Pallas kernels  75 us (64%)
  local copies, waits for them, and re-layouts  22.3 us (19%)
  matrix products  11 us (9%)
  other arithmetic  6.32 us (5%)
  between operations  1.23 us (1%)
    pallas_call x1, Pallas kernels, allreduce(): pl.pallas_call(functools.partial(allreduce_kernel, bits, halvings, offset...  50.2 us
    pallas_call x1, Pallas kernels, halo_swap(): pl.pallas_call(functools.partial(halo_kernel, NEIGHBOURS), out_shape=[jax...  24.7 us
    dot_general x18, matrix products, conv_taps(): jnp.einsum('oj,jzyx->ozyx', weight[tap_z, tap_y], window, preferred_eleme...  5.79 us
    unnamed x46, local copies, waits for them, and re-layouts  5.39 us
    concatenate x2, other arithmetic, widen(): jnp.concatenate([jnp.roll(framed, 1 - tap_x, axis=3) for tap_x in range(3...  3.89 us
    dot_general x9, matrix products, body(): jnp.einsum('ozyx,jzyx->oj', gate_grad, window, preferred_element_type=jnp...  3.32 us
    transpose x6, local copies, waits for them, and re-layouts, as_rows(): return jnp.transpose(piece, (1, 2, 0, 3)).reshape(-1, piece.shape[3])  2.7 us

profile of v8, /device:TPU:1, one launch (start us, length us, event | category | flops | bytes accessed | tf_op | source)
XLA Modules:
  0.0 115.8 jit_solution(8333773042507423258)
XLA Ops:
  0.6 0.9 copy.110
  1.6 1.0 copy.109
  2.6 0.3 convolution_bitcast_fusion
  3.0 0.8 copy.111
  3.8 0.3 copy.112
  4.1 0.7 copy.96
  4.8 0.7 copy.97
  5.6 0.6 copy.98
  6.2 0.6 copy.99
  6.9 0.6 slice_bitcast_fusion.26
  7.5 24.7 %shard_map.75 = (bf16[512,128]{1,0:T(8,128)(2,1)}, bf16[512,128]{1,0:T(8,128)(2,1)}, bf16[128,128]{1,0:T(8,128)(2,1)}, bf16[128,128]{1,0:T(8,128)(2,1)}, bf16[64...) custom-call(bf16[512,128]{1,0:T(8,128)(2,1)} %bitcast.353, ...), custom_call_target="tpu_custom_call" | custom-call | tf_op jit(solution)/shard_map/pallas_call | solution.py:89
  32.3 1.1 maximum_maximum_fusion.2
  33.4 0.3 fusion.64
  33.8 0.3 fusion.65
  34.1 0.5 copy-done.6
  34.7 2.0 %maximum_maximum_fusion = bf16[192,4,10,128]{3,0,2,1:T(8,128)(2,1)S(1)} fusion(bf16[64,4,10,1]{3,0,2,1:T(8,128)(2,1)S(1)} %get-tuple-element.64, bf16[64,4,10,127]{3,0,2,1:T(8,128)(2,1)S(1)} %get-tuple-element.66, bf16[64,1,1,128]{3,0,2,1:T(8,128)(2,1)S(1)} %bitcast.385, bf16[64,1,8,128]{3,0,2,1:T(8,128)(2,1)S(1)} %bitcast.350, ...), kind=kLoop, calls=%fused_computation | loop fusion | flops 25559040 | bytes 3932160 | tf_op jit(solution)/shard_map/concatenate | solution.py:43
  37.1 0.3 convolution_add_fusion.15
  37.3 0.3 convolution_add_fusion.14
  37.6 0.3 convolution_add_fusion.13
  37.9 0.3 convolution_add_fusion.12
  38.4 0.3 convolution_add_fusion.10
  38.7 0.3 convolution_add_fusion.9
  38.9 1.1 multiply_convert_fusion
  40.1 1.2 %copy.107 = bf16[64,2,8,128]{0,3,2,1:T(8,128)(2,1)S(1)} copy(bf16[64,2,8,128]{3,0,2,1:T(8,128)(2,1)} %get-tuple-element.68) | data formatting | bytes 524288 | tf_op jit(solution)/shard_map/convert_element_type | solution.py:337
  41.3 0.5 copy.108
  41.8 1.0 dot_general.126
  42.8 1.2 %fusion.3 = bf16[128,1,256]{0,2,1:T(8,128)(2,1)S(1)} fusion(bf16[256,2,2,2,64]{0,4,3,2,1:T(8,128)(2,1)} %dot_general.126, bf16[2,2,128,2,64]{2,4,3,1,0:T(8,128)(2,1)S(1)} %bitcast.352), kind=kOutput, calls=%fused_computation.33 | convolution fusion | flops 33587200 | bytes 458752 | tf_op jit(solution)/shard_map/aboei,iZaYbXe->oZYX/dot_general | solution.py:340
  44.1 0.7 copy.144
  44.8 0.3 convolution_bitcast_fusion.1
  45.4 0.3 reshape_reshape.3
  45.7 1.8 %fusion.61 = (bf16[192,2,8,128]{3,0,2,1:T(8,128)(2,1)S(1)}, bf16[192,2,8,128]{3,0,2,1:T(8,128)(2,1)S(1)}, bf16[192,2,8,128]{3,0,2,1:T(8,128)(2,1)S(1)}, bf16[192...) fusion(bf16[192,4,10,128]{3,0,2,1:T(8,128)(2,1)S(1)} %maximum_m, ...), kind=kLoop, calls=%fused_computation.124 | loop fusion | bytes 14155776 | tf_op jit(solution)/shard_map/slice | solution.py:136
  47.5 0.4 convolution_bitcast_fusion.3
  47.9 0.4 convolution_bitcast_fusion.4
  48.2 0.4 convolution_bitcast_fusion.5
  48.6 0.4 convolution_bitcast_fusion.9
  49.0 0.4 convolution_bitcast_fusion.10
  49.4 0.4 convolution_bitcast_fusion.11
  49.7 0.4 convolution_bitcast_fusion.6
  50.1 0.4 convolution_bitcast_fusion.7
  50.5 0.4 convolution_bitcast_fusion.8
  50.9 0.3 reshape.118
  51.3 0.9 pad_bitcast_fusion.x_ref
  52.2 0.7 fusion.67
  53.0 0.6 fusion.66
  53.6 0.6 slice_bitcast_fusion.22
  54.2 50.2 %shard_map.76 = (f32[1408,128]{1,0:T(8,128)}, bf16[512,128]{1,0:T(8,128)(2,1)}, bf16[512,128]{1,0:T(8,128)(2,1)}, bf16[128,128]{1,0:T(8,128)(2,1)}, bf16[128,128...) custom-call(f32[1408,128]{1,0:T(8,128)} %pad_bitcast_fusion.x_ref, ...), custom_call_target="tpu_custom_call" | custom-call | tf_op jit(solution)/shard_map/pallas_call | solution.py:303
  104.5 1.1 maximum_maximum_fusion.3
  105.6 0.3 fusion.62
  106.0 0.3 fusion.63
  106.3 0.5 copy-done.4
  106.9 1.9 %maximum_maximum_fusion.1 = bf16[192,4,10,128]{3,0,2,1:T(8,128)(2,1)S(1)} fusion(bf16[64,4,10,1]{3,0,2,1:T(8,128)(2,1)S(1)} %get-tuple-element.60, bf16[64,4,10,127]{3,0,2,1:T(8,128)(2,1)S(1)} %get-tuple-element.62, bf16[64,1,1,128]{3,0,2,1:T(8,128)(2,1)S(1)} %bitcast.377, bf16[64,1,8,128]{3,0,2,1:T(8,128)(2,1)S(1)} %bitcast.346, ...), kind=kLoop, calls=%fused_computation.1 | loop fusion | flops 25559040 | bytes 3932160 | tf_op jit(solution)/shard_map/concatenate | solution.py:43
  108.8 0.3 copy.133
  109.4 0.3 fusion.12
  109.7 0.3 convolution_add_fusion.7
  110.0 0.3 convolution_add_fusion.6
  110.3 0.3 convolution_add_fusion.5
  110.5 0.3 convolution_add_fusion.4
  110.8 0.3 convolution_add_fusion.3
  111.1 0.3 convolution_add_fusion.2
  111.4 0.3 convolution_add_fusion.1
  111.7 0.3 fusion
  112.0 1.1 copy.145
  113.2 1.0 reshape.130
  114.1 1.7 %slice.262 = f32[512,128]{1,0:T(8,128)} slice(f32[1408,128]{1,0:T(8,128)} %get-tuple-element.37), slice={[864:1376], [0:128]} | slice | bytes 524288 | tf_op jit(solution)/shard_map/slice | solution.py:325
  (51 shorter events, 1.6 us)
Async XLA Ops:
  2.9 1.2 copy-start
  33.7 0.9 copy-start.6
  33.7 1.0 copy-start.7
  33.8 1.0 copy-start.10
  33.8 0.9 copy-start.11
  33.8 0.9 copy-start.16
  33.8 0.9 copy-start.17
  33.8 0.9 copy-start.18
  33.8 0.9 copy-start.19
  34.7 2.1 %copy-start.1 = (bf16[3,3,64,192]{3,2,1,0:T(8,128)(2,1)S(1)}, bf16[3,3,64,192]{3,2,1,0:T(8,128)(2,1)}, u32[]{:S(2)}) copy-start(bf16[3,3,64,192]{3,2,1,0:T(8,128)(2,1)} %param.5) | copy-start | bytes 663556
  105.9 0.9 copy-start.4
  105.9 1.0 copy-start.5
  105.9 1.0 copy-start.8
  106.0 0.9 copy-start.9
  106.0 0.9 copy-start.12
  106.0 0.9 copy-start.13
  106.0 0.9 copy-start.14
  106.0 0.9 copy-start.15
  106.9 1.9 %copy-start.2 = (bf16[3,3,64,192]{3,2,1,0:T(8,128)(2,1)S(1)}, bf16[3,3,64,192]{3,2,1,0:T(8,128)(2,1)}, u32[]{:S(2)}) copy-start(bf16[3,3,64,192]{3,2,1,0:T(8,128)(2,1)} %param.5) | copy-start | bytes 663556
  111.4 1.7 %copy-start.3 = (f32[1408,128]{1,0:T(8,128)S(1)}, f32[1408,128]{1,0:T(8,128)}, u32[]{:S(2)}) copy-start(f32[1408,128]{1,0:T(8,128)} %get-tuple-element.37) | copy-start | bytes 2162692

commit v9 on v8

--- a/solution.py
+++ b/solution.py
@@ -20,7 +20,7 @@
     (("gz", 2), ("gz", 4)),
     (("gy", 3), ("gy", 3)),
 )
-HALVINGS = 4
+HALVINGS = 3
 
 
 def extended(cells, sides, width):

time: 117 us -> 122 us (1.043)
  Pallas kernels: 75 us -> 80.9 us
    pallas_call x1, Pallas kernels: 50.2 us -> 56.1 us  [allreduce(): pl.pallas_call(functools.partial(allreduce_kernel, bits, halvings, offset...]
where the time goes in v9:
time: 122 us
  Pallas kernels  80.9 us (66%)
  local copies, waits for them, and re-layouts  22.3 us (18%)
  matrix products  11 us (9%)
  other arithmetic  6.54 us (5%)
  between operations  1.23 us (1%)
    pallas_call x1, Pallas kernels, allreduce(): pl.pallas_call(functools.partial(allreduce_kernel, bits, halvings, offset...  56.1 us
    pallas_call x1, Pallas kernels, halo_swap(): pl.pallas_call(functools.partial(halo_kernel, NEIGHBOURS), out_shape=[jax...  24.7 us
    dot_general x18, matrix products, conv_taps(): jnp.einsum('oj,jzyx->ozyx', weight[tap_z, tap_y], window, preferred_eleme...  5.78 us
    unnamed x46, local copies, waits for them, and re-layouts  5.39 us
    concatenate x2, other arithmetic, widen(): jnp.concatenate([jnp.roll(framed, 1 - tap_x, axis=3) for tap_x in range(3...  4.11 us
    dot_general x9, matrix products, body(): jnp.einsum('ozyx,jzyx->oj', gate_grad, window, preferred_element_type=jnp...  3.32 us
    transpose x6, local copies, waits for them, and re-layouts, as_rows(): return jnp.transpose(piece, (1, 2, 0, 3)).reshape(-1, piece.shape[3])  2.7 us

profile of v9, /device:TPU:1, one launch (start us, length us, event | category | flops | bytes accessed | tf_op | source)
XLA Modules:
  0.0 121.9 jit_solution(8551752524013953334)
XLA Ops:
  0.6 0.9 copy.110
  1.6 1.0 copy.109
  2.6 0.3 convolution_bitcast_fusion
  3.0 0.8 copy.111
  3.8 0.3 copy.112
  4.1 0.7 copy.96
  4.8 0.7 copy.97
  5.6 0.6 copy.98
  6.2 0.6 copy.99
  6.9 0.6 slice_bitcast_fusion.26
  7.5 24.7 %shard_map.75 = (bf16[512,128]{1,0:T(8,128)(2,1)}, bf16[512,128]{1,0:T(8,128)(2,1)}, bf16[128,128]{1,0:T(8,128)(2,1)}, bf16[128,128]{1,0:T(8,128)(2,1)}, bf16[64...) custom-call(bf16[512,128]{1,0:T(8,128)(2,1)} %bitcast.353, ...), custom_call_target="tpu_custom_call" | custom-call | tf_op jit(solution)/shard_map/pallas_call | solution.py:89
  32.3 1.1 maximum_maximum_fusion.2
  33.4 0.3 fusion.64
  33.8 0.3 fusion.65
  34.1 0.5 copy-done.6
  34.7 2.0 %maximum_maximum_fusion = bf16[192,4,10,128]{3,0,2,1:T(8,128)(2,1)S(1)} fusion(bf16[64,4,10,1]{3,0,2,1:T(8,128)(2,1)S(1)} %get-tuple-element.64, bf16[64,4,10,127]{3,0,2,1:T(8,128)(2,1)S(1)} %get-tuple-element.66, bf16[64,1,1,128]{3,0,2,1:T(8,128)(2,1)S(1)} %bitcast.385, bf16[64,1,8,128]{3,0,2,1:T(8,128)(2,1)S(1)} %bitcast.350, ...), kind=kLoop, calls=%fused_computation | loop fusion | flops 25559040 | bytes 3932160 | tf_op jit(solution)/shard_map/concatenate | solution.py:43
  37.1 0.3 convolution_add_fusion.15
  37.3 0.3 convolution_add_fusion.14
  37.6 0.3 convolution_add_fusion.13
  37.9 0.3 convolution_add_fusion.12
  38.4 0.3 convolution_add_fusion.10
  38.7 0.3 convolution_add_fusion.9
  38.9 1.1 multiply_convert_fusion
  40.1 1.2 %copy.107 = bf16[64,2,8,128]{0,3,2,1:T(8,128)(2,1)S(1)} copy(bf16[64,2,8,128]{3,0,2,1:T(8,128)(2,1)} %get-tuple-element.68) | data formatting | bytes 524288 | tf_op jit(solution)/shard_map/convert_element_type | solution.py:337
  41.3 0.5 copy.108
  41.8 1.0 dot_general.126
  42.8 1.2 %fusion.3 = bf16[128,1,256]{0,2,1:T(8,128)(2,1)S(1)} fusion(bf16[256,2,2,2,64]{0,4,3,2,1:T(8,128)(2,1)} %dot_general.126, bf16[2,2,128,2,64]{2,4,3,1,0:T(8,128)(2,1)S(1)} %bitcast.352), kind=kOutput, calls=%fused_computation.33 | convolution fusion | flops 33587200 | bytes 458752 | tf_op jit(solution)/shard_map/aboei,iZaYbXe->oZYX/dot_general | solution.py:340
  44.1 0.7 copy.144
  44.8 0.3 convolution_bitcast_fusion.1
  45.4 0.3 reshape_reshape.3
  45.7 1.8 %fusion.61 = (bf16[192,2,8,128]{3,0,2,1:T(8,128)(2,1)S(1)}, bf16[192,2,8,128]{3,0,2,1:T(8,128)(2,1)S(1)}, bf16[192,2,8,128]{3,0,2,1:T(8,128)(2,1)S(1)}, bf16[192...) fusion(bf16[192,4,10,128]{3,0,2,1:T(8,128)(2,1)S(1)} %maximum_m, ...), kind=kLoop, calls=%fused_computation.124 | loop fusion | bytes 14155776 | tf_op jit(solution)/shard_map/slice | solution.py:136
  47.5 0.4 convolution_bitcast_fusion.3
  47.9 0.4 convolution_bitcast_fusion.4
  48.2 0.4 convolution_bitcast_fusion.5
  48.6 0.4 convolution_bitcast_fusion.9
  49.0 0.4 convolution_bitcast_fusion.10
  49.4 0.4 convolution_bitcast_fusion.11
  49.7 0.4 convolution_bitcast_fusion.6
  50.1 0.4 convolution_bitcast_fusion.7
  50.5 0.4 convolution_bitcast_fusion.8
  50.9 0.3 reshape.118
  51.3 0.9 pad_bitcast_fusion.x_ref
  52.2 0.7 fusion.67
  53.0 0.6 fusion.66
  53.6 0.6 slice_bitcast_fusion.22
  54.2 56.1 %shard_map.76 = (f32[1408,128]{1,0:T(8,128)}, bf16[512,128]{1,0:T(8,128)(2,1)}, bf16[512,128]{1,0:T(8,128)(2,1)}, bf16[128,128]{1,0:T(8,128)(2,1)}, bf16[128,128...) custom-call(f32[1408,128]{1,0:T(8,128)} %pad_bitcast_fusion.x_ref, ...), custom_call_target="tpu_custom_call" | custom-call | tf_op jit(solution)/shard_map/pallas_call | solution.py:303
  110.4 1.1 maximum_maximum_fusion.3
  111.5 0.3 fusion.62
  111.9 0.3 fusion.63
  112.2 0.5 copy-done.4
  112.8 2.1 %maximum_maximum_fusion.1 = bf16[192,4,10,128]{3,0,2,1:T(8,128)(2,1)S(1)} fusion(bf16[64,4,10,1]{3,0,2,1:T(8,128)(2,1)S(1)} %get-tuple-element.60, bf16[64,4,10,127]{3,0,2,1:T(8,128)(2,1)S(1)} %get-tuple-element.62, bf16[64,1,1,128]{3,0,2,1:T(8,128)(2,1)S(1)} %bitcast.377, bf16[64,1,8,128]{3,0,2,1:T(8,128)(2,1)S(1)} %bitcast.346, ...), kind=kLoop, calls=%fused_computation.1 | loop fusion | flops 25559040 | bytes 3932160 | tf_op jit(solution)/shard_map/concatenate | solution.py:43
  114.9 0.3 copy.133
  115.5 0.3 fusion.12
  115.8 0.3 convolution_add_fusion.7
  116.1 0.3 convolution_add_fusion.6
  116.4 0.3 convolution_add_fusion.5
  116.7 0.3 convolution_add_fusion.4
  117.0 0.3 convolution_add_fusion.3
  117.3 0.3 convolution_add_fusion.2
  117.6 0.3 convolution_add_fusion.1
  117.9 0.3 fusion
  118.1 1.1 copy.145
  119.3 1.0 reshape.130
  120.3 1.7 %slice.262 = f32[512,128]{1,0:T(8,128)} slice(f32[1408,128]{1,0:T(8,128)} %get-tuple-element.37), slice={[864:1376], [0:128]} | slice | bytes 524288 | tf_op jit(solution)/shard_map/slice | solution.py:325
  (51 shorter events, 1.6 us)
Async XLA Ops:
  2.9 1.2 copy-start
  33.7 0.9 copy-start.6
  33.7 1.0 copy-start.7
  33.8 1.0 copy-start.10
  33.8 0.9 copy-start.11
  33.8 0.9 copy-start.16
  33.8 0.9 copy-start.17
  33.8 0.9 copy-start.18
  33.8 0.9 copy-start.19
  34.7 2.1 %copy-start.1 = (bf16[3,3,64,192]{3,2,1,0:T(8,128)(2,1)S(1)}, bf16[3,3,64,192]{3,2,1,0:T(8,128)(2,1)}, u32[]{:S(2)}) copy-start(bf16[3,3,64,192]{3,2,1,0:T(8,128)(2,1)} %param.5) | copy-start | bytes 663556
  111.8 0.9 copy-start.4
  111.8 1.0 copy-start.5
  111.8 1.0 copy-start.8
  111.9 0.9 copy-start.9
  111.9 0.9 copy-start.12
  111.9 0.9 copy-start.13
  111.9 0.9 copy-start.14
  111.9 0.9 copy-start.15
  112.8 2.1 %copy-start.2 = (bf16[3,3,64,192]{3,2,1,0:T(8,128)(2,1)S(1)}, bf16[3,3,64,192]{3,2,1,0:T(8,128)(2,1)}, u32[]{:S(2)}) copy-start(bf16[3,3,64,192]{3,2,1,0:T(8,128)(2,1)} %param.5) | copy-start | bytes 663556
  117.5 1.7 %copy-start.3 = (f32[1408,128]{1,0:T(8,128)S(1)}, f32[1408,128]{1,0:T(8,128)}, u32[]{:S(2)}) copy-start(f32[1408,128]{1,0:T(8,128)} %get-tuple-element.37) | copy-start | bytes 2162692

commit v10 on v8

--- a/solution.py
+++ b/solution.py
@@ -215,6 +215,33 @@
     for dz, dy in offsets:
         pl.semaphore_signal(barrier, inc=1, device_id=neighbour(dz, dy), device_id_type=MESH_ID)
     pl.semaphore_wait(barrier, len(reach) + count)
+
+    def exchange(step, pair, src, dst):
+        start_copy(step, (pair,), src, dst).wait()
+
+    def start_copy(step, pairs, src, dst):
+        copy = pltpu.make_async_remote_copy(
+            src_ref=src,
+            dst_ref=dst,
+            send_sem=send_sems.at[step],
+            recv_sem=recv_sems.at[step],
+            device_id=partner(*pairs),
+            device_id_type=MESH_ID,
+        )
+        copy.start()
+        return copy
+
+    lo, length, step = 0, o_ref.shape[0], 0
+    for k in range(halvings):
+        pair = bits[k]
+        half = length // 2
+        bit = bit_of(pair)
+        keep = pl.multiple_of(lo + bit * half, 8)
+        give = pl.multiple_of(lo + (1 - bit) * half, 8)
+        source = x_ref if k == 0 else work
+        exchange(step, pair, source.at[pl.ds(give, half)], halve_bufs[k])
+        work[pl.ds(keep, half)] = source[pl.ds(keep, half)] + halve_bufs[k][...]
+        lo, length, step = keep, half, step + 1
     halo = []
     for i, (dz, dy) in enumerate(offsets):
         copy = pltpu.make_async_remote_copy(
@@ -227,33 +254,6 @@
         )
         copy.start()
         halo.append(copy)
-
-    def exchange(step, pair, src, dst):
-        start_copy(step, (pair,), src, dst).wait()
-
-    def start_copy(step, pairs, src, dst):
-        copy = pltpu.make_async_remote_copy(
-            src_ref=src,
-            dst_ref=dst,
-            send_sem=send_sems.at[step],
-            recv_sem=recv_sems.at[step],
-            device_id=partner(*pairs),
-            device_id_type=MESH_ID,
-        )
-        copy.start()
-        return copy
-
-    lo, length, step = 0, o_ref.shape[0], 0
-    for k in range(halvings):
-        pair = bits[k]
-        half = length // 2
-        bit = bit_of(pair)
-        keep = pl.multiple_of(lo + bit * half, 8)
-        give = pl.multiple_of(lo + (1 - bit) * half, 8)
-        source = x_ref if k == 0 else work
-        exchange(step, pair, source.at[pl.ds(give, half)], halve_bufs[k])
-        work[pl.ds(keep, half)] = source[pl.ds(keep, half)] + halve_bufs[k][...]
-        lo, length, step = keep, half, step + 1
     slot = 0
     for group in groups:
         own = work.at[pl.ds(lo, length)]

time: 117 us -> 120 us (1.026)
  Pallas kernels: 75 us -> 79 us
    pallas_call x1, Pallas kernels: 50.2 us -> 54.2 us  [allreduce(): pl.pallas_call(functools.partial(allreduce_kernel, bits, halvings, offset...]
where the time goes in v10:
time: 120 us
  Pallas kernels  79 us (66%)
  local copies, waits for them, and re-layouts  22.3 us (19%)
  matrix products  11 us (9%)
  other arithmetic  6.32 us (5%)
  between operations  1.23 us (1%)
    pallas_call x1, Pallas kernels, allreduce(): pl.pallas_call(functools.partial(allreduce_kernel, bits, halvings, offset...  54.2 us
    pallas_call x1, Pallas kernels, halo_swap(): pl.pallas_call(functools.partial(halo_kernel, NEIGHBOURS), out_shape=[jax...  24.7 us
    dot_general x18, matrix products, conv_taps(): jnp.einsum('oj,jzyx->ozyx', weight[tap_z, tap_y], window, preferred_eleme...  5.79 us
    unnamed x46, local copies, waits for them, and re-layouts  5.39 us
    concatenate x2, other arithmetic, widen(): jnp.concatenate([jnp.roll(framed, 1 - tap_x, axis=3) for tap_x in range(3...  3.89 us
    dot_general x9, matrix products, body(): jnp.einsum('ozyx,jzyx->oj', gate_grad, window, preferred_element_type=jnp...  3.32 us
    transpose x6, local copies, waits for them, and re-layouts, as_rows(): return jnp.transpose(piece, (1, 2, 0, 3)).reshape(-1, piece.shape[3])  2.7 us

profile of v10, /device:TPU:1, one launch (start us, length us, event | category | flops | bytes accessed | tf_op | source)
XLA Modules:
  0.0 119.8 jit_solution(7674177586979970957)
XLA Ops:
  0.6 0.9 copy.110
  1.6 1.0 copy.109
  2.6 0.3 convolution_bitcast_fusion
  3.0 0.8 copy.111
  3.8 0.3 copy.112
  4.1 0.7 copy.96
  4.8 0.7 copy.97
  5.6 0.6 copy.98
  6.2 0.6 copy.99
  6.9 0.6 slice_bitcast_fusion.26
  7.5 24.7 %shard_map.75 = (bf16[512,128]{1,0:T(8,128)(2,1)}, bf16[512,128]{1,0:T(8,128)(2,1)}, bf16[128,128]{1,0:T(8,128)(2,1)}, bf16[128,128]{1,0:T(8,128)(2,1)}, bf16[64...) custom-call(bf16[512,128]{1,0:T(8,128)(2,1)} %bitcast.353, ...), custom_call_target="tpu_custom_call" | custom-call | tf_op jit(solution)/shard_map/pallas_call | solution.py:89
  32.3 1.1 maximum_maximum_fusion.2
  33.4 0.3 fusion.64
  33.8 0.3 fusion.65
  34.1 0.5 copy-done.6
  34.7 2.0 %maximum_maximum_fusion = bf16[192,4,10,128]{3,0,2,1:T(8,128)(2,1)S(1)} fusion(bf16[64,4,10,1]{3,0,2,1:T(8,128)(2,1)S(1)} %get-tuple-element.64, bf16[64,4,10,127]{3,0,2,1:T(8,128)(2,1)S(1)} %get-tuple-element.66, bf16[64,1,1,128]{3,0,2,1:T(8,128)(2,1)S(1)} %bitcast.385, bf16[64,1,8,128]{3,0,2,1:T(8,128)(2,1)S(1)} %bitcast.350, ...), kind=kLoop, calls=%fused_computation | loop fusion | flops 25559040 | bytes 3932160 | tf_op jit(solution)/shard_map/concatenate | solution.py:43
  37.1 0.3 convolution_add_fusion.15
  37.3 0.3 convolution_add_fusion.14
  37.6 0.3 convolution_add_fusion.13
  37.9 0.3 convolution_add_fusion.12
  38.4 0.3 convolution_add_fusion.10
  38.7 0.3 convolution_add_fusion.9
  38.9 1.1 multiply_convert_fusion
  40.1 1.2 %copy.107 = bf16[64,2,8,128]{0,3,2,1:T(8,128)(2,1)S(1)} copy(bf16[64,2,8,128]{3,0,2,1:T(8,128)(2,1)} %get-tuple-element.68) | data formatting | bytes 524288 | tf_op jit(solution)/shard_map/convert_element_type | solution.py:337
  41.3 0.5 copy.108
  41.8 1.0 dot_general.126
  42.8 1.2 %fusion.3 = bf16[128,1,256]{0,2,1:T(8,128)(2,1)S(1)} fusion(bf16[256,2,2,2,64]{0,4,3,2,1:T(8,128)(2,1)} %dot_general.126, bf16[2,2,128,2,64]{2,4,3,1,0:T(8,128)(2,1)S(1)} %bitcast.352), kind=kOutput, calls=%fused_computation.33 | convolution fusion | flops 33587200 | bytes 458752 | tf_op jit(solution)/shard_map/aboei,iZaYbXe->oZYX/dot_general | solution.py:340
  44.1 0.7 copy.144
  44.8 0.3 convolution_bitcast_fusion.1
  45.4 0.3 reshape_reshape.3
  45.7 1.8 %fusion.61 = (bf16[192,2,8,128]{3,0,2,1:T(8,128)(2,1)S(1)}, bf16[192,2,8,128]{3,0,2,1:T(8,128)(2,1)S(1)}, bf16[192,2,8,128]{3,0,2,1:T(8,128)(2,1)S(1)}, bf16[192...) fusion(bf16[192,4,10,128]{3,0,2,1:T(8,128)(2,1)S(1)} %maximum_m, ...), kind=kLoop, calls=%fused_computation.124 | loop fusion | bytes 14155776 | tf_op jit(solution)/shard_map/slice | solution.py:136
  47.5 0.4 convolution_bitcast_fusion.3
  47.9 0.4 convolution_bitcast_fusion.4
  48.2 0.4 convolution_bitcast_fusion.5
  48.6 0.4 convolution_bitcast_fusion.9
  49.0 0.4 convolution_bitcast_fusion.10
  49.4 0.4 convolution_bitcast_fusion.11
  49.7 0.4 convolution_bitcast_fusion.6
  50.1 0.4 convolution_bitcast_fusion.7
  50.5 0.4 convolution_bitcast_fusion.8
  50.9 0.3 reshape.118
  51.3 0.9 pad_bitcast_fusion.x_ref
  52.2 0.7 fusion.67
  53.0 0.6 fusion.66
  53.6 0.6 slice_bitcast_fusion.22
  54.2 54.2 %shard_map.76 = (f32[1408,128]{1,0:T(8,128)}, bf16[512,128]{1,0:T(8,128)(2,1)}, bf16[512,128]{1,0:T(8,128)(2,1)}, bf16[128,128]{1,0:T(8,128)(2,1)}, bf16[128,128...) custom-call(f32[1408,128]{1,0:T(8,128)} %pad_bitcast_fusion.x_ref, ...), custom_call_target="tpu_custom_call" | custom-call | tf_op jit(solution)/shard_map/pallas_call | solution.py:303
  108.4 1.1 maximum_maximum_fusion.3
  109.6 0.3 fusion.62
  110.0 0.3 fusion.63
  110.3 0.5 copy-done.4
  110.9 1.9 %maximum_maximum_fusion.1 = bf16[192,4,10,128]{3,0,2,1:T(8,128)(2,1)S(1)} fusion(bf16[64,4,10,1]{3,0,2,1:T(8,128)(2,1)S(1)} %get-tuple-element.60, bf16[64,4,10,127]{3,0,2,1:T(8,128)(2,1)S(1)} %get-tuple-element.62, bf16[64,1,1,128]{3,0,2,1:T(8,128)(2,1)S(1)} %bitcast.377, bf16[64,1,8,128]{3,0,2,1:T(8,128)(2,1)S(1)} %bitcast.346, ...), kind=kLoop, calls=%fused_computation.1 | loop fusion | flops 25559040 | bytes 3932160 | tf_op jit(solution)/shard_map/concatenate | solution.py:43
  112.8 0.3 copy.133
  113.3 0.3 fusion.12
  113.6 0.3 convolution_add_fusion.7
  113.9 0.3 convolution_add_fusion.6
  114.2 0.3 convolution_add_fusion.5
  114.5 0.3 convolution_add_fusion.4
  114.8 0.3 convolution_add_fusion.3
  115.1 0.3 convolution_add_fusion.2
  115.4 0.3 convolution_add_fusion.1
  115.7 0.3 fusion
  116.0 1.1 copy.145
  117.1 1.0 reshape.130
  118.1 1.7 %slice.262 = f32[512,128]{1,0:T(8,128)} slice(f32[1408,128]{1,0:T(8,128)} %get-tuple-element.37), slice={[864:1376], [0:128]} | slice | bytes 524288 | tf_op jit(solution)/shard_map/slice | solution.py:325
  (51 shorter events, 1.6 us)
Async XLA Ops:
  2.9 1.2 copy-start
  33.7 0.9 copy-start.6
  33.7 1.0 copy-start.7
  33.8 1.0 copy-start.10
  33.8 0.9 copy-start.11
  33.8 0.9 copy-start.16
  33.8 0.9 copy-start.17
  33.8 0.9 copy-start.18
  33.8 0.9 copy-start.19
  34.7 2.1 %copy-start.1 = (bf16[3,3,64,192]{3,2,1,0:T(8,128)(2,1)S(1)}, bf16[3,3,64,192]{3,2,1,0:T(8,128)(2,1)}, u32[]{:S(2)}) copy-start(bf16[3,3,64,192]{3,2,1,0:T(8,128)(2,1)} %param.5) | copy-start | bytes 663556
  109.9 0.9 copy-start.4
  109.9 1.0 copy-start.5
  109.9 1.0 copy-start.8
  109.9 0.9 copy-start.9
  109.9 0.9 copy-start.12
  110.0 0.9 copy-start.13
  110.0 0.9 copy-start.14
  110.0 0.9 copy-start.15
  110.9 1.9 %copy-start.2 = (bf16[3,3,64,192]{3,2,1,0:T(8,128)(2,1)S(1)}, bf16[3,3,64,192]{3,2,1,0:T(8,128)(2,1)}, u32[]{:S(2)}) copy-start(bf16[3,3,64,192]{3,2,1,0:T(8,128)(2,1)} %param.5) | copy-start | bytes 663556
  115.4 1.7 %copy-start.3 = (f32[1408,128]{1,0:T(8,128)S(1)}, f32[1408,128]{1,0:T(8,128)}, u32[]{:S(2)}) copy-start(f32[1408,128]{1,0:T(8,128)} %get-tuple-element.37) | copy-start | bytes 2162692

commit v11 on v8

--- a/solution.py
+++ b/solution.py
@@ -14,11 +14,11 @@
     (("gy", 1), ("gz", 0)),
     (("gz", 0), ("gz", 3)),
     (("gz", 3), ("gy", 1)),
-    (("gy", 2), ("gz", 1)),
-    (("gz", 1), ("gy", 2)),
-    (("gz", 4), ("gz", 2)),
-    (("gz", 2), ("gz", 4)),
-    (("gy", 3), ("gy", 3)),
+    (("gz", 1), ("gz", 4)),
+    (("gz", 2), ("gy", 3)),
+    (("gz", 4), ("gz", 1)),
+    (("gy", 3), ("gz", 2)),
+    (("gy", 2), ("gy", 2)),
 )
 HALVINGS = 4
 

time: 117 us -> 115 us (0.983)
  Pallas kernels: 75 us -> 72.9 us
    pallas_call x1, Pallas kernels: 50.2 us -> 48.2 us  [allreduce(): pl.pallas_call(functools.partial(allreduce_kernel, bits, halvings, offset...]
where the time goes in v11:
time: 115 us; the launch traced here: 114 us
  Pallas kernels  72.9 us (63%)
  local copies, waits for them, and re-layouts  22.3 us (19%)
  matrix products  11 us (10%)
  other arithmetic  6.32 us (5%)
  between operations  1.23 us (1%)
    pallas_call x1, Pallas kernels, allreduce(): pl.pallas_call(functools.partial(allreduce_kernel, bits, halvings, offset...  48.2 us
    pallas_call x1, Pallas kernels, halo_swap(): pl.pallas_call(functools.partial(halo_kernel, NEIGHBOURS), out_shape=[jax...  24.7 us
    dot_general x18, matrix products, conv_taps(): jnp.einsum('oj,jzyx->ozyx', weight[tap_z, tap_y], window, preferred_eleme...  5.79 us
    unnamed x46, local copies, waits for them, and re-layouts  5.39 us
    concatenate x2, other arithmetic, widen(): jnp.concatenate([jnp.roll(framed, 1 - tap_x, axis=3) for tap_x in range(3...  3.89 us
    dot_general x9, matrix products, body(): jnp.einsum('ozyx,jzyx->oj', gate_grad, window, preferred_element_type=jnp...  3.32 us
    transpose x6, local copies, waits for them, and re-layouts, as_rows(): return jnp.transpose(piece, (1, 2, 0, 3)).reshape(-1, piece.shape[3])  2.7 us

profile of v11, /device:TPU:1, one launch (start us, length us, event | category | flops | bytes accessed | tf_op | source)
XLA Modules:
  0.0 113.7 jit_solution(14959798293474698530)
XLA Ops:
  0.6 0.9 copy.110
  1.6 1.0 copy.109
  2.6 0.3 convolution_bitcast_fusion
  3.0 0.8 copy.111
  3.8 0.3 copy.112
  4.1 0.7 copy.96
  4.8 0.7 copy.97
  5.6 0.6 copy.98
  6.2 0.6 copy.99
  6.9 0.6 slice_bitcast_fusion.26
  7.5 24.7 %shard_map.75 = (bf16[512,128]{1,0:T(8,128)(2,1)}, bf16[512,128]{1,0:T(8,128)(2,1)}, bf16[128,128]{1,0:T(8,128)(2,1)}, bf16[128,128]{1,0:T(8,128)(2,1)}, bf16[64...) custom-call(bf16[512,128]{1,0:T(8,128)(2,1)} %bitcast.353, ...), custom_call_target="tpu_custom_call" | custom-call | tf_op jit(solution)/shard_map/pallas_call | solution.py:89
  32.3 1.1 %maximum_maximum_fusion.2 = bf16[64,4,10,128]{3,0,2,1:T(8,128)(2,1)S(1)} fusion(bf16[64,1,1,128]{3,0,2,1:T(8,128)(2,1)} %bitcast.384, bf16[64,1,8,128]{3,0,2,1:T(8,128)(2,1)} %bitcast.349, bf16[64,1,1,128]{3,0,2,1:T(8,128)(2,1)} %bitcast.382, bf16[64,2,1,128]{3,0,2,1:T(8,128)(2,1)} %bitcast.364, bf16[64,2,8,128]{3,0,2,1:T(8,128)(2,1)S(1)} %copy.100, ...), kind=kLoop, calls=%fused_computation.55 | loop fusion | flops 2621440 | bytes 1310720 | tf_op jit(solution)/shard_map/concatenate | solution.py:128
  33.4 0.3 fusion.64
  33.8 0.3 fusion.65
  34.1 0.5 copy-done.6
  34.7 2.0 %maximum_maximum_fusion = bf16[192,4,10,128]{3,0,2,1:T(8,128)(2,1)S(1)} fusion(bf16[64,4,10,1]{3,0,2,1:T(8,128)(2,1)S(1)} %get-tuple-element.64, bf16[64,4,10,127]{3,0,2,1:T(8,128)(2,1)S(1)} %get-tuple-element.66, bf16[64,1,1,128]{3,0,2,1:T(8,128)(2,1)S(1)} %bitcast.385, bf16[64,1,8,128]{3,0,2,1:T(8,128)(2,1)S(1)} %bitcast.350, ...), kind=kLoop, calls=%fused_computation | loop fusion | flops 25559040 | bytes 3932160 | tf_op jit(solution)/shard_map/concatenate | solution.py:43
  37.1 0.3 convolution_add_fusion.15
  37.3 0.3 convolution_add_fusion.14
  37.6 0.3 convolution_add_fusion.13
  37.9 0.3 convolution_add_fusion.12
  38.4 0.3 convolution_add_fusion.10
  38.7 0.3 convolution_add_fusion.9
  38.9 1.1 multiply_convert_fusion
  40.1 1.2 %copy.107 = bf16[64,2,8,128]{0,3,2,1:T(8,128)(2,1)S(1)} copy(bf16[64,2,8,128]{3,0,2,1:T(8,128)(2,1)} %get-tuple-element.68) | data formatting | bytes 524288 | tf_op jit(solution)/shard_map/convert_element_type | solution.py:337
  41.3 0.5 copy.108
  41.8 1.0 dot_general.126
  42.8 1.2 %fusion.3 = bf16[128,1,256]{0,2,1:T(8,128)(2,1)S(1)} fusion(bf16[256,2,2,2,64]{0,4,3,2,1:T(8,128)(2,1)} %dot_general.126, bf16[2,2,128,2,64]{2,4,3,1,0:T(8,128)(2,1)S(1)} %bitcast.352), kind=kOutput, calls=%fused_computation.33 | convolution fusion | flops 33587200 | bytes 458752 | tf_op jit(solution)/shard_map/aboei,iZaYbXe->oZYX/dot_general | solution.py:340
  44.1 0.7 copy.144
  44.8 0.3 convolution_bitcast_fusion.1
  45.4 0.3 reshape_reshape.3
  45.7 1.8 %fusion.61 = (bf16[192,2,8,128]{3,0,2,1:T(8,128)(2,1)S(1)}, bf16[192,2,8,128]{3,0,2,1:T(8,128)(2,1)S(1)}, bf16[192,2,8,128]{3,0,2,1:T(8,128)(2,1)S(1)}, bf16[192...) fusion(bf16[192,4,10,128]{3,0,2,1:T(8,128)(2,1)S(1)} %maximum_m, ...), kind=kLoop, calls=%fused_computation.124 | loop fusion | bytes 14155776 | tf_op jit(solution)/shard_map/slice | solution.py:136
  47.5 0.4 convolution_bitcast_fusion.3
  47.9 0.4 convolution_bitcast_fusion.4
  48.2 0.4 convolution_bitcast_fusion.5
  48.6 0.4 convolution_bitcast_fusion.9
  49.0 0.4 convolution_bitcast_fusion.10
  49.4 0.4 convolution_bitcast_fusion.11
  49.7 0.4 convolution_bitcast_fusion.6
  50.1 0.4 convolution_bitcast_fusion.7
  50.5 0.4 convolution_bitcast_fusion.8
  50.9 0.3 reshape.118
  51.3 0.9 pad_bitcast_fusion.x_ref
  52.2 0.7 fusion.67
  53.0 0.6 fusion.66
  53.6 0.6 slice_bitcast_fusion.22
  54.2 48.2 %shard_map.76 = (f32[1408,128]{1,0:T(8,128)}, bf16[512,128]{1,0:T(8,128)(2,1)}, bf16[512,128]{1,0:T(8,128)(2,1)}, bf16[128,128]{1,0:T(8,128)(2,1)}, bf16[128,128...) custom-call(f32[1408,128]{1,0:T(8,128)} %pad_bitcast_fusion.x_ref, ...), custom_call_target="tpu_custom_call" | custom-call | tf_op jit(solution)/shard_map/pallas_call | solution.py:303
  102.4 1.1 %maximum_maximum_fusion.3 = bf16[64,4,10,128]{3,0,2,1:T(8,128)(2,1)S(1)} fusion(bf16[64,1,1,128]{3,0,2,1:T(8,128)(2,1)} %bitcast.376, bf16[64,1,8,128]{3,0,2,1:T(8,128)(2,1)} %bitcast.345, bf16[64,1,1,128]{3,0,2,1:T(8,128)(2,1)} %bitcast.374, bf16[64,2,1,128]{3,0,2,1:T(8,128)(2,1)} %bitcast.360, bf16[64,2,8,128]{3,0,2,1:T(8,128)(2,1)S(1)} %get-tuple-element.67, ...), kind=kLoop, calls=%fused_computation.56 | loop fusion | flops 2621440 | bytes 1310720 | tf_op jit(solution)/shard_map/concatenate | solution.py:128
  103.5 0.3 fusion.62
  103.9 0.3 fusion.63
  104.2 0.5 copy-done.4
  104.9 1.9 %maximum_maximum_fusion.1 = bf16[192,4,10,128]{3,0,2,1:T(8,128)(2,1)S(1)} fusion(bf16[64,4,10,1]{3,0,2,1:T(8,128)(2,1)S(1)} %get-tuple-element.60, bf16[64,4,10,127]{3,0,2,1:T(8,128)(2,1)S(1)} %get-tuple-element.62, bf16[64,1,1,128]{3,0,2,1:T(8,128)(2,1)S(1)} %bitcast.377, bf16[64,1,8,128]{3,0,2,1:T(8,128)(2,1)S(1)} %bitcast.346, ...), kind=kLoop, calls=%fused_computation.1 | loop fusion | flops 25559040 | bytes 3932160 | tf_op jit(solution)/shard_map/concatenate | solution.py:43
  106.7 0.3 copy.133
  107.3 0.3 fusion.12
  107.6 0.3 convolution_add_fusion.7
  107.9 0.3 convolution_add_fusion.6
  108.2 0.3 convolution_add_fusion.5
  108.5 0.3 convolution_add_fusion.4
  108.8 0.3 convolution_add_fusion.3
  109.1 0.3 convolution_add_fusion.2
  109.4 0.3 convolution_add_fusion.1
  109.7 0.3 fusion
  110.0 1.1 copy.145
  111.1 1.0 reshape.130
  112.1 1.7 %slice.262 = f32[512,128]{1,0:T(8,128)} slice(f32[1408,128]{1,0:T(8,128)} %get-tuple-element.37), slice={[864:1376], [0:128]} | slice | bytes 524288 | tf_op jit(solution)/shard_map/slice | solution.py:325
  (51 shorter events, 1.6 us)
Async XLA Ops:
  2.9 1.2 %copy-start = (bf16[64,2,8,128]{3,2,1,0:T(8,128)(2,1)S(1)}, bf16[64,2,8,128]{3,2,1,0:T(8,128)(2,1)}, u32[]{:S(2)}) copy-start(bf16[64,2,8,128]{3,2,1,0:T(8,128)(2,1)} %param.4) | copy-start | bytes 786436
  33.7 0.9 copy-start.6
  33.7 1.0 copy-start.7
  33.8 1.0 copy-start.10
  33.8 0.9 copy-start.11
  33.8 0.9 copy-start.16
  33.8 0.9 copy-start.17
  33.8 0.9 copy-start.18
  33.8 0.9 copy-start.19
  34.7 2.1 %copy-start.1 = (bf16[3,3,64,192]{3,2,1,0:T(8,128)(2,1)S(1)}, bf16[3,3,64,192]{3,2,1,0:T(8,128)(2,1)}, u32[]{:S(2)}) copy-start(bf16[3,3,64,192]{3,2,1,0:T(8,128)(2,1)} %param.5) | copy-start | bytes 663556
  103.9 0.9 copy-start.4
  103.9 1.0 copy-start.5
  103.9 1.0 copy-start.8
  103.9 0.9 copy-start.9
  103.9 0.9 copy-start.12
  103.9 0.9 copy-start.13
  103.9 0.9 copy-start.14
  103.9 0.9 copy-start.15
  104.9 1.9 %copy-start.2 = (bf16[3,3,64,192]{3,2,1,0:T(8,128)(2,1)S(1)}, bf16[3,3,64,192]{3,2,1,0:T(8,128)(2,1)}, u32[]{:S(2)}) copy-start(bf16[3,3,64,192]{3,2,1,0:T(8,128)(2,1)} %param.5) | copy-start | bytes 663556
  109.4 1.7 %copy-start.3 = (f32[1408,128]{1,0:T(8,128)S(1)}, f32[1408,128]{1,0:T(8,128)}, u32[]{:S(2)}) copy-start(f32[1408,128]{1,0:T(8,128)} %get-tuple-element.37) | copy-start | bytes 2162692

commit v12 on v11

--- a/solution.py
+++ b/solution.py
@@ -173,13 +173,19 @@
     return list(zip(*orders))
 
 
+def halving_groups(bits, halvings):
+    if halvings < 3:
+        return [(pair,) for pair in bits[:halvings]]
+    return [(pair,) for pair in bits[: halvings - 2]] + [tuple(bits[halvings - 2 : halvings])]
+
+
 def allreduce_kernel(bits, halvings, offsets, x_ref, *refs):
     count = len(offsets)
     pieces, o_ref = refs[:count], refs[count]
     landed = refs[count + 1 : 2 * count + 1]
     scratch = refs[2 * count + 1 :]
-    halve_bufs = scratch[:halvings]
-    work, double_buf, send_sems, recv_sems, halo_send, halo_recv = scratch[halvings:]
+    halve_bufs = scratch[: len(halving_groups(bits, halvings))]
+    work, double_buf, send_sems, recv_sems, halo_send, halo_recv = scratch[len(halve_bufs) :]
     here = {"gz": lax.axis_index("gz"), "gy": lax.axis_index("gy")}
     sizes = {"gz": lax.axis_size("gz"), "gy": lax.axis_size("gy")}
 
@@ -207,7 +213,8 @@
         return tuple(device)
 
     groups = [bits[i : i + 2] for i in range(halvings, len(bits), 2)]
-    reach = [(pair,) for pair in bits] + [tuple(g) for g in groups if len(g) == 2]
+    wide = [tuple(g) for g in groups + halving_groups(bits, halvings) if len(g) == 2]
+    reach = [(pair,) for pair in bits] + wide
 
     barrier = pltpu.get_barrier_semaphore()
     for pairs in reach:
@@ -244,16 +251,30 @@
         return copy
 
     lo, length, step = 0, o_ref.shape[0], 0
-    for k in range(halvings):
-        pair = bits[k]
-        half = length // 2
-        bit = bit_of(pair)
-        keep = pl.multiple_of(lo + bit * half, 8)
-        give = pl.multiple_of(lo + (1 - bit) * half, 8)
+    for k, group in enumerate(halving_groups(bits, halvings)):
         source = x_ref if k == 0 else work
-        exchange(step, pair, source.at[pl.ds(give, half)], halve_bufs[k])
-        work[pl.ds(keep, half)] = source[pl.ds(keep, half)] + halve_bufs[k][...]
-        lo, length, step = keep, half, step + 1
+        flips = [group] if len(group) == 1 else [group[:1], group[1:], group]
+        parts = 1 << len(group)
+        piece = length // parts
+        mine = 0
+        for pair in group:
+            mine = 2 * mine + bit_of(pair)
+        copies = []
+        for m, flip in enumerate(flips):
+            theirs = 0
+            for pair in group:
+                flipped = bit_of(pair) + (1 - 2 * bit_of(pair)) * int(pair in flip)
+                theirs = 2 * theirs + flipped
+            start = pl.multiple_of(lo + theirs * piece, 8)
+            copies.append(start_copy(step + m, flip, source.at[pl.ds(start, piece)], halve_bufs[k].at[m]))
+        for copy in copies:
+            copy.wait()
+        keep = pl.multiple_of(lo + mine * piece, 8)
+        total = source[pl.ds(keep, piece)]
+        for m in range(len(flips)):
+            total = total + halve_bufs[k][m]
+        work[pl.ds(keep, piece)] = total
+        lo, length, step = keep, piece, step + len(flips)
     slot = 0
     for group in groups:
         own = work.at[pl.ds(lo, length)]
@@ -270,12 +291,17 @@
         work[pl.ds(lo, length)] = near + far
         slot, step = slot + 3, step + 3
     o_ref[pl.ds(lo, length)] = work[pl.ds(lo, length)]
-    for k in reversed(range(halvings)):
-        pair = bits[k]
+    for group in reversed(halving_groups(bits, halvings)):
+        flips = [group] if len(group) == 1 else [group[:1], group[1:], group]
         region = o_ref.at[pl.ds(lo, length)]
-        exchange(step, pair, region, region)
-        lo = pl.multiple_of(lo - bit_of(pair) * length, 8)
-        length, step = length * 2, step + 1
+        copies = [start_copy(step + m, flip, region, region) for m, flip in enumerate(flips)]
+        for copy in copies:
+            copy.wait()
+        mine = 0
+        for pair in group:
+            mine = 2 * mine + bit_of(pair)
+        lo = pl.multiple_of(lo - mine * length, 8)
+        length, step = length << len(group), step + len(flips)
     for copy in halo:
         copy.wait()
 
@@ -289,8 +315,11 @@
     segment = rows >> halvings
     far = len(bits) - halvings
     slots = 3 * (far // 2) + far % 2
-    steps = 2 * halvings + slots
-    scratch = [pltpu.VMEM((rows >> (k + 1), 128), jnp.float32) for k in range(halvings)]
+    steps = 2 * sum((1 << len(g)) - 1 for g in halving_groups(bits, halvings)) + slots
+    scratch, length = [], rows
+    for group in halving_groups(bits, halvings):
+        length >>= len(group)
+        scratch.append(pltpu.VMEM(((1 << len(group)) - 1, length, 128), jnp.float32))
     scratch += [
         pltpu.VMEM(flat.shape, jnp.float32),
         pltpu.VMEM((max(slots, 1), segment, 128), jnp.float32),

time: 115 us -> 110 us (0.957)
  Pallas kernels: 72.9 us -> 67.9 us
    pallas_call x1, Pallas kernels: 48.2 us -> 43.2 us  [allreduce(): pl.pallas_call(functools.partial(allreduce_kernel, bits, halvings, offset...]
where the time goes in v12:
time: 110 us; the launch traced here: 109 us
  Pallas kernels  67.9 us (62%)
  local copies, waits for them, and re-layouts  22.3 us (20%)
  matrix products  11 us (10%)
  other arithmetic  6.32 us (6%)
  between operations  1.23 us (1%)
    pallas_call x1, Pallas kernels, allreduce(): pl.pallas_call(functools.partial(allreduce_kernel, bits, halvings, offset...  43.2 us
    pallas_call x1, Pallas kernels, halo_swap(): pl.pallas_call(functools.partial(halo_kernel, NEIGHBOURS), out_shape=[jax...  24.7 us
    dot_general x18, matrix products, conv_taps(): jnp.einsum('oj,jzyx->ozyx', weight[tap_z, tap_y], window, preferred_eleme...  5.78 us
    unnamed x46, local copies, waits for them, and re-layouts  5.39 us
    concatenate x2, other arithmetic, widen(): jnp.concatenate([jnp.roll(framed, 1 - tap_x, axis=3) for tap_x in range(3...  3.89 us
    dot_general x9, matrix products, body(): jnp.einsum('ozyx,jzyx->oj', gate_grad, window, preferred_element_type=jnp...  3.32 us
    transpose x6, local copies, waits for them, and re-layouts, as_rows(): return jnp.transpose(piece, (1, 2, 0, 3)).reshape(-1, piece.shape[3])  2.7 us
    concatenate x2, other arithmetic, framed(): return jnp.concatenate(lines, axis=1)  2.29 us

profile of v12, /device:TPU:1, one launch (start us, length us, event | category | flops | bytes accessed | tf_op | source)
XLA Modules:
  0.0 108.7 jit_solution(3278793278508169972)
XLA Ops:
  0.6 0.9 copy.110
  1.6 1.0 copy.109
  2.6 0.3 convolution_bitcast_fusion
  3.0 0.8 copy.111
  3.8 0.3 copy.112
  4.1 0.7 copy.96
  4.8 0.7 copy.97
  5.6 0.6 copy.98
  6.2 0.6 copy.99
  6.9 0.6 slice_bitcast_fusion.26
  7.5 24.7 %shard_map.75 = (bf16[512,128]{1,0:T(8,128)(2,1)}, bf16[512,128]{1,0:T(8,128)(2,1)}, bf16[128,128]{1,0:T(8,128)(2,1)}, bf16[128,128]{1,0:T(8,128)(2,1)}, bf16[64...) custom-call(bf16[512,128]{1,0:T(8,128)(2,1)} %bitcast.353, ...), custom_call_target="tpu_custom_call" | custom-call | tf_op jit(solution)/shard_map/pallas_call | solution.py:89
  32.3 1.1 %maximum_maximum_fusion.2 = bf16[64,4,10,128]{3,0,2,1:T(8,128)(2,1)S(1)} fusion(bf16[64,1,1,128]{3,0,2,1:T(8,128)(2,1)} %bitcast.384, bf16[64,1,8,128]{3,0,2,1:T(8,128)(2,1)} %bitcast.349, bf16[64,1,1,128]{3,0,2,1:T(8,128)(2,1)} %bitcast.382, bf16[64,2,1,128]{3,0,2,1:T(8,128)(2,1)} %bitcast.364, bf16[64,2,8,128]{3,0,2,1:T(8,128)(2,1)S(1)} %copy.100, ...), kind=kLoop, calls=%fused_computation.55 | loop fusion | flops 2621440 | bytes 1310720 | tf_op jit(solution)/shard_map/concatenate | solution.py:128
  33.4 0.3 fusion.64
  33.8 0.3 fusion.65
  34.1 0.5 copy-done.6
  34.7 2.0 %maximum_maximum_fusion = bf16[192,4,10,128]{3,0,2,1:T(8,128)(2,1)S(1)} fusion(bf16[64,4,10,1]{3,0,2,1:T(8,128)(2,1)S(1)} %get-tuple-element.64, bf16[64,4,10,127]{3,0,2,1:T(8,128)(2,1)S(1)} %get-tuple-element.66, bf16[64,1,1,128]{3,0,2,1:T(8,128)(2,1)S(1)} %bitcast.385, bf16[64,1,8,128]{3,0,2,1:T(8,128)(2,1)S(1)} %bitcast.350, ...), kind=kLoop, calls=%fused_computation | loop fusion | flops 25559040 | bytes 3932160 | tf_op jit(solution)/shard_map/concatenate | solution.py:43
  37.1 0.3 convolution_add_fusion.15
  37.3 0.3 convolution_add_fusion.14
  37.6 0.3 convolution_add_fusion.13
  37.9 0.3 convolution_add_fusion.12
  38.4 0.3 convolution_add_fusion.10
  38.7 0.3 convolution_add_fusion.9
  38.9 1.1 %multiply_convert_fusion = (bf16[64,2,8,128]{3,0,2,1:T(8,128)(2,1)S(1)}, bf16[64,2,8,128]{3,0,2,1:T(8,128)(2,1)}) fusion(f32[64,2,8,128]{3,0,2,1:T(8,128)S(1)} %copy.112, f32[2,8,128,64]{2,3,1,0:T(8,128)S(1)} %convolution_add_fusion.9, bf16[192,4,10,128]{3,0,2,1:T(8,128)(2,1)S(1)} %maximum_maximum_fusion, bf16[3,3,64,192]{3,2,1,0:T(8,128)(2,1)S(1)} %copy-done.1), kind=kOutput, calls=%fused_computation.59 | convolution fusion | flops 51904512 | bytes 2392064 | tf_op jit(solution)/shard_map/oj,jzyx->ozyx/dot_general | solution.py:137
  40.1 1.2 %copy.107 = bf16[64,2,8,128]{0,3,2,1:T(8,128)(2,1)S(1)} copy(bf16[64,2,8,128]{3,0,2,1:T(8,128)(2,1)} %get-tuple-element.68) | data formatting | bytes 524288 | tf_op jit(solution)/shard_map/convert_element_type | solution.py:366
  41.3 0.5 copy.108
  41.8 1.0 dot_general.126
  42.8 1.2 %fusion.3 = bf16[128,1,256]{0,2,1:T(8,128)(2,1)S(1)} fusion(bf16[256,2,2,2,64]{0,4,3,2,1:T(8,128)(2,1)} %dot_general.126, bf16[2,2,128,2,64]{2,4,3,1,0:T(8,128)(2,1)S(1)} %bitcast.352), kind=kOutput, calls=%fused_computation.33 | convolution fusion | flops 33587200 | bytes 458752 | tf_op jit(solution)/shard_map/aboei,iZaYbXe->oZYX/dot_general | solution.py:369
  44.1 0.7 copy.144
  44.8 0.3 convolution_bitcast_fusion.1
  45.4 0.3 reshape_reshape.3
  45.7 1.8 %fusion.61 = (bf16[192,2,8,128]{3,0,2,1:T(8,128)(2,1)S(1)}, bf16[192,2,8,128]{3,0,2,1:T(8,128)(2,1)S(1)}, bf16[192,2,8,128]{3,0,2,1:T(8,128)(2,1)S(1)}, bf16[192...) fusion(bf16[192,4,10,128]{3,0,2,1:T(8,128)(2,1)S(1)} %maximum_m, ...), kind=kLoop, calls=%fused_computation.124 | loop fusion | bytes 14155776 | tf_op jit(solution)/shard_map/slice | solution.py:136
  47.5 0.4 convolution_bitcast_fusion.3
  47.9 0.4 convolution_bitcast_fusion.4
  48.2 0.4 convolution_bitcast_fusion.5
  48.6 0.4 convolution_bitcast_fusion.9
  49.0 0.4 convolution_bitcast_fusion.10
  49.4 0.4 convolution_bitcast_fusion.11
  49.7 0.4 convolution_bitcast_fusion.6
  50.1 0.4 convolution_bitcast_fusion.7
  50.5 0.4 convolution_bitcast_fusion.8
  50.9 0.3 reshape.118
  51.3 0.9 pad_bitcast_fusion.x_ref
  52.2 0.7 fusion.67
  53.0 0.6 fusion.66
  53.6 0.6 slice_bitcast_fusion.22
  54.2 43.2 %shard_map.76 = (f32[1408,128]{1,0:T(8,128)}, bf16[512,128]{1,0:T(8,128)(2,1)}, bf16[512,128]{1,0:T(8,128)(2,1)}, bf16[128,128]{1,0:T(8,128)(2,1)}, bf16[128,128...) custom-call(f32[1408,128]{1,0:T(8,128)} %pad_bitcast_fusion.x_ref, ...), custom_call_target="tpu_custom_call" | custom-call | tf_op jit(solution)/shard_map/pallas_call | solution.py:332
  97.4 1.1 %maximum_maximum_fusion.3 = bf16[64,4,10,128]{3,0,2,1:T(8,128)(2,1)S(1)} fusion(bf16[64,1,1,128]{3,0,2,1:T(8,128)(2,1)} %bitcast.376, bf16[64,1,8,128]{3,0,2,1:T(8,128)(2,1)} %bitcast.345, bf16[64,1,1,128]{3,0,2,1:T(8,128)(2,1)} %bitcast.374, bf16[64,2,1,128]{3,0,2,1:T(8,128)(2,1)} %bitcast.360, bf16[64,2,8,128]{3,0,2,1:T(8,128)(2,1)S(1)} %get-tuple-element.67, ...), kind=kLoop, calls=%fused_computation.56 | loop fusion | flops 2621440 | bytes 1310720 | tf_op jit(solution)/shard_map/concatenate | solution.py:128
  98.6 0.3 fusion.62
  98.9 0.3 fusion.63
  99.3 0.5 copy-done.4
  99.9 1.9 %maximum_maximum_fusion.1 = bf16[192,4,10,128]{3,0,2,1:T(8,128)(2,1)S(1)} fusion(bf16[64,4,10,1]{3,0,2,1:T(8,128)(2,1)S(1)} %get-tuple-element.60, bf16[64,4,10,127]{3,0,2,1:T(8,128)(2,1)S(1)} %get-tuple-element.62, bf16[64,1,1,128]{3,0,2,1:T(8,128)(2,1)S(1)} %bitcast.377, bf16[64,1,8,128]{3,0,2,1:T(8,128)(2,1)S(1)} %bitcast.346, ...), kind=kLoop, calls=%fused_computation.1 | loop fusion | flops 25559040 | bytes 3932160 | tf_op jit(solution)/shard_map/concatenate | solution.py:43
  101.8 0.3 copy.133
  102.3 0.3 fusion.12
  102.6 0.3 convolution_add_fusion.7
  102.9 0.3 convolution_add_fusion.6
  103.2 0.3 convolution_add_fusion.5
  103.5 0.3 convolution_add_fusion.4
  103.8 0.3 convolution_add_fusion.3
  104.1 0.3 convolution_add_fusion.2
  104.4 0.3 convolution_add_fusion.1
  104.7 0.3 fusion
  105.0 1.1 %copy.145 = f32[64,2,8,128]{3,2,1,0:T(8,128)} copy(f32[64,2,8,128]{3,0,2,1:T(8,128)S(1)} %fusion) | data formatting | bytes 1048576
  106.1 1.0 reshape.130
  107.1 1.7 %slice.262 = f32[512,128]{1,0:T(8,128)} slice(f32[1408,128]{1,0:T(8,128)} %get-tuple-element.37), slice={[864:1376], [0:128]} | slice | bytes 524288 | tf_op jit(solution)/shard_map/slice | solution.py:354
  (51 shorter events, 1.6 us)
Async XLA Ops:
  2.9 1.2 %copy-start = (bf16[64,2,8,128]{3,2,1,0:T(8,128)(2,1)S(1)}, bf16[64,2,8,128]{3,2,1,0:T(8,128)(2,1)}, u32[]{:S(2)}) copy-start(bf16[64,2,8,128]{3,2,1,0:T(8,128)(2,1)} %param.4) | copy-start | bytes 786436
  33.7 0.9 copy-start.6
  33.7 1.0 copy-start.7
  33.8 1.0 copy-start.10
  33.8 0.9 copy-start.11
  33.8 0.9 copy-start.16
  33.8 0.9 copy-start.17
  33.8 0.9 copy-start.18
  33.8 0.9 copy-start.19
  34.7 2.1 %copy-start.1 = (bf16[3,3,64,192]{3,2,1,0:T(8,128)(2,1)S(1)}, bf16[3,3,64,192]{3,2,1,0:T(8,128)(2,1)}, u32[]{:S(2)}) copy-start(bf16[3,3,64,192]{3,2,1,0:T(8,128)(2,1)} %param.5) | copy-start | bytes 663556
  98.9 0.9 copy-start.4
  98.9 1.0 copy-start.5
  98.9 1.0 copy-start.8
  98.9 0.9 copy-start.9
  98.9 0.9 copy-start.12
  98.9 0.9 copy-start.13
  98.9 0.9 copy-start.14
  98.9 0.9 copy-start.15
  99.9 1.9 %copy-start.2 = (bf16[3,3,64,192]{3,2,1,0:T(8,128)(2,1)S(1)}, bf16[3,3,64,192]{3,2,1,0:T(8,128)(2,1)}, u32[]{:S(2)}) copy-start(bf16[3,3,64,192]{3,2,1,0:T(8,128)(2,1)} %param.5) | copy-start | bytes 663556
  104.4 1.7 %copy-start.3 = (f32[1408,128]{1,0:T(8,128)S(1)}, f32[1408,128]{1,0:T(8,128)}, u32[]{:S(2)}) copy-start(f32[1408,128]{1,0:T(8,128)} %get-tuple-element.37) | copy-start | bytes 2162692

commit v13 on v12

--- a/solution.py
+++ b/solution.py
@@ -181,9 +181,9 @@
 
 def allreduce_kernel(bits, halvings, offsets, x_ref, *refs):
     count = len(offsets)
-    pieces, o_ref = refs[:count], refs[count]
-    landed = refs[count + 1 : 2 * count + 1]
-    scratch = refs[2 * count + 1 :]
+    pieces, outs = refs[:count], refs[count : count + 2]
+    landed = refs[count + 2 : 2 * count + 2]
+    scratch, o_ref = refs[2 * count + 2 : -1], refs[-1]
     halve_bufs = scratch[: len(halving_groups(bits, halvings))]
     work, double_buf, send_sems, recv_sems, halo_send, halo_recv = scratch[len(halve_bufs) :]
     here = {"gz": lax.axis_index("gz"), "gy": lax.axis_index("gy")}
@@ -304,9 +304,13 @@
         length, step = length << len(group), step + len(flips)
     for copy in halo:
         copy.wait()
-
-
-def allreduce(flat, pieces=(), halvings=HALVINGS):
+    start = 0
+    for out in outs:
+        out[...] = o_ref[pl.ds(start, out.shape[0])]
+        start += out.shape[0]
+
+
+def allreduce(flat, splits, pieces=(), halvings=HALVINGS):
     offsets = NEIGHBOURS[: len(pieces)]
     pieces = [p.reshape(-1, 128) for p in pieces]
     bits = mesh_bits()
@@ -327,18 +331,19 @@
         pltpu.SemaphoreType.DMA((steps,)),
         pltpu.SemaphoreType.DMA((max(len(pieces), 1),)),
         pltpu.SemaphoreType.DMA((max(len(pieces), 1),)),
+        pltpu.VMEM(flat.shape, jnp.float32),
     ]
     vmem = pl.BlockSpec(memory_space=pltpu.VMEM)
     outs = pl.pallas_call(
         functools.partial(allreduce_kernel, bits, halvings, offsets),
-        out_shape=[jax.ShapeDtypeStruct(flat.shape, jnp.float32)]
+        out_shape=[jax.ShapeDtypeStruct((rows_out, 128), jnp.float32) for rows_out in splits]
         + [jax.ShapeDtypeStruct(p.shape, p.dtype) for p in pieces],
         in_specs=[vmem] * (1 + len(pieces)),
-        out_specs=[vmem] * (1 + len(pieces)),
+        out_specs=[vmem] * (len(splits) + len(pieces)),
         scratch_shapes=scratch,
         compiler_params=pltpu.CompilerParams(collective_id=0, has_side_effects=True),
     )(flat, *pieces)
-    return outs[0], outs[1:]
+    return outs[: len(splits)], outs[len(splits) :]
 
 
 def summed_gradients(local_conv, local_down, pieces, scale):
@@ -347,11 +352,10 @@
     unit = 128 * 8 << HALVINGS
     padded = -(-flat.size // unit) * unit
     flat = jnp.pad(flat, (0, padded - flat.size)).reshape(-1, 128)
-    total, got = allreduce(flat, [as_rows(p) for p in pieces])
-    total = total.reshape(-1)
+    (conv_rows, down_rows), got = allreduce(flat, (sizes[0] // 128, sizes[1] // 128), [as_rows(p) for p in pieces])
     return (
-        total[: sizes[0]].reshape(local_conv.shape),
-        total[sizes[0] : sizes[0] + sizes[1]].reshape(local_down.shape),
+        conv_rows.reshape(local_conv.shape),
+        down_rows.reshape(local_down.shape),
         [from_rows(g, p.shape) for g, p in zip(got, pieces)],
     )
 

time: 110 us -> 109 us (level)
    slice x2 -> x0, local copies, waits for them, and re-layouts: 1.7 us -> none  [the longest x1 1.67 us: summed_gradients(): total[sizes[0]:sizes[0] + sizes[1]].reshape(local_down.shape)]
    unnamed x46 -> x49, local copies, waits for them, and re-layouts: 5.39 us -> 6.1 us
where the time goes in v13:
time: 109 us; the launch traced here: 108 us
  Pallas kernels  67.9 us (62%)
  local copies, waits for them, and re-layouts  21.3 us (20%)
  matrix products  11 us (10%)
  other arithmetic  6.32 us (6%)
  between operations  1.24 us (1%)
    pallas_call x1, Pallas kernels, allreduce(): pl.pallas_call(functools.partial(allreduce_kernel, bits, halvings, offset...  43.2 us
    pallas_call x1, Pallas kernels, halo_swap(): pl.pallas_call(functools.partial(halo_kernel, NEIGHBOURS), out_shape=[jax...  24.7 us
    unnamed x49, local copies, waits for them, and re-layouts  6.1 us
    dot_general x18, matrix products, conv_taps(): jnp.einsum('oj,jzyx->ozyx', weight[tap_z, tap_y], window, preferred_eleme...  5.78 us
    concatenate x2, other arithmetic, widen(): jnp.concatenate([jnp.roll(framed, 1 - tap_x, axis=3) for tap_x in range(3...  3.89 us
    dot_general x9, matrix products, body(): jnp.einsum('ozyx,jzyx->oj', gate_grad, window, preferred_element_type=jnp...  3.32 us
    transpose x6, local copies, waits for them, and re-layouts, as_rows(): return jnp.transpose(piece, (1, 2, 0, 3)).reshape(-1, piece.shape[3])  2.7 us
    concatenate x2, other arithmetic, framed(): return jnp.concatenate(lines, axis=1)  2.29 us

profile of v13, /device:TPU:1, one launch (start us, length us, event | category | flops | bytes accessed | tf_op | source)
XLA Modules:
  0.0 107.7 jit_solution(2028904163797531453)
XLA Ops:
  0.6 0.9 copy.110
  1.6 1.0 copy.109
  2.6 0.3 convolution_bitcast_fusion
  3.0 0.8 copy.111
  3.8 0.3 copy.112
  4.1 0.7 copy.96
  4.8 0.7 copy.97
  5.6 0.6 copy.98
  6.2 0.6 copy.99
  6.9 0.6 slice_bitcast_fusion.26
  7.5 24.7 %shard_map.75 = (bf16[512,128]{1,0:T(8,128)(2,1)}, bf16[512,128]{1,0:T(8,128)(2,1)}, bf16[128,128]{1,0:T(8,128)(2,1)}, bf16[128,128]{1,0:T(8,128)(2,1)}, bf16[64...) custom-call(bf16[512,128]{1,0:T(8,128)(2,1)} %bitcast.353, ...), custom_call_target="tpu_custom_call" | custom-call | tf_op jit(solution)/shard_map/pallas_call | solution.py:89
  32.3 1.1 %maximum_maximum_fusion.2 = bf16[64,4,10,128]{3,0,2,1:T(8,128)(2,1)S(1)} fusion(bf16[64,1,1,128]{3,0,2,1:T(8,128)(2,1)} %bitcast.384, bf16[64,1,8,128]{3,0,2,1:T(8,128)(2,1)} %bitcast.349, bf16[64,1,1,128]{3,0,2,1:T(8,128)(2,1)} %bitcast.382, bf16[64,2,1,128]{3,0,2,1:T(8,128)(2,1)} %bitcast.364, bf16[64,2,8,128]{3,0,2,1:T(8,128)(2,1)S(1)} %copy.100, ...), kind=kLoop, calls=%fused_computation.55 | loop fusion | flops 2621440 | bytes 1310720 | tf_op jit(solution)/shard_map/concatenate | solution.py:128
  33.4 0.3 fusion.64
  33.8 0.3 fusion.65
  34.1 0.5 copy-done.5
  34.7 2.0 %maximum_maximum_fusion = bf16[192,4,10,128]{3,0,2,1:T(8,128)(2,1)S(1)} fusion(bf16[64,4,10,1]{3,0,2,1:T(8,128)(2,1)S(1)} %get-tuple-element.66, bf16[64,4,10,127]{3,0,2,1:T(8,128)(2,1)S(1)} %get-tuple-element.68, bf16[64,1,1,128]{3,0,2,1:T(8,128)(2,1)S(1)} %bitcast.385, bf16[64,1,8,128]{3,0,2,1:T(8,128)(2,1)S(1)} %bitcast.350, ...), kind=kLoop, calls=%fused_computation | loop fusion | flops 25559040 | bytes 3932160 | tf_op jit(solution)/shard_map/concatenate | solution.py:43
  37.0 0.3 convolution_add_fusion.15
  37.3 0.3 convolution_add_fusion.14
  37.6 0.3 convolution_add_fusion.13
  37.9 0.3 convolution_add_fusion.12
  38.1 0.3 convolution_add_fusion.11
  38.4 0.3 convolution_add_fusion.10
  38.9 1.1 %multiply_convert_fusion = (bf16[64,2,8,128]{3,0,2,1:T(8,128)(2,1)S(1)}, bf16[64,2,8,128]{3,0,2,1:T(8,128)(2,1)}) fusion(f32[64,2,8,128]{3,0,2,1:T(8,128)S(1)} %copy.112, f32[2,8,128,64]{2,3,1,0:T(8,128)S(1)} %convolution_add_fusion.9, bf16[192,4,10,128]{3,0,2,1:T(8,128)(2,1)S(1)} %maximum_maximum_fusion, bf16[3,3,64,192]{3,2,1,0:T(8,128)(2,1)S(1)} %copy-done.1), kind=kOutput, calls=%fused_computation.59 | convolution fusion | flops 51904512 | bytes 2392064 | tf_op jit(solution)/shard_map/oj,jzyx->ozyx/dot_general | solution.py:137
  40.0 1.2 %copy.107 = bf16[64,2,8,128]{0,3,2,1:T(8,128)(2,1)S(1)} copy(bf16[64,2,8,128]{3,0,2,1:T(8,128)(2,1)} %get-tuple-element.70) | data formatting | bytes 524288 | tf_op jit(solution)/shard_map/convert_element_type | solution.py:370
  41.3 0.5 copy.108
  41.8 1.0 dot_general.126
  42.8 1.2 %fusion.3 = bf16[128,1,256]{0,2,1:T(8,128)(2,1)S(1)} fusion(bf16[256,2,2,2,64]{0,4,3,2,1:T(8,128)(2,1)} %dot_general.126, bf16[2,2,128,2,64]{2,4,3,1,0:T(8,128)(2,1)S(1)} %bitcast.352), kind=kOutput, calls=%fused_computation.33 | convolution fusion | flops 33587200 | bytes 458752 | tf_op jit(solution)/shard_map/aboei,iZaYbXe->oZYX/dot_general | solution.py:373
  44.1 0.7 copy.144
  44.8 0.3 convolution_bitcast_fusion.1
  45.4 0.3 reshape_reshape.3
  45.7 1.8 %fusion.61 = (bf16[192,2,8,128]{3,0,2,1:T(8,128)(2,1)S(1)}, bf16[192,2,8,128]{3,0,2,1:T(8,128)(2,1)S(1)}, bf16[192,2,8,128]{3,0,2,1:T(8,128)(2,1)S(1)}, bf16[192...) fusion(bf16[192,4,10,128]{3,0,2,1:T(8,128)(2,1)S(1)} %maximum_m, ...), kind=kLoop, calls=%fused_computation.124 | loop fusion | bytes 14155776 | tf_op jit(solution)/shard_map/slice | solution.py:136
  47.5 0.4 convolution_bitcast_fusion.3
  47.8 0.4 convolution_bitcast_fusion.4
  48.2 0.4 convolution_bitcast_fusion.5
  48.6 0.4 convolution_bitcast_fusion.9
  49.0 0.4 convolution_bitcast_fusion.10
  49.3 0.4 convolution_bitcast_fusion.11
  49.7 0.4 convolution_bitcast_fusion.6
  50.1 0.4 convolution_bitcast_fusion.7
  50.5 0.4 convolution_bitcast_fusion.8
  50.9 0.3 reshape.113
  51.3 0.9 pad_bitcast_fusion.x_ref
  52.2 0.7 fusion.67
  52.9 0.6 fusion.66
  53.6 0.6 slice_bitcast_fusion.22
  54.2 43.2 %shard_map.76 = (f32[864,128]{1,0:T(8,128)}, f32[512,128]{1,0:T(8,128)}, bf16[512,128]{1,0:T(8,128)(2,1)}, bf16[512,128]{1,0:T(8,128)(2,1)}, bf16[128,128]{1,0:T...) custom-call(f32[1408,128]{1,0:T(8,128)} %pad_bitcast_fusion.x_ref, ...), custom_call_target="tpu_custom_call" | custom-call | tf_op jit(solution)/shard_map/pallas_call | solution.py:337
  97.3 1.1 %maximum_maximum_fusion.3 = bf16[64,4,10,128]{3,0,2,1:T(8,128)(2,1)S(1)} fusion(bf16[64,1,1,128]{3,0,2,1:T(8,128)(2,1)} %bitcast.376, bf16[64,1,8,128]{3,0,2,1:T(8,128)(2,1)} %bitcast.345, bf16[64,1,1,128]{3,0,2,1:T(8,128)(2,1)} %bitcast.374, bf16[64,2,1,128]{3,0,2,1:T(8,128)(2,1)} %bitcast.360, bf16[64,2,8,128]{3,0,2,1:T(8,128)(2,1)S(1)} %get-tuple-element.69, ...), kind=kLoop, calls=%fused_computation.56 | loop fusion | flops 2621440 | bytes 1310720 | tf_op jit(solution)/shard_map/concatenate | solution.py:128
  98.5 0.3 fusion.62
  98.9 0.3 fusion.63
  99.2 0.5 copy-done.3
  99.8 1.9 %maximum_maximum_fusion.1 = bf16[192,4,10,128]{3,0,2,1:T(8,128)(2,1)S(1)} fusion(bf16[64,4,10,1]{3,0,2,1:T(8,128)(2,1)S(1)} %get-tuple-element.62, bf16[64,4,10,127]{3,0,2,1:T(8,128)(2,1)S(1)} %get-tuple-element.64, bf16[64,1,1,128]{3,0,2,1:T(8,128)(2,1)S(1)} %bitcast.377, bf16[64,1,8,128]{3,0,2,1:T(8,128)(2,1)S(1)} %bitcast.346, ...), kind=kLoop, calls=%fused_computation.1 | loop fusion | flops 25559040 | bytes 3932160 | tf_op jit(solution)/shard_map/concatenate | solution.py:43
  101.7 0.3 copy.133
  102.3 0.3 fusion.12
  102.5 0.3 convolution_add_fusion.7
  102.8 0.3 convolution_add_fusion.6
  103.1 0.3 convolution_add_fusion.5
  103.4 0.3 convolution_add_fusion.4
  103.7 0.3 convolution_add_fusion.3
  104.0 0.3 convolution_add_fusion.2
  104.3 0.3 convolution_add_fusion.1
  104.6 0.3 fusion
  104.9 1.1 %copy.145 = f32[64,2,8,128]{3,2,1,0:T(8,128)} copy(f32[64,2,8,128]{3,0,2,1:T(8,128)S(1)} %fusion) | data formatting | bytes 1048576
  106.0 1.0 reshape.125
  107.0 0.7 copy.225
  (52 shorter events, 1.6 us)
Async XLA Ops:
  2.9 1.2 %copy-start = (bf16[64,2,8,128]{3,2,1,0:T(8,128)(2,1)S(1)}, bf16[64,2,8,128]{3,2,1,0:T(8,128)(2,1)}, u32[]{:S(2)}) copy-start(bf16[64,2,8,128]{3,2,1,0:T(8,128)(2,1)} %param.4) | copy-start | bytes 786436
  33.7 0.9 copy-start.5
  33.7 1.0 copy-start.6
  33.7 1.0 copy-start.11
  33.7 0.9 copy-start.12
  33.8 0.9 copy-start.17
  33.8 0.9 copy-start.18
  33.8 0.9 copy-start.19
  33.8 0.9 copy-start.20
  34.7 2.1 %copy-start.1 = (bf16[3,3,64,192]{3,2,1,0:T(8,128)(2,1)S(1)}, bf16[3,3,64,192]{3,2,1,0:T(8,128)(2,1)}, u32[]{:S(2)}) copy-start(bf16[3,3,64,192]{3,2,1,0:T(8,128)(2,1)} %param.5) | copy-start | bytes 663556
  98.8 0.9 copy-start.3
  98.8 1.0 copy-start.4
  98.8 1.0 copy-start.9
  98.8 0.9 copy-start.10
  98.8 0.9 copy-start.13
  98.9 0.9 copy-start.14
  98.9 0.9 copy-start.15
  98.9 0.9 copy-start.16
  99.8 1.9 %copy-start.2 = (bf16[3,3,64,192]{3,2,1,0:T(8,128)(2,1)S(1)}, bf16[3,3,64,192]{3,2,1,0:T(8,128)(2,1)}, u32[]{:S(2)}) copy-start(bf16[3,3,64,192]{3,2,1,0:T(8,128)(2,1)} %param.5) | copy-start | bytes 663556
  104.3 1.7 %copy-start.7 = (f32[864,128]{1,0:T(8,128)S(1)}, f32[864,128]{1,0:T(8,128)}, u32[]{:S(2)}) copy-start(f32[864,128]{1,0:T(8,128)} %get-tuple-element.38) | copy-start | bytes 1327108
  104.6 2.4 %copy-start.8 = (f32[512,128]{1,0:T(8,128)S(1)}, f32[512,128]{1,0:T(8,128)}, u32[]{:S(2)}) copy-start(f32[512,128]{1,0:T(8,128)} %get-tuple-element.39) | copy-start | bytes 786436

commit v14 on v13

--- a/solution.py
+++ b/solution.py
@@ -365,7 +365,9 @@
     out_channels = down_weight.shape[2]
     cell_count = plane_count * row_count * breadth * lax.axis_size("gz") * lax.axis_size("gy")
     grad_scale = 1.0 / math.sqrt(cell_count)
-    columns = widen(framed(features, halo_swap(halo_pieces(features), 1)))
+    received = halo_swap(halo_pieces(features), 1)
+    received, down_weight, cotangent = lax.optimization_barrier((received, down_weight, cotangent))
+    columns = widen(framed(features, received))
     preact = conv_taps(columns, conv_weight, features.shape)
     hidden = jax.nn.silu(preact).astype(jnp.bfloat16)
     blocks = hidden.reshape(channels, plane_count // 2, 2, row_count // 2, 2, breadth // 2, 2)

time: 109 us -> 107 us (0.982)
    unnamed x49 -> x48, local copies, waits for them, and re-layouts: 6.1 us -> 3.75 us
    transpose x6, local copies, waits for them, and re-layouts: 2.7 us -> 4.76 us  [as_rows(): return jnp.transpose(piece, (1, 2, 0, 3)).reshape(-1, piece.shape[3])]
where the time goes in v14:
time: 107 us; the launch traced here: 106 us
  Pallas kernels  67.9 us (63%)
  local copies, waits for them, and re-layouts  20.3 us (19%)
  matrix products  10.8 us (10%)
  other arithmetic  5.27 us (5%)
  between operations  1.29 us (1%)
    pallas_call x1, Pallas kernels, allreduce(): pl.pallas_call(functools.partial(allreduce_kernel, bits, halvings, offset...  43.1 us
    pallas_call x1, Pallas kernels, halo_swap(): pl.pallas_call(functools.partial(halo_kernel, NEIGHBOURS), out_shape=[jax...  24.7 us
    dot_general x18, matrix products, conv_taps(): jnp.einsum('oj,jzyx->ozyx', weight[tap_z, tap_y], window, preferred_eleme...  5.08 us
    transpose x6, local copies, waits for them, and re-layouts, as_rows(): return jnp.transpose(piece, (1, 2, 0, 3)).reshape(-1, piece.shape[3])  4.76 us
    concatenate x2, other arithmetic, widen(): jnp.concatenate([jnp.roll(framed, 1 - tap_x, axis=3) for tap_x in range(3...  3.89 us
    unnamed x48, local copies, waits for them, and re-layouts  3.75 us
    dot_general x9, matrix products, body(): jnp.einsum('ozyx,jzyx->oj', gate_grad, window, preferred_element_type=jnp...  3.32 us

profile of v14, /device:TPU:1, one launch (start us, length us, event | category | flops | bytes accessed | tf_op | source)
XLA Modules:
  0.0 105.6 jit_solution(17845111385695518451)
XLA Ops:
  0.7 1.0 slice_bitcast_fusion
  1.7 0.7 copy.94
  2.4 0.7 copy.95
  3.0 1.1 %slice_bitcast_fusion.2 = (bf16[2,1,64,128]{3,1,0,2:T(2,128)(2,1)S(1)}, bf16[2,1,64,128]{3,1,0,2:T(2,128)(2,1)S(1)}) fusion(bf16[64,2,8,128]{3,2,1,0:T(8,128)(2,1)} %param.4), kind=kLoop, calls=%fused_computation.68 | loop fusion | bytes 131072 | tf_op jit(solution)/shard_map/transpose | solution.py:101
  4.2 0.6 copy.96
  4.8 0.6 copy.97
  5.4 1.0 copy.98
  6.4 0.6 slice_bitcast_fusion.26
  7.1 24.7 %shard_map.75 = (bf16[512,128]{1,0:T(8,128)(2,1)}, bf16[512,128]{1,0:T(8,128)(2,1)}, bf16[128,128]{1,0:T(8,128)(2,1)}, bf16[128,128]{1,0:T(8,128)(2,1)}, bf16[64...) custom-call(bf16[512,128]{1,0:T(8,128)(2,1)} %bitcast.351, ...), custom_call_target="tpu_custom_call" | custom-call | tf_op jit(solution)/shard_map/pallas_call | solution.py:89
  32.1 0.3 convolution_bitcast_fusion
  32.5 0.8 copy.109
  33.3 0.3 copy.110
  33.8 0.3 fusion.64
  34.1 0.3 fusion.65
  34.5 2.0 %maximum_maximum_fusion = bf16[192,4,10,128]{3,0,2,1:T(8,128)(2,1)S(1)} fusion(bf16[64,4,10,1]{3,0,2,1:T(8,128)(2,1)S(1)} %get-tuple-element.86, bf16[64,4,10,127]{3,0,2,1:T(8,128)(2,1)S(1)} %get-tuple-element.88, bf16[64,1,1,128]{3,0,2,1:T(8,128)(2,1)S(1)} %bitcast.375, bf16[64,1,8,128]{3,0,2,1:T(8,128)(2,1)S(1)} %bitcast.346, ...), kind=kLoop, calls=%fused_computation | loop fusion | flops 25559040 | bytes 3932160 | tf_op jit(solution)/shard_map/concatenate | solution.py:43
  36.5 0.3 fusion.32
  36.8 0.3 convolution_add_fusion.15
  37.1 0.3 convolution_add_fusion.14
  37.3 0.3 convolution_add_fusion.13
  37.6 0.3 convolution_add_fusion.12
  37.9 0.3 convolution_add_fusion.11
  38.1 0.3 convolution_add_fusion.10
  38.4 0.3 convolution_add_fusion.9
  38.7 0.4 multiply_convert_fusion
  39.1 0.3 copy.106
  39.4 0.5 copy.107
  39.9 1.0 dot_general.126
  40.9 1.8 %fusion.3 = bf16[128,1,256]{2,0,1:T(8,128)(2,1)} fusion(bf16[2,2,128,2,64]{2,4,3,1,0:T(8,128)(2,1)S(1)} %bitcast.340, bf16[256,2,2,2,64]{0,4,3,2,1:T(8,128)(2,1)} %dot_general.126), kind=kOutput, calls=%fused_computation.33 | convolution fusion | flops 33587200 | bytes 458752 | tf_op jit(solution)/shard_map/aboei,iZaYbXe->oZYX/dot_general | solution.py:375
  42.7 0.3 convolution_bitcast_fusion.1
  43.3 0.3 reshape_reshape.3
  43.6 1.8 %fusion.61 = (bf16[192,2,8,128]{3,0,2,1:T(8,128)(2,1)S(1)}, bf16[192,2,8,128]{3,0,2,1:T(8,128)(2,1)S(1)}, bf16[192,2,8,128]{3,0,2,1:T(8,128)(2,1)S(1)}, bf16[192...) fusion(bf16[192,4,10,128]{3,0,2,1:T(8,128)(2,1)S(1)} %maximum_m, ...), kind=kLoop, calls=%fused_computation.124 | loop fusion | bytes 14155776 | tf_op jit(solution)/shard_map/slice | solution.py:136
  45.4 0.4 convolution_bitcast_fusion.3
  45.8 0.4 convolution_bitcast_fusion.4
  46.1 0.4 convolution_bitcast_fusion.5
  46.5 0.4 convolution_bitcast_fusion.9
  46.9 0.4 convolution_bitcast_fusion.10
  47.3 0.4 convolution_bitcast_fusion.11
  47.7 0.4 convolution_bitcast_fusion.6
  48.0 0.4 convolution_bitcast_fusion.7
  48.4 0.4 convolution_bitcast_fusion.8
  48.9 0.3 reshape.113
  49.2 0.9 pad_bitcast_fusion.x_ref
  50.2 0.7 fusion.67
  50.9 0.6 fusion.66
  51.5 0.6 slice_bitcast_fusion.22
  52.1 43.1 %shard_map.76 = (f32[864,128]{1,0:T(8,128)}, f32[512,128]{1,0:T(8,128)}, bf16[512,128]{1,0:T(8,128)(2,1)}, bf16[512,128]{1,0:T(8,128)(2,1)}, bf16[128,128]{1,0:T...) custom-call(f32[1408,128]{1,0:T(8,128)} %pad_bitcast_fusion.x_ref, ...), custom_call_target="tpu_custom_call" | custom-call | tf_op jit(solution)/shard_map/pallas_call | solution.py:337
  95.3 1.1 %maximum_maximum_fusion.3 = bf16[64,4,10,128]{3,0,2,1:T(8,128)(2,1)S(1)} fusion(bf16[64,1,1,128]{3,0,2,1:T(8,128)(2,1)} %bitcast.382, bf16[64,1,8,128]{3,0,2,1:T(8,128)(2,1)} %bitcast.349, bf16[64,1,1,128]{3,0,2,1:T(8,128)(2,1)} %bitcast.380, bf16[64,2,1,128]{3,0,2,1:T(8,128)(2,1)} %bitcast.362, bf16[64,2,8,128]{3,0,2,1:T(8,128)(2,1)S(1)} %get-tuple-element.89, ...), kind=kLoop, calls=%fused_computation.56 | loop fusion | flops 2621440 | bytes 1310720 | tf_op jit(solution)/shard_map/concatenate | solution.py:128
  96.4 0.3 fusion.62
  96.8 0.3 fusion.63
  97.1 0.5 copy-done.4
  97.8 1.9 %maximum_maximum_fusion.1 = bf16[192,4,10,128]{3,0,2,1:T(8,128)(2,1)S(1)} fusion(bf16[64,4,10,1]{3,0,2,1:T(8,128)(2,1)S(1)} %get-tuple-element.82, bf16[64,4,10,127]{3,0,2,1:T(8,128)(2,1)S(1)} %get-tuple-element.84, bf16[64,1,1,128]{3,0,2,1:T(8,128)(2,1)S(1)} %bitcast.383, bf16[64,1,8,128]{3,0,2,1:T(8,128)(2,1)S(1)} %bitcast.350, ...), kind=kLoop, calls=%fused_computation.1 | loop fusion | flops 25559040 | bytes 3932160 | tf_op jit(solution)/shard_map/concatenate | solution.py:43
  99.6 0.3 copy.131
  100.2 0.3 fusion.12
  100.5 0.3 convolution_add_fusion.7
  100.8 0.3 convolution_add_fusion.6
  101.1 0.3 convolution_add_fusion.5
  101.4 0.3 convolution_add_fusion.4
  101.6 0.3 convolution_add_fusion.3
  101.9 0.3 convolution_add_fusion.2
  102.2 0.3 convolution_add_fusion.1
  102.6 0.3 fusion
  102.8 1.1 %copy.142 = f32[64,2,8,128]{3,2,1,0:T(8,128)} copy(f32[64,2,8,128]{3,0,2,1:T(8,128)S(1)} %fusion) | data formatting | bytes 1048576
  104.0 1.0 reshape.125
  104.9 0.7 copy.222
  (53 shorter events, 1.2 us)
Async XLA Ops:
  0.6 31.2 %copy-start.12 = (bf16[2,2,128,128]{3,2,1,0:T(8,128)(2,1)S(1)}, bf16[2,2,128,128]{3,2,1,0:T(8,128)(2,1)}, u32[]{:S(2)}) copy-start(bf16[2,2,128,128]{3,2,1,0:T(8,128)(2,1)} %param.6) | copy-start | bytes 393220
  0.6 31.3 %copy-start.21 = (bf16[128,1,256]{2,0,1:T(8,128)(2,1)S(1)}, bf16[128,1,256]{2,0,1:T(8,128)(2,1)}, u32[]{:S(2)}) copy-start(bf16[128,1,256]{2,0,1:T(8,128)(2,1)} %param.7) | copy-start | bytes 196612
  32.4 1.2 %copy-start.2 = (bf16[512,128]{1,0:T(8,128)(2,1)S(1)}, bf16[512,128]{1,0:T(8,128)(2,1)}, u32[]{:S(2)}) copy-start(bf16[512,128]{1,0:T(8,128)(2,1)} %get-tuple-element.32) | copy-start | bytes 393220
  32.4 1.2 %copy-start.3 = (bf16[512,128]{1,0:T(8,128)(2,1)S(1)}, bf16[512,128]{1,0:T(8,128)(2,1)}, u32[]{:S(2)}) copy-start(bf16[512,128]{1,0:T(8,128)(2,1)} %get-tuple-element.33) | copy-start | bytes 393220
  32.4 1.2 %copy-start.8 = (bf16[128,128]{1,0:T(8,128)(2,1)S(1)}, bf16[128,128]{1,0:T(8,128)(2,1)}, u32[]{:S(2)}) copy-start(bf16[128,128]{1,0:T(8,128)(2,1)} %get-tuple-element.34) | copy-start | bytes 98308
  32.4 1.2 %copy-start.9 = (bf16[128,128]{1,0:T(8,128)(2,1)S(1)}, bf16[128,128]{1,0:T(8,128)(2,1)}, u32[]{:S(2)}) copy-start(bf16[128,128]{1,0:T(8,128)(2,1)} %get-tuple-element.35) | copy-start | bytes 98308
  32.5 1.2 %copy-start.13 = (bf16[64,128]{1,0:T(8,128)(2,1)S(1)}, bf16[64,128]{1,0:T(8,128)(2,1)}, u32[]{:S(2)}) copy-start(bf16[64,128]{1,0:T(8,128)(2,1)} %get-tuple-element.36) | copy-start | bytes 49156
  32.5 1.2 %copy-start.14 = (bf16[64,128]{1,0:T(8,128)(2,1)S(1)}, bf16[64,128]{1,0:T(8,128)(2,1)}, u32[]{:S(2)}) copy-start(bf16[64,128]{1,0:T(8,128)(2,1)} %get-tuple-element.37) | copy-start | bytes 49156
  32.5 1.2 %copy-start.15 = (bf16[64,128]{1,0:T(8,128)(2,1)S(1)}, bf16[64,128]{1,0:T(8,128)(2,1)}, u32[]{:S(2)}) copy-start(bf16[64,128]{1,0:T(8,128)(2,1)} %get-tuple-element.38) | copy-start | bytes 49156
  32.5 1.2 %copy-start.16 = (bf16[64,128]{1,0:T(8,128)(2,1)S(1)}, bf16[64,128]{1,0:T(8,128)(2,1)}, u32[]{:S(2)}) copy-start(bf16[64,128]{1,0:T(8,128)(2,1)} %get-tuple-element.39) | copy-start | bytes 49156
  34.5 2.1 %copy-start = (bf16[3,3,64,192]{3,2,1,0:T(8,128)(2,1)S(1)}, bf16[3,3,64,192]{3,2,1,0:T(8,128)(2,1)}, u32[]{:S(2)}) copy-start(bf16[3,3,64,192]{3,2,1,0:T(8,128)(2,1)} %param.5) | copy-start | bytes 663556
  96.7 0.9 copy-start.4
  96.7 1.0 copy-start.5
  96.8 1.0 copy-start.10
  96.8 0.9 copy-start.11
  96.8 0.9 copy-start.17
  96.8 0.9 copy-start.18
  96.8 0.9 copy-start.19
  96.8 0.9 copy-start.20
  97.7 1.9 %copy-start.1 = (bf16[3,3,64,192]{3,2,1,0:T(8,128)(2,1)S(1)}, bf16[3,3,64,192]{3,2,1,0:T(8,128)(2,1)}, u32[]{:S(2)}) copy-start(bf16[3,3,64,192]{3,2,1,0:T(8,128)(2,1)} %param.5) | copy-start | bytes 663556
  102.2 1.7 %copy-start.6 = (f32[864,128]{1,0:T(8,128)S(1)}, f32[864,128]{1,0:T(8,128)}, u32[]{:S(2)}) copy-start(f32[864,128]{1,0:T(8,128)} %get-tuple-element.58) | copy-start | bytes 1327108
  102.5 2.4 %copy-start.7 = (f32[512,128]{1,0:T(8,128)S(1)}, f32[512,128]{1,0:T(8,128)}, u32[]{:S(2)}) copy-start(f32[512,128]{1,0:T(8,128)} %get-tuple-element.59) | copy-start | bytes 786436
